TPU v7x, 256 devices: a whole 4x4x8 slice. The times are simulated.
256 devices in a mesh: gx: 8 (over z), yz: 32 (over x, y, core).
Axes of the slice: x: 4, y: 4, z: 8, core: 2. Of those that a mesh axis runs over, the one named last changes fastest.
Arguments:
- camera_accel: float32 [8, 2048, 3, 16, 128], P('gx', 'yz'), may hold values from -8 to 8
- camera_weight: float32 [8, 2048, 16, 128], P('gx', 'yz'), may hold values from 0.25 to 4
- brick_slot: int32 [8, 2048], P('gx', 'yz'), may hold values from 0 to 2047, as said below
- brick_solid: int32 [8, 2048], P('gx', 'yz'), may hold values from 0 to 1, as said below
Outputs:
- solution: float32 [32, 1024, 1024], P('yz', 'gx')
- residual: float32 [32, 1024, 1024], P('yz', 'gx')
Inputs may be any that keep to these rules, and one draw needn't show every extreme that they name: `brick_slot`: row g lists each in-slab brick number of slab g once; entries j * 64 to (j + 1) * 64 - 1 are the bricks that camera owner j holds; brick number i belongs to solver owner i // 64. One camera owner holds at most 3 bricks of one solver owner, and exactly 3 of some in every slab. `brick_solid`: 1 marks a solid brick, numbered as in brick_slot; every slab has solid and fluid bricks.
All inputs are finite; a program needn't handle non-finite values.
Results may differ from a plain program's by a relative error of at most 0.00024.
Values sent between devices are 32-bit elements; how exact they have to be, the bound alone decides.
No kernel may reach another device: no remote copies, remote signals or barrier semaphores. Data moves between devices by JAX's collectives and lax.ppermute only.
A program may use at most 128 MiB of HBM per device.

v0:
```python
import functools

import jax
import jax.numpy as jnp
from jax import lax
from jax.sharding import Mesh
from jax.sharding import PartitionSpec as P

NX = 1024
NY = 1024
BR = 16
B = 128
ITERS = 2
GX_YZ = ("gx", "yz_0", "yz_1", "yz_2")
YZ = ("yz_0", "yz_1", "yz_2")


shift_rate = 0.05
spectral_gain = 1.0
spectral_floor = 2.0
highest = lax.Precision.HIGHEST


def padded_2(shard, sides, width):
    edges = {}
    for axis, dim in sides:
        devices, length = (lax.axis_size(axis), shard.shape[dim])
        up = [(i, (i + 1) % devices) for i in range(devices - 1)]
        last = lax.slice_in_dim(shard, length - width, length, axis=dim)
        first = lax.slice_in_dim(shard, 0, width, axis=dim)
        edges[dim] = (
            lax.ppermute(last, axis, up),
            lax.ppermute(first, axis, [(b, a) for a, b in up]),
        )
    done = []
    for _, dim in sides:
        low, high = edges[dim]
        around = [(width, width) if d in done else (0, 0) for d in range(shard.ndim)]
        shard = jnp.concatenate([jnp.pad(low, around), shard, jnp.pad(high, around)], axis=dim)
        done.append(dim)
    return shard


def one_axis_at_a_time(shard, axes):
    return functools.reduce(lax.psum, axes, shard)


def cosine_table(length, row_count, col_count):
    row_ids = jnp.arange(row_count, dtype=jnp.int32)
    col_ids = jnp.arange(col_count, dtype=jnp.int32)
    phases = jnp.remainder(row_ids[:, None] * (2 * col_ids[None, :] + 1), 4 * length).astype(
        jnp.float32
    )
    angles = phases * (jnp.pi / (2.0 * length))
    norm_scale = jnp.where(row_ids == 0, 1.0 / length, 2.0 / length).astype(jnp.float32)
    return jnp.sqrt(norm_scale)[:, None] * jnp.cos(angles)


def eigen_values(length, first_mode, mode_count):
    modes = (first_mode + jnp.arange(mode_count, dtype=jnp.int32)).astype(jnp.float32)
    return 2.0 - 2.0 * jnp.cos(modes * (jnp.pi / length))


def to_block(bricks, x_bricks, y_bricks, z_cells, x_rows):
    channels = bricks.shape[1]
    col_cells = bricks.shape[3]
    shaped = bricks.reshape(x_bricks, y_bricks, channels, z_cells, x_rows, col_cells)
    shaped = jnp.transpose(shaped, (2, 3, 0, 4, 1, 5))
    return shaped.reshape(channels, z_cells, x_bricks * x_rows, y_bricks * col_cells)


def operate(values_in, coefs):
    face_z, face_x, face_y, diagonal = coefs
    padded = padded_2(values_in, (("gx", 1), (YZ, 0)), 1)
    nearby = face_z[:-1] * padded[:-2, 1:-1] + face_z[1:] * padded[2:, 1:-1]
    nearby = nearby + face_x[:, :-1] * padded[1:-1, :-2] + face_x[:, 1:] * padded[1:-1, 2:]
    nearby = (
        nearby
        + face_y * jnp.roll(values_in, -1, 2)
        + jnp.roll(face_y, 1, 2) * jnp.roll(values_in, 1, 2)
    )
    return diagonal * values_in - nearby


def precondition(residual, fluid_cells, table_y, table_x):
    y_cells = residual.shape[2]
    spectrum = jnp.einsum("zxy,ky->zxk", residual, table_y, precision=highest)
    pencil = lax.all_to_all(spectrum, "gx", split_axis=2, concat_axis=1, tiled=True)
    y_part = pencil.shape[2]
    first_y = lax.axis_index("gx") * y_part
    denom = (
        spectral_gain
        * (eigen_values(NX, 0, NX)[:, None] + eigen_values(y_cells, first_y, y_part)[None, :])
        + spectral_floor
    )
    modes = jnp.einsum("kx,zxy->zky", table_x, pencil, precision=highest) / denom[None]
    spatial = jnp.einsum("kx,zky->zxy", table_x, modes, precision=highest)
    mixed = lax.all_to_all(spatial, "gx", split_axis=1, concat_axis=2, tiled=True)
    spatial_out = jnp.einsum("zxk,ky->zxy", mixed, table_y, precision=highest)
    return fluid_cells * spatial_out


def paired(residual, update, image_of):
    return (
        one_axis_at_a_time(jnp.sum(residual * update), GX_YZ),
        one_axis_at_a_time(jnp.sum(image_of * update), GX_YZ),
    )


def on_device(camera_accel, camera_weight, brick_slot, brick_solid):
    owner_count = lax.axis_size(YZ)
    slot_count = brick_slot.shape[1]
    per_owner = 3 * slot_count // (2 * owner_count)
    row_cells = camera_weight.shape[2]
    col_cells = camera_weight.shape[3]
    z_cells = row_cells // BR
    x_bricks = NX // lax.axis_size("gx") // BR
    y_bricks = NY // B
    brick_ids = brick_slot[0]
    owners_of = brick_ids // slot_count
    owner_ids = jnp.arange(owner_count, dtype=jnp.int32)
    one_hot = (owners_of[:, None] == owner_ids[None, :]).astype(jnp.int32)
    earlier = jnp.cumsum(one_hot, axis=0) - one_hot
    target = owners_of * per_owner + jnp.sum(earlier * one_hot, axis=1)
    positions = jnp.arange(owner_count * per_owner, dtype=jnp.int32)
    matches = target[None, :] == positions[:, None]
    filled = jnp.any(matches, axis=1)
    source = jnp.sum(
        jnp.where(matches, jnp.arange(slot_count, dtype=jnp.int32)[None, :], 0), axis=1
    )
    send_ids = jnp.where(filled, brick_ids[source] % slot_count, -1).reshape(owner_count, per_owner)
    send_accel = jnp.where(filled[:, None, None, None], camera_accel[0][source], 0.0)
    send_accel = send_accel.reshape(owner_count, per_owner, 3, row_cells, col_cells)
    send_weight = jnp.where(filled[:, None, None], camera_weight[0][source], 0.0)
    send_weight = send_weight.reshape(owner_count, per_owner, row_cells, col_cells)
    recv_ids, recv_accel, recv_weight = (
        lax.all_to_all(send_ids, YZ, split_axis=0, concat_axis=0, tiled=True),
        lax.all_to_all(send_accel, YZ, split_axis=0, concat_axis=0, tiled=True),
        lax.all_to_all(send_weight, YZ, split_axis=0, concat_axis=0, tiled=True),
    )
    flat_ids = recv_ids.reshape(-1)
    wanted = jnp.arange(slot_count, dtype=jnp.int32)
    arrived = flat_ids[None, :] == wanted[:, None]
    anchor = jnp.sum(
        jnp.where(arrived, jnp.arange(flat_ids.shape[0], dtype=jnp.int32)[None, :], 0), axis=1
    )
    fluid_bricks = (1 - brick_solid[0]).astype(jnp.float32)
    accel_bricks = recv_accel.reshape(-1, 3, row_cells, col_cells)[anchor]
    weight_bricks = recv_weight.reshape(-1, 1, row_cells, col_cells)[anchor]
    payload = (
        jnp.concatenate([accel_bricks, weight_bricks], axis=1) * fluid_bricks[:, None, None, None]
    )
    fields = to_block(payload, x_bricks, y_bricks, z_cells, BR)
    fluid_tiles = jnp.broadcast_to(
        fluid_bricks[:, None, None, None], (slot_count, 1, row_cells, col_cells)
    )
    fluid_cells = to_block(fluid_tiles, x_bricks, y_bricks, z_cells, BR)[0]
    weight = fields[3]
    rim_stack = padded_2(jnp.stack([weight, fields[0], fields[1]]), (("gx", 2), (YZ, 1)), 1)
    rim_weight = rim_stack[0]
    face_z = jnp.sqrt(rim_weight[:-1, 1:-1] * rim_weight[1:, 1:-1])
    face_x = jnp.sqrt(rim_weight[1:-1, :-1] * rim_weight[1:-1, 1:])
    y_index = jnp.arange(weight.shape[2], dtype=jnp.int32)
    face_y = jnp.where(
        y_index < weight.shape[2] - 1, jnp.sqrt(weight * jnp.roll(weight, -1, 2)), 0.0
    )
    flux_z = face_z * (rim_stack[1][:-1, 1:-1] + rim_stack[1][1:, 1:-1]) * 0.5
    flux_x = face_x * (rim_stack[2][1:-1, :-1] + rim_stack[2][1:-1, 1:]) * 0.5
    flux_y = face_y * (fields[2] + jnp.roll(fields[2], -1, 2)) * 0.5
    source_term = (
        flux_z[:-1] - flux_z[1:] + flux_x[:, :-1] - flux_x[:, 1:] + jnp.roll(flux_y, 1, 2) - flux_y
    )
    diagonal = shift_rate * weight + (1.0 - fluid_cells) + face_z[:-1] + face_z[1:]
    diagonal = diagonal + face_x[:, :-1] + face_x[:, 1:] + face_y + jnp.roll(face_y, 1, 2)
    coefs = (face_z, face_x, face_y, diagonal)
    table_y = cosine_table(NY, NY, NY)
    table_x = cosine_table(NX, NX, NX)
    solution = jnp.zeros_like(source_term)
    residual = source_term
    update = precondition(residual, fluid_cells, table_y, table_x)
    image_of = operate(update, coefs)
    energy_now, curvature = paired(residual, update, image_of)
    step_size = energy_now / curvature
    direction = update
    along_dir = image_of
    for step_index in range(ITERS):
        solution = solution + step_size * direction
        residual = residual - step_size * along_dir
        if step_index + 1 < ITERS:
            update = precondition(residual, fluid_cells, table_y, table_x)
            image_of = operate(update, coefs)
            energy_next, curvature = paired(residual, update, image_of)
            beta_ratio = energy_next / energy_now
            step_size = energy_next / (curvature - beta_ratio * energy_next / step_size)
            direction = update + beta_ratio * direction
            along_dir = image_of + beta_ratio * along_dir
            energy_now = energy_next
    return (solution, residual)


def solution(mesh):
    finer = Mesh(mesh.devices.reshape(mesh.shape["gx"], 4, 4, 2), ("gx", "yz_0", "yz_1", "yz_2"))
    in_specs = (P("gx", YZ, None, None, None), P("gx", YZ, None, None), P("gx", YZ), P("gx", YZ))
    out_specs = (P(YZ, "gx", None), P(YZ, "gx", None))
    return jax.shard_map(
        on_device, mesh=finer, in_specs=in_specs, out_specs=out_specs, check_vma=False
    )
```

profile of v0, /device:TPU:1, one launch (start us, length us, event | category | flops | bytes accessed | tf_op | source)
XLA Modules:
  0.0 489.5 jit_solution(8973376226336064747)
XLA Ops:
  2.7 1.6 gather_fusion.1
  5.1 8.6 %all-to-all-start.1 = ((s32[32,1,3]{2,1,0:T(1,128)}), s32[32,1,3]{2,1,0:T(1,128)S(1)}, u32[]{:S(2)}, u32[]{:S(2)}) async-start(s32[32,1,3]{2,1,0:T(1,128)} %bitcast.8), calls=%async_computation.1 | async-start | bytes 32768 | tf_op jit(solution)/shard_map/all_to_all | solution.py:137
  13.8 1.7 gather_fusion.3
  16.6 4.0 all-to-all-done.1
  20.6 4.2 all-to-all-start.2
  24.8 2.1 gather_fusion
  27.0 3.3 broadcast_select_fusion
  30.3 8.9 %all-to-all-done.2 = f32[32,3,16,128]{3,2,1,0:T(8,128)S(1)} async-done(((f32[32,3,16,128]{3,2,1,0:T(8,128)}), f32[32,3,16,128]{3,2,1,0:T(8,128)S(1)}, u32[]{:S(2)}, u32[]{:S(2)}) %all-to-all-start.2) | async-done | bytes 786464 | tf_op jit(solution)/shard_map/all_to_all | solution.py:139
  39.2 4.6 all-to-all-start
  46.0 28.8 %all-to-all-done = f32[32,3,3,16,128]{4,3,2,1,0:T(8,128)} async-done(((f32[32,3,3,16,128]{4,3,2,1,0:T(8,128)}), f32[32,3,3,16,128]{4,3,2,1,0:T(8,128)}, u32[]{:S(2)}, u32[]{:S(2)}) %all-to-all-start) | async-done | bytes 2359328 | tf_op jit(solution)/shard_map/all_to_all | solution.py:138
  74.8 3.5 gather_fusion.2
  78.3 1.6 fusion.8
  83.4 2.0 copy.46
  88.3 2.3 collective-permute-start
  90.6 3.1 collective-permute-start.3
  94.9 1.2 copy.48
  97.5 3.5 collective-permute-start.1
  101.0 1.3 collective-permute-start.2
  102.3 1.3 fusion.80
  103.8 2.2 collective-permute-done.2
  106.0 2.3 collective-permute-done
  108.3 4.4 collective-permute-done.3
  112.7 2.5 select_maximum_fusion
  115.9 1.6 fusion.44
  118.9 19.4 %fusion.23 = f32[128,1024]{0,1:T(8,128)} fusion(s32[1024]{0:T(1024)S(1)} %multiply_add_fusion.1, f32[1024]{0:T(1024)S(1)} %get-tuple-element.52, f32[1,128,1024]{2,1,0:T(8,128)S(1)} %fusion.76), kind=kOutput, calls=%fused_computation.29 | convolution fusion | flops 1626341376 | bytes 1056768 | tf_op jit(solution)/shard_map/zxy,ky->zxk/dot_general | solution.py:87
  138.3 8.3 %all-to-all-start.3 = ((f32[1,128,1024]{1,0,2:T(1,128)}), f32[1,128,1024]{1,0,2:T(1,128)S(1)}, u32[]{:S(2)}, u32[]{:S(2)}) async-start(f32[1,128,1024]{1,0,2:T(1,128)} %bitcast.151), calls=%async_computation.3 | async-start | bytes 1048576 | tf_op jit(solution)/shard_map/all_to_all | solution.py:88
  146.7 11.9 %all-to-all-done.3 = f32[1,128,1024]{1,0,2:T(1,128)S(1)} async-done(((f32[1,128,1024]{1,0,2:T(1,128)}), f32[1,128,1024]{1,0,2:T(1,128)S(1)}, u32[]{:S(2)}, u32[]{:S(2)}) %all-to-all-start.3) | async-done | bytes 524320 | tf_op jit(solution)/shard_map/all_to_all | solution.py:88
  159.6 20.3 %fusion.55 = f32[1024,128]{0,1:T(8,128)S(1)} fusion(f32[1024,128]{1,0:T(8,128)} %bitcast.155, s32[1024]{0:T(1024)S(1)} %multiply_add_fusion.1, f32[1024]{0:T(1024)S(1)} %get-tuple-element.52, f32[128]{0:T(128)S(1)} %multiply_subtract_fusion.4, f32[1024]{0:T(1024)S(1)} %get-tuple-element.51), kind=kOutput, calls=%fused_computation.48 | convolution fusion | flops 1626734592 | bytes 1061376 | tf_op jit(solution)/shard_map/kx,zxy->zky/dot_general | solution.py:96
  179.9 18.4 %fusion.28 = f32[1,1024,128]{1,2,0:T(8,128)S(1)} fusion(f32[1024,128]{0,1:T(8,128)S(1)} %fusion.55, s32[1024]{0:T(1024)S(1)} %multiply_add_fusion.1, f32[1024]{0:T(1024)S(1)} %get-tuple-element.52), kind=kOutput, calls=%fused_computation.34 | convolution fusion | flops 1626341376 | bytes 1056768 | tf_op jit(solution)/shard_map/kx,zky->zxy/dot_general | solution.py:97
  199.4 3.5 all-to-all-start.4
  203.8 1.9 sub.88
  205.8 10.3 %all-to-all-done.4 = f32[1,1024,128]{2,0,1:T(1,128)S(1)} async-done(((f32[1,1024,128]{2,0,1:T(1,128)}), f32[1,1024,128]{2,0,1:T(1,128)S(1)}, u32[]{:S(2)}, u32[]{:S(2)}) %all-to-all-start.4) | async-done | bytes 524320 | tf_op jit(solution)/shard_map/all_to_all | solution.py:98
  217.2 19.2 %fusion.37 = f32[128,1024]{1,0:T(8,128)S(1)} fusion(f32[128,1024]{0,1:T(8,128)} %bitcast.153, s32[1024]{0:T(1024)S(1)} %multiply_add_fusion.1, f32[1024]{0:T(1024)S(1)} %get-tuple-element.52, f32[16,8,8,128]{3,2,1,0:T(8,128)S(1)} %bitcast.149), kind=kOutput, calls=%fused_computation.37 | convolution fusion | flops 1626472448 | bytes 1581056 | tf_op jit(solution)/shard_map/zxk,ky->zxy/dot_general | solution.py:99
  236.5 13.4 %collective-permute-start.4 = (f32[1,128,1024]{2,1,0:T(8,128)S(1)}, f32[1,128,1024]{2,1,0:T(8,128)S(1)}, u32[]{:S(2)}, u32[]{:S(2)}) collective-permute-start(f32[1,128,1024]{2,1,0:T(8,128)S(1)} %bitcast.130), channel_id=1, source_target_pairs={{0,1},{1,2},{2,3},{3,4},{4,5},{5,6},{6,7},{7,8},{8,9},{9,10},{10,1... | collective-permute-start | bytes 1572872 | tf_op jit(solution)/shard_map/ppermute | solution.py:32
  250.0 1.9 collective-permute-start.5
  251.9 2.2 collective-permute-start.6
  254.1 1.3 collective-permute-start.7
  255.7 2.8 collective-permute-done.7
  258.5 2.3 collective-permute-done.5
  260.8 2.3 multiply_reduce_fusion.2
  263.1 11.8 %all-reduce.3 = (f32[]{:T(128)}, f32[]{:T(128)}) all-reduce(f32[]{:T(128)} %get-tuple-element.5, f32[]{:T(128)} %get-tuple-element.4), channel_id=1, replica_groups=mesh['gx'=8,'yz_0'=4,'yz_1'=4,'yz_2'=2] {'gx'}, use_global_device_ids=true, to_apply=%region_6.7 | all-reduce | flops 2 | bytes 16 | tf_op jit(solution)/shard_map/psum | solution.py:45
  274.9 6.7 %all-reduce.7 = (f32[]{:T(128)}, f32[]{:T(128)}) all-reduce(f32[]{:T(128)} %get-tuple-element.8, f32[]{:T(128)} %get-tuple-element.9), channel_id=1, replica_groups=mesh['gx'=8,'yz_0'=4,'yz_1'=4,'yz_2'=2] {'yz_0'}, use_global_device_ids=true, to_apply=%region_7.8 | all-reduce | flops 2 | bytes 16 | tf_op jit(solution)/shard_map/psum | solution.py:45
  281.6 8.7 %all-reduce.5 = (f32[]{:T(128)}, f32[]{:T(128)}) all-reduce(f32[]{:T(128)} %get-tuple-element.16, f32[]{:T(128)} %get-tuple-element.17), channel_id=1, replica_groups=mesh['gx'=8,'yz_0'=4,'yz_1'=4,'yz_2'=2] {'yz_1'}, use_global_device_ids=true, to_apply=%region_8.9 | all-reduce | flops 2 | bytes 16 | tf_op jit(solution)/shard_map/psum | solution.py:45
  290.3 9.4 %all-reduce.9 = (f32[]{:T(128)}, f32[]{:T(128)}) all-reduce(f32[]{:T(128)} %get-tuple-element.12, f32[]{:T(128)} %get-tuple-element.13), channel_id=1, replica_groups=mesh['gx'=8,'yz_0'=4,'yz_1'=4,'yz_2'=2] {'yz_2'}, use_global_device_ids=true, to_apply=%region_9.10 | all-reduce | flops 2 | bytes 16 | tf_op jit(solution)/shard_map/psum | solution.py:45
  300.9 19.5 %fusion.15 = f32[128,1024]{0,1:T(8,128)S(1)} fusion(s32[1024]{0:T(1024)S(1)} %multiply_add_fusion.1, f32[1024]{0:T(1024)S(1)} %get-tuple-element.52, f32[1,128,1024]{2,1,0:T(8,128)} %copy-done.7, f32[1,128,1024]{2,1,0:T(8,128)} %get-tuple-element.23, f32[]{:T(128)S(6)} %div.47), kind=kOutput, calls=%fused_computation.25 | convolution fusion | flops 1626603520 | bytes 1581060 | tf_op jit(solution)/shard_map/zxy,ky->zxk/dot_general | solution.py:87
  320.4 22.1 %all_to_all.76 = f32[1,128,1024]{1,0,2:T(1,128)S(1)} all-to-all(f32[1,128,1024]{1,0,2:T(1,128)S(1)} %bitcast.156), channel_id=1, replica_groups=mesh['gx'=8,'yz_0'=4,'yz_1'=4,'yz_2'=2] {'gx'}, dimensions={2} | all-to-all | bytes 1048576 | tf_op jit(solution)/shard_map/all_to_all | solution.py:88
  343.6 20.5 %fusion.49 = f32[1024,128]{0,1:T(8,128)S(1)} fusion(f32[1024,128]{1,0:T(8,128)} %bitcast.154, s32[1024]{0:T(1024)S(1)} %multiply_add_fusion.1, f32[1024]{0:T(1024)S(1)} %get-tuple-element.52, f32[128]{0:T(128)S(1)} %multiply_subtract_fusion.4, f32[1024]{0:T(1024)S(1)} %get-tuple-element.51), kind=kOutput, calls=%fused_computation.46 | convolution fusion | flops 1626734592 | bytes 1061376 | tf_op jit(solution)/shard_map/kx,zxy->zky/dot_general | solution.py:96
  364.0 18.9 %fusion.34 = f32[1,1024,128]{1,2,0:T(8,128)} fusion(f32[1024,128]{0,1:T(8,128)S(1)} %fusion.49, s32[1024]{0:T(1024)S(1)} %multiply_add_fusion.1, f32[1024]{0:T(1024)S(1)} %get-tuple-element.52), kind=kOutput, calls=%fused_computation.36 | convolution fusion | flops 1626341376 | bytes 1056768 | tf_op jit(solution)/shard_map/kx,zky->zxy/dot_general | solution.py:97
  383.0 1.2 copy.55
  384.2 18.4 %all_to_all.77 = f32[1,1024,128]{2,0,1:T(1,128)} all-to-all(f32[1,1024,128]{2,0,1:T(1,128)S(1)} %copy.55), channel_id=1, replica_groups=mesh['gx'=8,'yz_0'=4,'yz_1'=4,'yz_2'=2] {'gx'}, dimensions={1} | all-to-all | bytes 1048576 | tf_op jit(solution)/shard_map/all_to_all | solution.py:98
  402.6 2.0 copy.56
  404.7 19.5 %fusion.40 = f32[128,1024]{1,0:T(8,128)S(1)} fusion(f32[128,1024]{0,1:T(8,128)} %bitcast.152, s32[1024]{0:T(1024)S(1)} %multiply_add_fusion.1, f32[1024]{0:T(1024)S(1)} %get-tuple-element.52, f32[16,8,8,128]{3,2,1,0:T(8,128)} %bitcast.150), kind=kOutput, calls=%fused_computation.38 | convolution fusion | flops 1626472448 | bytes 1581056 | tf_op jit(solution)/shard_map/zxk,ky->zxy/dot_general | solution.py:99
  424.2 6.0 %collective-permute-start.8 = (f32[1,128,1024]{2,1,0:T(8,128)S(1)}, f32[1,128,1024]{2,1,0:T(8,128)S(1)}, u32[]{:S(2)}, u32[]{:S(2)}) collective-permute-start(f32[1,128,1024]{2,1,0:T(8,128)S(1)} %bitcast.124), channel_id=1, source_target_pairs={{0,1},{1,2},{2,3},{3,4},{4,5},{5,6},{6,7},{7,8},{8,9},{9,10},{10,1... | collective-permute-start | bytes 1572872 | tf_op jit(solution)/shard_map/ppermute | solution.py:32
  430.2 1.9 collective-permute-start.9
  432.1 2.2 collective-permute-start.10
  434.3 1.3 collective-permute-start.11
  435.9 2.8 collective-permute-done.11
  438.7 2.0 collective-permute-done.9
  440.7 2.4 multiply_reduce_fusion
  443.2 12.0 %all-reduce.2 = (f32[]{:T(128)}, f32[]{:T(128)}) all-reduce(f32[]{:T(128)} %get-tuple-element.3, f32[]{:T(128)} %get-tuple-element.2), channel_id=1, replica_groups=mesh['gx'=8,'yz_0'=4,'yz_1'=4,'yz_2'=2] {'gx'}, use_global_device_ids=true, to_apply=%region_16.17 | all-reduce | flops 2 | bytes 16 | tf_op jit(solution)/shard_map/psum | solution.py:45
  455.1 6.7 %all-reduce.6 = (f32[]{:T(128)}, f32[]{:T(128)}) all-reduce(f32[]{:T(128)} %get-tuple-element.6, f32[]{:T(128)} %get-tuple-element.7), channel_id=1, replica_groups=mesh['gx'=8,'yz_0'=4,'yz_1'=4,'yz_2'=2] {'yz_0'}, use_global_device_ids=true, to_apply=%region_17.18 | all-reduce | flops 2 | bytes 16 | tf_op jit(solution)/shard_map/psum | solution.py:45
  461.8 10.9 %all-reduce.4 = (f32[]{:T(128)}, f32[]{:T(128)}) all-reduce(f32[]{:T(128)} %get-tuple-element.14, f32[]{:T(128)} %get-tuple-element.15), channel_id=1, replica_groups=mesh['gx'=8,'yz_0'=4,'yz_1'=4,'yz_2'=2] {'yz_1'}, use_global_device_ids=true, to_apply=%region_18.19 | all-reduce | flops 2 | bytes 16 | tf_op jit(solution)/shard_map/psum | solution.py:45
  472.7 8.9 %all-reduce.8 = (f32[]{:T(128)}, f32[]{:T(128)}) all-reduce(f32[]{:T(128)} %get-tuple-element.10, f32[]{:T(128)} %get-tuple-element.11), channel_id=1, replica_groups=mesh['gx'=8,'yz_0'=4,'yz_1'=4,'yz_2'=2] {'yz_2'}, use_global_device_ids=true, to_apply=%region_19.20 | all-reduce | flops 2 | bytes 16 | tf_op jit(solution)/shard_map/psum | solution.py:45
  487.0 2.3 multiply_subtract_fusion
  (99 shorter events, 24.1 us)
Async XLA Ops:
  0.6 24.2 %copy-start = (f32[1,64,3,16,128]{4,3,2,1,0:T(8,128)S(1)}, f32[1,64,3,16,128]{4,3,2,1,0:T(8,128)}, u32[]{:S(2)}) copy-start(f32[1,64,3,16,128]{4,3,2,1,0:T(8,128)} %param.4) | copy-start | bytes 4718596
  5.1 15.5 %all-to-all-start.1 = ((s32[32,1,3]{2,1,0:T(1,128)}), s32[32,1,3]{2,1,0:T(1,128)S(1)}, u32[]{:S(2)}, u32[]{:S(2)}) async-start(s32[32,1,3]{2,1,0:T(1,128)} %bitcast.8), calls=%async_computation.1 | async-start | bytes 32768 | tf_op jit(solution)/shard_map/all_to_all | solution.py:137
  20.6 18.6 %all-to-all-start.2 = ((f32[32,3,16,128]{3,2,1,0:T(8,128)}), f32[32,3,16,128]{3,2,1,0:T(8,128)S(1)}, u32[]{:S(2)}, u32[]{:S(2)}) async-start(f32[32,3,16,128]{3,2,1,0:T(8,128)} %broadcast_select_fusion.1), calls=%async_computation.2 | async-start | bytes 1572864 | tf_op jit(solution)/shard_map/all_to_all | solution.py:139
  27.0 16.8 %copy-start.15 = (s32[1,64]{1,0:T(1,128)S(1)}, s32[1,64]{1,0:T(1,128)}, u32[]{:S(2)}) copy-start(s32[1,64]{1,0:T(1,128)} %param.7) | copy-start | bytes 772
  39.2 35.6 %all-to-all-start = ((f32[32,3,3,16,128]{4,3,2,1,0:T(8,128)}), f32[32,3,3,16,128]{4,3,2,1,0:T(8,128)}, u32[]{:S(2)}, u32[]{:S(2)}) async-start(f32[32,3,3,16,128]{4,3,2,1,0:T(8,128)} %broadcast_select_fusion), calls=%async_computation | async-start | bytes 4718592 | tf_op jit(solution)/shard_map/all_to_all | solution.py:138
  88.3 20.0 %collective-permute-start = (f32[3,1,128,1024]{3,2,1,0:T(8,128)}, f32[3,1,128,1024]{3,2,1,0:T(8,128)}, u32[]{:S(2)}, u32[]{:S(2)}) collective-permute-start(f32[3,1,128,1024]{3,2,1,0:T(8,128)} %constant_dynamic-update-slice_fusion), channel_id=1, source_target_pairs={{0,1},{1,2},{2,3},{3,4},{4,5},{5,6},{6,7},{7,8},{8,9},{9,10},{10,1... | collective-permute-start | bytes 4718600 | tf_op jit(solution)/shard_map/ppermute | solution.py:32
  90.6 22.1 %collective-permute-start.3 = (f32[3,1,128,1024]{3,2,1,0:T(8,128)}, f32[3,1,128,1024]{3,2,1,0:T(8,128)}, u32[]{:S(2)}, u32[]{:S(2)}) collective-permute-start(f32[3,1,128,1024]{3,2,1,0:T(8,128)} %constant_dynamic-update-slice_fusion), channel_id=1, source_target_pairs={{1,0},{2,1},{3,2},{4,3},{5,4},{6,5},{7,6},{8,7},{9,8},{10,9},{11,1... | collective-permute-start | bytes 4718600 | tf_op jit(solution)/shard_map/ppermute | solution.py:33
  96.2 16.5 %copy-start.13 = (f32[3,1,128,1024]{3,2,1,0:T(8,128)S(1)}, f32[3,1,128,1024]{3,2,1,0:T(8,128)}, u32[]{:S(2)}) copy-start(f32[3,1,128,1024]{3,2,1,0:T(8,128)} %constant_dynamic-update-slice_fusion) | copy-start | bytes 4718596
  97.5 6.3 %collective-permute-start.1 = (f32[3,1,1,1024]{3,2,1,0:T(1,128)S(1)}, f32[3,1,1,1024]{3,2,1,0:T(1,128)S(1)}, u32[]{:S(2)}, u32[]{:S(2)}) collective-permute-start(f32[3,1,1,1024]{3,2,1,0:T(1,128)S(1)} %get-tuple-element.37), channel_id=1, source_target_pairs={{0,32},{32,64},{64,96},{96,128},{128,160},{160,192},{192,224},{1,3... | collective-permute-start | bytes 36872 | tf_op jit(solution)/shard_map/ppermute | solution.py:32
  101.0 4.9 %collective-permute-start.2 = (f32[3,1,1,1024]{3,2,1,0:T(1,128)S(1)}, f32[3,1,1,1024]{3,2,1,0:T(1,128)S(1)}, u32[]{:S(2)}, u32[]{:S(2)}) collective-permute-start(f32[3,1,1,1024]{3,2,1,0:T(1,128)S(1)} %get-tuple-element.38), channel_id=1, source_target_pairs={{32,0},{64,32},{96,64},{128,96},{160,128},{192,160},{224,192},{33,... | collective-permute-start | bytes 36872 | tf_op jit(solution)/shard_map/ppermute | solution.py:33
  103.7 157.1 %copy-start.1 = (f32[1,128,1024]{2,1,0:T(8,128)}, f32[1,128,1024]{2,1,0:T(8,128)S(1)}, u32[]{:S(2)}) copy-start(f32[1,128,1024]{2,1,0:T(8,128)S(1)} %get-tuple-element.29) | copy-start | bytes 1572868
  118.9 19.4 %copy-start.7 = (f32[1,128,1024]{2,1,0:T(8,128)}, f32[1,128,1024]{2,1,0:T(8,128)S(1)}, u32[]{:S(2)}) copy-start(f32[1,128,1024]{2,1,0:T(8,128)S(1)} %fusion.76) | copy-start | bytes 1572868
  138.3 20.3 %all-to-all-start.3 = ((f32[1,128,1024]{1,0,2:T(1,128)}), f32[1,128,1024]{1,0,2:T(1,128)S(1)}, u32[]{:S(2)}, u32[]{:S(2)}) async-start(f32[1,128,1024]{1,0,2:T(1,128)} %bitcast.151), calls=%async_computation.3 | async-start | bytes 1048576 | tf_op jit(solution)/shard_map/all_to_all | solution.py:88
  199.4 16.7 %all-to-all-start.4 = ((f32[1,1024,128]{2,0,1:T(1,128)}), f32[1,1024,128]{2,0,1:T(1,128)S(1)}, u32[]{:S(2)}, u32[]{:S(2)}) async-start(f32[1,1024,128]{2,0,1:T(1,128)} %copy.51), calls=%async_computation.4 | async-start | bytes 1048576 | tf_op jit(solution)/shard_map/all_to_all | solution.py:98
  217.2 19.3 %copy-start.14 = (f32[8,16,8,128]{3,2,1,0:T(8,128)}, f32[8,16,8,128]{3,2,1,0:T(8,128)S(1)}, u32[]{:S(2)}) copy-start(f32[8,16,8,128]{3,2,1,0:T(8,128)S(1)} %transpose.39) | copy-start | bytes 1572868
  217.2 43.5 %copy-start.3 = (f32[1,129,1024]{2,1,0:T(8,128)S(1)}, f32[1,129,1024]{2,1,0:T(8,128)}, u32[]{:S(2)}) copy-start(f32[1,129,1024]{2,1,0:T(8,128)} %get-tuple-element.27) | copy-start | bytes 1585156
  217.2 43.5 %copy-start.5 = (f32[2,128,1024]{2,1,0:T(8,128)S(1)}, f32[2,128,1024]{2,1,0:T(8,128)}, u32[]{:S(2)}) copy-start(f32[2,128,1024]{2,1,0:T(8,128)} %get-tuple-element.25) | copy-start | bytes 3145732
  217.2 43.5 %copy-start.8 = (f32[1,128,1024]{2,1,0:T(8,128)S(1)}, f32[1,128,1024]{2,1,0:T(8,128)}, u32[]{:S(2)}) copy-start(f32[1,128,1024]{2,1,0:T(8,128)} %copy-done.7) | copy-start | bytes 1572868
  217.2 43.5 %copy-start.10 = (f32[1,128,1024]{2,1,0:T(8,128)S(1)}, f32[1,128,1024]{2,1,0:T(8,128)}, u32[]{:S(2)}) copy-start(f32[1,128,1024]{2,1,0:T(8,128)} %sub.88) | copy-start | bytes 1572868
  236.5 22.0 %collective-permute-start.4 = (f32[1,128,1024]{2,1,0:T(8,128)S(1)}, f32[1,128,1024]{2,1,0:T(8,128)S(1)}, u32[]{:S(2)}, u32[]{:S(2)}) collective-permute-start(f32[1,128,1024]{2,1,0:T(8,128)S(1)} %bitcast.130), channel_id=1, source_target_pairs={{0,1},{1,2},{2,3},{3,4},{4,5},{5,6},{6,7},{7,8},{8,9},{9,10},{10,1... | collective-permute-start | bytes 1572872 | tf_op jit(solution)/shard_map/ppermute | solution.py:32
  250.0 10.8 %collective-permute-start.5 = (f32[1,128,1024]{2,1,0:T(8,128)S(1)}, f32[1,128,1024]{2,1,0:T(8,128)S(1)}, u32[]{:S(2)}, u32[]{:S(2)}) collective-permute-start(f32[1,128,1024]{2,1,0:T(8,128)S(1)} %bitcast.131), channel_id=1, source_target_pairs={{1,0},{2,1},{3,2},{4,3},{5,4},{6,5},{7,6},{8,7},{9,8},{10,9},{11,1... | collective-permute-start | bytes 1572872 | tf_op jit(solution)/shard_map/ppermute | solution.py:33
  251.9 3.8 collective-permute-start.6
  254.1 4.4 collective-permute-start.7
  404.6 36.1 %copy-start.2 = (f32[1,128,1024]{2,1,0:T(8,128)S(1)}, f32[1,128,1024]{2,1,0:T(8,128)}, u32[]{:S(2)}) copy-start(f32[1,128,1024]{2,1,0:T(8,128)} %copy-done.1) | copy-start | bytes 1572868
  404.6 36.1 %copy-start.4 = (f32[1,129,1024]{2,1,0:T(8,128)S(1)}, f32[1,129,1024]{2,1,0:T(8,128)}, u32[]{:S(2)}) copy-start(f32[1,129,1024]{2,1,0:T(8,128)} %get-tuple-element.27) | copy-start | bytes 1585156
  404.6 36.1 %copy-start.6 = (f32[2,128,1024]{2,1,0:T(8,128)S(1)}, f32[2,128,1024]{2,1,0:T(8,128)}, u32[]{:S(2)}) copy-start(f32[2,128,1024]{2,1,0:T(8,128)} %get-tuple-element.25) | copy-start | bytes 3145732
  404.6 36.1 %copy-start.9 = (f32[1,128,1024]{2,1,0:T(8,128)S(1)}, f32[1,128,1024]{2,1,0:T(8,128)}, u32[]{:S(2)}) copy-start(f32[1,128,1024]{2,1,0:T(8,128)} %copy-done.7) | copy-start | bytes 1572868
  404.6 36.1 %copy-start.11 = (f32[1,128,1024]{2,1,0:T(8,128)S(1)}, f32[1,128,1024]{2,1,0:T(8,128)}, u32[]{:S(2)}) copy-start(f32[1,128,1024]{2,1,0:T(8,128)} %sub.88) | copy-start | bytes 1572868
  404.7 36.1 %copy-start.12 = (f32[1,128,1024]{2,1,0:T(8,128)S(1)}, f32[1,128,1024]{2,1,0:T(8,128)}, u32[]{:S(2)}) copy-start(f32[1,128,1024]{2,1,0:T(8,128)} %get-tuple-element.23) | copy-start | bytes 1572868
  424.2 14.5 %collective-permute-start.8 = (f32[1,128,1024]{2,1,0:T(8,128)S(1)}, f32[1,128,1024]{2,1,0:T(8,128)S(1)}, u32[]{:S(2)}, u32[]{:S(2)}) collective-permute-start(f32[1,128,1024]{2,1,0:T(8,128)S(1)} %bitcast.124), channel_id=1, source_target_pairs={{0,1},{1,2},{2,3},{3,4},{4,5},{5,6},{6,7},{7,8},{8,9},{9,10},{10,1... | collective-permute-start | bytes 1572872 | tf_op jit(solution)/shard_map/ppermute | solution.py:32
  430.2 10.5 %collective-permute-start.9 = (f32[1,128,1024]{2,1,0:T(8,128)S(1)}, f32[1,128,1024]{2,1,0:T(8,128)S(1)}, u32[]{:S(2)}, u32[]{:S(2)}) collective-permute-start(f32[1,128,1024]{2,1,0:T(8,128)S(1)} %bitcast.125), channel_id=1, source_target_pairs={{1,0},{2,1},{3,2},{4,3},{5,4},{6,5},{7,6},{8,7},{9,8},{10,9},{11,1... | collective-permute-start | bytes 1572872 | tf_op jit(solution)/shard_map/ppermute | solution.py:33
  432.1 3.8 collective-permute-start.10
  434.3 4.4 collective-permute-start.11
where the time goes:
time: 496 us; the launch traced here: 489 us
  matrix products  156 us (31%)
  blocking collectives  116 us (23%)
  waiting for transfers between devices  82.6 us (17%)
  starting transfers between devices  69.7 us (14%)
  local copies, waits for them, and re-layouts  34.4 us (7%)
  other arithmetic  24.3 us (5%)
  between operations  7.14 us (1%)
    psum x8, blocking collectives, one_axis_at_a_time(): return functools.reduce(lax.psum, axes, shard)  75 us
    dot_general x2, matrix products, precondition(): jnp.einsum('kx,zxy->zky', table_x, pencil, precision=highest) / denom[None]  40.8 us
    dot_general x2, matrix products, precondition(): spectrum = jnp.einsum('zxy,ky->zxk', residual, table_y, precision=highest)  38.9 us
    dot_general x2, matrix products, precondition(): spatial_out = jnp.einsum('zxk,ky->zxy', mixed, table_y, precision=highest)  38.8 us
    dot_general x2, matrix products, precondition(): spatial = jnp.einsum('kx,zky->zxy', table_x, modes, precision=highest)  37.4 us
    ppermute x6, starting transfers between devices, padded_2(): lax.ppermute(last, axis, up)  29.7 us
    all_to_all x1, waiting for transfers between devices, on_device(): lax.all_to_all(send_accel, YZ, split_axis=0, concat_axis=0, tiled=True)  28.8 us
    all_to_all x1, blocking collectives, precondition(): lax.all_to_all(spectrum, 'gx', split_axis=2, concat_axis=1, tiled=True)  22.1 us
  transfers between devices with their start and end apart: 17, of which 12 were waited for; matrix products, arithmetic and copies ran while one was open for 4% of the time, Pallas kernels for 0%

commit v1 on v0

v1 whole, which is shorter than its diff:
```python
import functools

import jax
import jax.numpy as jnp
import ml_dtypes
import numpy as np
from jax import lax
from jax.experimental import pallas as pl
from jax.experimental.pallas import tpu as pltpu
from jax.sharding import Mesh
from jax.sharding import PartitionSpec as P

N = 1024
H = N // 2
XL = 128
SLABS = 8
BR = 16
B = 128
PLANE_BRICKS = 64
OWNERS = 32
PER_PAIR = 3
BRICK_ROWS = 4 * BR
PAIR_ROWS = PER_PAIR * BRICK_ROWS
SEND_ROWS = PAIR_ROWS + 8
YZ = ("yz_0", "yz_1", "yz_2")
SHIFT_RATE = 0.05
FLOOR = 2.0
F32 = jnp.float32
BF16 = jnp.bfloat16
VMEM = pl.BlockSpec(memory_space=pltpu.VMEM)
SMEM = pl.BlockSpec(memory_space=pltpu.SMEM)
ANY = pl.BlockSpec(memory_space=pl.ANY)


def cosine_rows(length):
    k = np.arange(length, dtype=np.int64)[:, None]
    i = np.arange(length, dtype=np.int64)[None, :]
    m = (k * (2 * i + 1)) % (4 * length)
    scale = np.sqrt(np.where(k == 0, 1.0, 2.0) / length)
    return scale * np.cos(np.pi * m / (2.0 * length))


def two_bf16(table):
    high = table.astype(np.float32).astype(ml_dtypes.bfloat16)
    low = (table - high.astype(np.float64)).astype(np.float32).astype(ml_dtypes.bfloat16)
    return high, low


@functools.lru_cache(None)
def tables():
    out = {}
    big = cosine_rows(N)
    out["even"] = np.stack(two_bf16(big[0::2, :H]))
    out["odd"] = np.stack(two_bf16(big[1::2, :H]))
    small = cosine_rows(XL)
    out["small"] = np.concatenate(two_bf16(small), axis=0)
    out["small_t"] = np.concatenate(two_bf16(small.T.copy()), axis=0)
    lam_x = 2.0 - 2.0 * np.cos(np.pi * np.arange(XL) / XL)
    ky = np.concatenate([np.arange(0, N, 2), np.arange(1, N, 2)])
    lam_y = 2.0 - 2.0 * np.cos(np.pi * ky / N)
    column = np.zeros((XL, 128), np.float32)
    column[:, 0] = lam_x + FLOOR
    column[:, 1] = small[:, 0]
    column[:, 2] = small[:, XL - 1]
    out["column"] = column
    out["lam_y"] = lam_y.astype(np.float32)[None]
    denom = lam_x[:, None] + lam_y[None] + FLOOR
    near = np.sum(small[:, :1] ** 2 / denom, axis=0)
    far = np.sum(small[:, :1] * small[:, XL - 1 :] / denom, axis=0)
    cuts = SLABS - 1
    system = np.zeros((N, cuts, cuts))
    for j in range(cuts):
        system[:, j, j] = 1.0 + 2.0 * near
    for j in range(cuts - 1):
        system[:, j, j + 1] = -far
        system[:, j + 1, j] = -far
    inverse = np.linalg.inv(system)
    joined = np.zeros((SLABS + 3, SLABS, 2, N))
    for i in range(cuts):
        for j in range(cuts):
            joined[i + 2, j, 1] += inverse[:, i, j]
            joined[i + 2, j + 1, 0] -= inverse[:, i, j]
    out["cut"] = joined.astype(np.float32).reshape(SLABS + 3, SLABS, 16, 128)
    out["ends"] = np.stack([near, far]).astype(np.float32).reshape(2, 8, 128)
    return out


def split(value):
    high = value.astype(BF16)
    return high, (value - high.astype(F32)).astype(BF16)


def product(a, b, transposed=False):
    dims = (((1,), (1 if transposed else 0,)), ((), ()))
    return lax.dot_general(a, b, dims, preferred_element_type=F32)


def by_table(data, table_ref, transposed):
    high, low = split(data)
    rows = data.shape[0]
    both = product(jnp.concatenate([high, low], axis=0), table_ref[0], transposed)
    return both[:rows] + both[rows:] + product(high, table_ref[1], transposed)


def of_table(table_ref, data):
    high, low = split(data)
    both = product(table_ref[...], high)
    return both[:XL] + both[XL:] + product(table_ref[:XL], low)


def mirrored(value):
    rows, width = value.shape
    index = 127 - lax.broadcasted_iota(jnp.int32, (rows, 128), 1)
    tiles = [
        jnp.take_along_axis(value[:, t * 128 : (t + 1) * 128], index, axis=1)
        for t in range(width // 128)
    ]
    return jnp.concatenate(tiles[::-1], axis=1)


def as_tile(row):
    return jnp.concatenate([row[:, t * 128 : (t + 1) * 128] for t in range(8)], axis=0)


def as_row(tile):
    return jnp.concatenate([tile[t : t + 1] for t in range(8)], axis=1)


def to_modes(field_ref, even_ref, odd_ref, small_ref, column_ref, lam_ref, fold_ref, modes_ref, ends_ref):
    for i in range(XL // 8):
        rows = pl.ds(8 * i, 8)
        low = field_ref[rows, :H]
        high = mirrored(field_ref[rows, H:])
        fold_ref[rows, :H] = low + high
        fold_ref[rows, H:] = low - high
    spectrum = jnp.concatenate(
        [
            by_table(fold_ref[:, :H], even_ref, True),
            by_table(fold_ref[:, H:], odd_ref, True),
        ],
        axis=1,
    )
    modes_ref[...] = of_table(small_ref, spectrum)
    first = jnp.zeros((8, N), F32)
    last = jnp.zeros((8, N), F32)
    for i in range(XL // 8):
        rows = pl.ds(8 * i, 8)
        modes = modes_ref[rows, :] / (column_ref[rows, 0:1] + lam_ref[...])
        modes_ref[rows, :] = modes
        first = first + modes * column_ref[rows, 1:2]
        last = last + modes * column_ref[rows, 2:3]
    first = as_tile(jnp.sum(first, axis=0, keepdims=True))
    last = as_tile(jnp.sum(last, axis=0, keepdims=True))
    for j in range(SLABS):
        ends_ref[j, 0:8] = first
        ends_ref[j, 8:16] = last


def pack_kernel(slot_ref, accel_ref, weight_ref, out_ref, count_ref, sem):
    for o in range(OWNERS):
        count_ref[o] = 0
    out_ref[:, PAIR_ROWS:] = jnp.full((OWNERS, 8, 128), -1.0, F32)

    def one(s, carry):
        brick = slot_ref[s]
        owner = brick // PLANE_BRICKS
        place = count_ref[owner]
        count_ref[owner] = place + 1
        number = jnp.full((1, 128), brick - owner * PLANE_BRICKS, jnp.int32)
        out_ref[owner, pl.ds(PAIR_ROWS + place, 1), :] = number.astype(F32)
        at = pl.multiple_of(place * BRICK_ROWS, 16)
        pltpu.make_async_copy(accel_ref.at[s], out_ref.at[owner, pl.ds(at, 3 * BR)], sem).start()
        pltpu.make_async_copy(weight_ref.at[s], out_ref.at[owner, pl.ds(at + 3 * BR, BR)], sem).start()
        return carry

    lax.fori_loop(0, PLANE_BRICKS, one, 0)
    sent = out_ref.at[:, pl.ds(0, PLANE_BRICKS * BRICK_ROWS // OWNERS)]
    pltpu.make_async_copy(sent, sent, sem).wait()


def place_kernel(ids_ref, solid_ref, got_ref, fields_ref, first_ref, last_ref, sem):
    def one(s, carry):
        brick = ids_ref[s]

        @pl.when(brick >= 0)
        def _():
            x_at = pl.multiple_of((brick // 8) * BR, BR)
            y_at = pl.multiple_of((brick % 8) * B, B)
            source = s // PER_PAIR
            row = (s % PER_PAIR) * BRICK_ROWS
            for channel in range(4):
                at = pl.multiple_of(row + channel * BR, BR)
                pltpu.make_async_copy(
                    got_ref.at[source, pl.ds(at, BR)],
                    fields_ref.at[channel, pl.ds(x_at, BR), pl.ds(y_at, B)],
                    sem,
                ).start()

        return carry

    lax.fori_loop(0, OWNERS * PER_PAIR, one, 0)
    pltpu.make_async_copy(fields_ref, fields_ref, sem).wait()
    for i in range(PLANE_BRICKS):
        fluid = (1 - solid_ref[i]).astype(F32)
        rows = pl.ds((i // 8) * BR, BR)
        cols = pl.ds((i % 8) * B, B)
        for channel in range(4):
            fields_ref[channel, rows, cols] = fields_ref[channel, rows, cols] * fluid
    for ref, row in ((first_ref, 0), (last_ref, XL - 1)):
        ref[0:1] = fields_ref[3, row : row + 1]
        ref[1:2] = fields_ref[1, row : row + 1]


def setup_kernel(
    fields_ref, above_ref, below_ref, xlo_ref, xhi_ref, even_ref, odd_ref, small_ref, column_ref, lam_ref,
    faces_ref, source_ref, modes_ref, ends_ref, wext_ref, aext_ref, fold_ref,
):
    for ref, channel, row in ((wext_ref, 3, 0), (aext_ref, 1, 1)):
        ref[7:8] = xlo_ref[row : row + 1]
        ref[XL + 8 : XL + 9] = xhi_ref[row : row + 1]
        ref[8 : XL + 8] = fields_ref[channel]
    inner = lax.broadcasted_iota(jnp.int32, (8, N), 1) < N - 1
    for i in range(XL // 8):
        rows = pl.ds(8 * i, 8)
        weight = fields_ref[3, rows]
        accel_z = fields_ref[0, rows]
        accel_x = fields_ref[1, rows]
        accel_y = fields_ref[2, rows]
        face_zp = jnp.sqrt(weight * above_ref[1, rows])
        face_zm = jnp.sqrt(weight * below_ref[1, rows])
        face_xp = jnp.sqrt(weight * wext_ref[pl.ds(8 * i + 9, 8)])
        face_xm = jnp.sqrt(weight * wext_ref[pl.ds(8 * i + 7, 8)])
        face_yp = jnp.where(inner, jnp.sqrt(weight * pltpu.roll(weight, N - 1, 1)), 0.0)
        face_ym = pltpu.roll(face_yp, 1, 1)
        diagonal = SHIFT_RATE * weight + jnp.where(weight > 0.0, 0.0, 1.0)
        diagonal = diagonal + face_zp + face_zm + face_xp + face_xm + face_yp + face_ym
        flux = face_zm * (below_ref[0, rows] + accel_z) - face_zp * (accel_z + above_ref[0, rows])
        flux = flux + face_xm * (aext_ref[pl.ds(8 * i + 7, 8)] + accel_x)
        flux = flux - face_xp * (accel_x + aext_ref[pl.ds(8 * i + 9, 8)])
        flux_y = face_yp * (accel_y + pltpu.roll(accel_y, N - 1, 1))
        flux = flux + pltpu.roll(flux_y, 1, 1) - flux_y
        source_ref[rows] = 0.5 * flux
        for k, face in enumerate((face_zp, face_zm, face_xp, face_xm, face_yp, face_ym, diagonal)):
            faces_ref[k, rows] = face
    to_modes(source_ref, even_ref, odd_ref, small_ref, column_ref, lam_ref, fold_ref, modes_ref, ends_ref)


def update_kernel(
    slab_ref, modes_ref, all_ends_ref, fields_ref, cut_ref, near_far_ref, even_ref, odd_ref, small_t_ref,
    column_ref, lam_ref, update_ref, rim_ref, work_ref,
):
    slab = slab_ref[0]

    def jump(m):
        total = jnp.zeros((16, 128), F32)
        for j in range(SLABS):
            total = total + cut_ref[slab + m, j] * all_ends_ref[j]
        return total[:8] + total[8:]

    farther_low, low, high, farther_high = (jump(m) for m in range(4))
    near, far = near_far_ref[0], near_far_ref[1]
    before = all_ends_ref[jnp.maximum(slab - 1, 0), 8:16] - (near * low - far * farther_low)
    after = all_ends_ref[jnp.minimum(slab + 1, SLABS - 1), 0:8] - (far * farther_high - near * high)
    low_row, high_row = as_row(low), as_row(high)
    for i in range(XL // 8):
        rows = pl.ds(8 * i, 8)
        change = column_ref[rows, 2:3] * high_row - column_ref[rows, 1:2] * low_row
        work_ref[rows] = modes_ref[rows] - change / (column_ref[rows, 0:1] + lam_ref[...])
    work_ref[0:XL] = of_table(small_t_ref, work_ref[0:XL])
    work_ref[XL : XL + 8] = jnp.concatenate([as_row(before), as_row(after), jnp.zeros((6, N), F32)], axis=0)
    even = by_table(work_ref[:, :H], even_ref, False)
    odd = by_table(work_ref[:, H:], odd_ref, False)
    work_ref[:, :H] = even
    work_ref[:, H:] = odd
    for i in range(XL // 8 + 1):
        rows = pl.ds(8 * i, 8)
        even = work_ref[rows, :H]
        odd = work_ref[rows, H:]
        value = jnp.concatenate([even + odd, mirrored(even - odd)], axis=1)
        if i < XL // 8:
            update_ref[rows] = jnp.where(fields_ref[3, rows] > 0.0, value, 0.0)
        else:
            rim_ref[...] = value


def image_rows(i, value_ref, above_ref, below_ref, faces_ref, ext_ref):
    rows = pl.ds(8 * i, 8)
    value = value_ref[rows]
    image = faces_ref[6, rows] * value
    image = image - (faces_ref[0, rows] * above_ref[rows] + faces_ref[1, rows] * below_ref[rows])
    image = image - (faces_ref[2, rows] * ext_ref[pl.ds(8 * i + 9, 8)] + faces_ref[3, rows] * ext_ref[pl.ds(8 * i + 7, 8)])
    image = image - (faces_ref[4, rows] * pltpu.roll(value, N - 1, 1) + faces_ref[5, rows] * pltpu.roll(value, 1, 1))
    return value, image


def extend(value_ref, rim_ref, ext_ref):
    ext_ref[7:8] = rim_ref[0:1]
    ext_ref[XL + 8 : XL + 9] = rim_ref[1:2]
    ext_ref[8 : XL + 8] = value_ref[...]


def image_kernel(
    value_ref, rim_ref, above_ref, below_ref, faces_ref, even_ref, odd_ref, small_ref, column_ref, lam_ref,
    image_ref, modes_ref, ends_ref, ext_ref, fold_ref,
):
    extend(value_ref, rim_ref, ext_ref)
    for i in range(XL // 8):
        image_ref[pl.ds(8 * i, 8)] = image_rows(i, value_ref, above_ref, below_ref, faces_ref, ext_ref)[1]
    to_modes(image_ref, even_ref, odd_ref, small_ref, column_ref, lam_ref, fold_ref, modes_ref, ends_ref)


def sums_kernel(
    value_ref, rim_ref, above_ref, below_ref, faces_ref, source_ref, update_ref, first_image_ref,
    image_ref, sums_ref, ext_ref,
):
    extend(value_ref, rim_ref, ext_ref)
    totals = [jnp.zeros((8, N), F32) for _ in range(6)]
    for i in range(XL // 8):
        rows = pl.ds(8 * i, 8)
        v, t = image_rows(i, value_ref, above_ref, below_ref, faces_ref, ext_ref)
        image_ref[rows] = t
        r, u, q = source_ref[rows], update_ref[rows], first_image_ref[rows]
        for k, (a, b) in enumerate(((r, u), (u, q), (r, v), (q, v), (u, t), (v, t))):
            totals[k] = totals[k] + a * b
    lines = []
    for total in totals:
        line = jnp.sum(total, axis=0, keepdims=True)
        lines.append(sum(line[:, t * 128 : (t + 1) * 128] for t in range(8)))
    lines = jnp.concatenate(lines + [jnp.zeros((2, 128), F32)], axis=0)
    for j in range(OWNERS):
        sums_ref[j] = lines


def final_kernel(sums_ref, source_ref, u_ref, q_ref, v_ref, t_ref, solution_ref, residual_ref):
    total = sums_ref[0]
    for j in range(1, SLABS):
        total = total + sums_ref[j]
    total = jnp.sum(total, axis=1, keepdims=True)
    ru, uq, rv, qv, ut, vt = (total[k : k + 1] for k in range(6))
    step = ru / uq
    energy = ru - step * (rv + uq) + step * step * qv
    beta = energy / ru
    cross = uq - step * ut
    curve = cross - step * qv + step * step * vt
    curve = curve + beta * (cross + uq - step * qv) + beta * beta * uq
    second = energy / curve
    spread = lambda s: jnp.broadcast_to(s, (8, N))
    step, beta, second = spread(step), spread(beta), spread(second)
    for i in range(XL // 8):
        rows = pl.ds(8 * i, 8)
        u, q = u_ref[rows], q_ref[rows]
        direction = u - step * v_ref[rows] + beta * u
        along = q - step * t_ref[rows] + beta * q
        solution_ref[rows] = step * u + second * direction
        residual_ref[rows] = source_ref[rows] - step * q - second * along


def shape(*dims):
    return jax.ShapeDtypeStruct(dims, F32)


def call(kernel, out_shape, in_specs, out_specs, scratch=(), name=None):
    return pl.pallas_call(
        kernel, out_shape=out_shape, in_specs=in_specs, out_specs=out_specs, scratch_shapes=list(scratch), name=name
    )


PLANE = (XL, N)
EXT = pltpu.VMEM((XL + 16, N), F32)
FOLD = pltpu.VMEM(PLANE, F32)


def on_device(camera_accel, camera_weight, brick_slot, brick_solid):
    constant = {name: jnp.asarray(value) for name, value in tables().items()}
    dct = (constant["even"], constant["odd"])
    slab_tables = (constant["column"], constant["lam_y"])
    forward = dct + (constant["small"],) + slab_tables
    slab = lax.axis_index("gx")
    slabs, owners = lax.axis_size("gx"), lax.axis_size(YZ)
    up_z = [(i, i + 1) for i in range(owners - 1)]
    down_z = [(b, a) for a, b in up_z]
    up_x = [(i, i + 1) for i in range(slabs - 1)]
    down_x = [(b, a) for a, b in up_x]

    send = call(
        pack_kernel,
        shape(OWNERS, SEND_ROWS, 128),
        [SMEM, ANY, ANY],
        VMEM,
        [pltpu.SMEM((OWNERS,), jnp.int32), pltpu.SemaphoreType.DMA],
        name="pack",
    )(brick_slot[0], camera_accel[0].reshape(PLANE_BRICKS, 3 * BR, B), camera_weight[0])
    got = lax.all_to_all(send, YZ, split_axis=0, concat_axis=0, tiled=True)
    ids = got[:, PAIR_ROWS : PAIR_ROWS + PER_PAIR, 0].astype(jnp.int32).reshape(-1)
    fields, first, last = call(
        place_kernel,
        (shape(4, *PLANE), shape(2, N), shape(2, N)),
        [SMEM, SMEM, ANY],
        (VMEM, VMEM, VMEM),
        [pltpu.SemaphoreType.DMA],
        name="place",
    )(ids, brick_solid[0], got)
    beside = fields[jnp.array([0, 3])]
    above = lax.ppermute(beside, YZ, down_z)
    below = lax.ppermute(beside, YZ, up_z)
    xlo = lax.ppermute(last, "gx", up_x)
    xhi = lax.ppermute(first, "gx", down_x)
    faces, source, modes, ends = call(
        setup_kernel,
        (shape(7, *PLANE), shape(*PLANE), shape(*PLANE), shape(SLABS, 16, 128)),
        [VMEM] * 10,
        (VMEM,) * 4,
        [EXT, EXT, FOLD],
        name="setup",
    )(fields, above, below, xlo, xhi, *forward)

    def updated(modes, ends):
        all_ends = lax.all_to_all(ends, "gx", split_axis=0, concat_axis=0, tiled=True)
        return call(
            update_kernel,
            (shape(*PLANE), shape(8, N)),
            [SMEM] + [VMEM] * 10,
            (VMEM, VMEM),
            [pltpu.VMEM((XL + 8, N), F32)],
            name="update",
        )(
            slab.reshape(1), modes, all_ends, fields, constant["cut"], constant["ends"],
            *dct, constant["small_t"], *slab_tables,
        )

    def neighbours(value):
        return lax.ppermute(value, YZ, down_z), lax.ppermute(value, YZ, up_z)

    u, rim = updated(modes, ends)
    q, modes, ends = call(
        image_kernel,
        (shape(*PLANE), shape(*PLANE), shape(SLABS, 16, 128)),
        [VMEM] * 10,
        (VMEM,) * 3,
        [EXT, FOLD],
        name="image",
    )(u, rim, *neighbours(u), faces, *forward)
    v, rim = updated(modes, ends)
    t, sums = call(
        sums_kernel,
        (shape(*PLANE), shape(OWNERS, 8, 128)),
        [VMEM] * 8,
        (VMEM, VMEM),
        [EXT],
        name="sums",
    )(v, rim, *neighbours(v), faces, source, u, q)
    sums = lax.all_to_all(sums, YZ, split_axis=0, concat_axis=0, tiled=True)
    sums = jnp.broadcast_to(jnp.sum(sums, axis=0)[None], (SLABS, 8, 128))
    sums = lax.all_to_all(sums, "gx", split_axis=0, concat_axis=0, tiled=True)
    result, residual = call(
        final_kernel, (shape(*PLANE), shape(*PLANE)), [VMEM] * 6, (VMEM, VMEM), name="final"
    )(sums, source, u, q, v, t)
    return result[None], residual[None]


def solution(mesh):
    finer = Mesh(mesh.devices.reshape(mesh.shape["gx"], 4, 4, 2), ("gx", "yz_0", "yz_1", "yz_2"))
    in_specs = (P("gx", YZ, None, None, None), P("gx", YZ, None, None), P("gx", YZ), P("gx", YZ))
    out_specs = (P(YZ, "gx", None), P(YZ, "gx", None))
    return jax.shard_map(
        on_device, mesh=finer, in_specs=in_specs, out_specs=out_specs, check_vma=False
    )
```

time: 496 us -> 200 us (0.40); the launches traced: 489 us -> 199 us
  matrix products: 156 us -> 0 us
  blocking collectives: 116 us -> 39.6 us
  Pallas kernels: 0 us -> 38.2 us
  starting transfers between devices: 69.7 us -> 40.4 us
  local copies, waits for them, and re-layouts: 34.4 us -> 6.46 us
  other arithmetic: 24.3 us -> 0.66 us
  waiting for transfers between devices: 82.6 us -> 72.7 us
  between operations: 7.14 us -> 0.78 us
    dot_general x8 -> x0, matrix products: 156 us -> none  [the longest x2 40.8 us: precondition(): jnp.einsum('kx,zxy->zky', table_x, pencil, precision=highest) / denom[None]]
    psum x8 -> x0, blocking collectives: 75 us -> none  [one_axis_at_a_time(): return functools.reduce(lax.psum, axes, shard)]
    pallas_call x0 -> x8, Pallas kernels: none -> 38.2 us  [the longest x2 9.16 us: updated(): call(update_kernel, (shape(*PLANE), shape(8, N)), [SMEM] + [VMEM] * 10, (...]
    ppermute x12 -> x8, starting transfers between devices: 40.5 us -> 23.6 us  [the longest x4 13.2 us: neighbours(): return (lax.ppermute(value, YZ, down_z), lax.ppermute(value, YZ, up_z))]
    all_to_all x5 -> x2, waiting for transfers between devices: 63.9 us -> 48.3 us  [the longest x1 41.1 us: on_device(): got = lax.all_to_all(send, YZ, split_axis=0, concat_axis=0, tiled=True)]
    all_to_all x5 -> x2, starting transfers between devices: 29.2 us -> 16.8 us  [the longest x1 8.59 us: on_device(): got = lax.all_to_all(send, YZ, split_axis=0, concat_axis=0, tiled=True)]
    slice x21 -> x0, local copies, waits for them, and re-layouts: 10.1 us -> none  [the longest x3 4.29 us: on_device(): fields[1]]
    gather x6 -> x1, local copies, waits for them, and re-layouts: 9.61 us -> 2.2 us  [on_device(): beside = fields[jnp.array([0, 3])]]
  transfers between devices with their start and end apart: 17 -> 10, of which waited for: 12 -> 9; matrix products, arithmetic and copies ran while one was open for 4% -> 0% of each run, Pallas kernels for 0% -> 0%
where the time goes in v1:
time: 200 us; the launch traced here: 199 us
  waiting for transfers between devices  72.7 us (36%)
  starting transfers between devices  40.4 us (20%)
  blocking collectives  39.6 us (20%)
  Pallas kernels  38.2 us (19%)
  local copies, waits for them, and re-layouts  6.46 us (3%)
    all_to_all x1, waiting for transfers between devices, on_device(): got = lax.all_to_all(send, YZ, split_axis=0, concat_axis=0, tiled=True)  41.1 us
    all_to_all x1, blocking collectives, on_device(): sums = lax.all_to_all(sums, YZ, split_axis=0, concat_axis=0, tiled=True)  18.6 us
    ppermute x4, waiting for transfers between devices, neighbours(): return (lax.ppermute(value, YZ, down_z), lax.ppermute(value, YZ, up_z))  17.6 us
    ppermute x4, starting transfers between devices, neighbours(): return (lax.ppermute(value, YZ, down_z), lax.ppermute(value, YZ, up_z))  13.2 us
    all_to_all x1, blocking collectives, updated(): lax.all_to_all(ends, 'gx', split_axis=0, concat_axis=0, tiled=True)  11.2 us
    all_to_all x1, blocking collectives, on_device(): sums = lax.all_to_all(sums, 'gx', split_axis=0, concat_axis=0, tiled=True)  9.92 us
    pallas_call x2, Pallas kernels, updated(): call(update_kernel, (shape(*PLANE), shape(8, N)), [SMEM] + [VMEM] * 10, (...  9.16 us
    all_to_all x1, starting transfers between devices, on_device(): got = lax.all_to_all(send, YZ, split_axis=0, concat_axis=0, tiled=True)  8.59 us
  transfers between devices with their start and end apart: 10, of which 9 were waited for; matrix products, arithmetic and copies ran while one was open for 0% of the time, Pallas kernels for 0%

profile of v1, /device:TPU:1, one launch (start us, length us, event | category | flops | bytes accessed | tf_op | source)
XLA Modules:
  0.0 198.9 jit_solution(6082404888839829311)
XLA Ops:
  0.6 4.4 %pack.1 = f32[32,200,128]{2,1,0:T(8,128)} custom-call(s32[64]{0:T(128)} %bitcast.9, f32[64,48,128]{2,1,0:T(8,128)} %bitcast.7, f32[64,16,128]{2,1,0:T(8,128)} %bitcast.8), custom_call_target="tpu_custom_call" | custom-call | tf_op jit(solution)/shard_map/pack/pallas_call | solution.py:385
  5.0 8.6 %all-to-all-start = ((f32[32,200,128]{2,1,0:T(8,128)}), f32[32,200,128]{2,1,0:T(8,128)S(1)}, u32[]{:S(2)}, u32[]{:S(2)}) async-start(f32[32,200,128]{2,1,0:T(8,128)} %pack.1), calls=%async_computation | async-start | bytes 6553600 | tf_op jit(solution)/shard_map/all_to_all | solution.py:393
  13.6 41.1 %all-to-all-done.got_ref = f32[32,200,128]{2,1,0:T(8,128)S(1)} async-done(((f32[32,200,128]{2,1,0:T(8,128)}), f32[32,200,128]{2,1,0:T(8,128)S(1)}, u32[]{:S(2)}, u32[]{:S(2)}) %all-to-all-start) | async-done | bytes 3276832 | tf_op jit(solution)/shard_map/all_to_all | solution.py:393
  54.8 0.0 copy-start
  54.8 0.6 fusion
  55.4 1.0 convert_element_type.8.ids_ref
  56.3 0.1 copy-done
  56.4 5.3 %place.1 = (f32[4,128,1024]{2,1,0:T(8,128)}, f32[2,1024]{1,0:T(2,128)}, f32[2,1024]{1,0:T(2,128)}) custom-call(s32[96]{0:T(128)} %convert_element_type.8.ids_ref, s32[64]{0:T(128)} %bitcast.10, f32[32,200,128]{2,1,0:T(8,128)} %copy-done), custom_call_target="tpu_custom_call" | custom-call | tf_op jit(solution)/shard_map/place/pallas_call | solution.py:395
  61.7 2.2 %gather_fusion = f32[2,128,1024]{2,1,0:T(8,128)S(1)} fusion(f32[4,128,1024]{2,1,0:T(8,128)} %get-tuple-element.20.fields_ref, s32[1024]{0:T(1024)S(1)} %pad_clamp_fusion), kind=kCustom, calls=%fused_computation | custom fusion | bytes 2097160 | tf_op jit(solution)/shard_map/gather | solution.py:403
  63.9 2.5 %collective-permute-start = (f32[2,128,1024]{2,1,0:T(8,128)S(1)}, f32[2,128,1024]{2,1,0:T(8,128)S(1)}, u32[]{:S(2)}, u32[]{:S(2)}) collective-permute-start(f32[2,128,1024]{2,1,0:T(8,128)S(1)} %gather_fusion), channel_id=1, source_target_pairs={{1,0},{2,1},{3,2},{4,3},{5,4},{6,5},{7,6},{8,7},{9,8},{10,9},{11,1... | collective-permute-start | bytes 3145736 | tf_op jit(solution)/shard_map/ppermute | solution.py:404
  66.4 3.1 %collective-permute-start.1 = (f32[2,128,1024]{2,1,0:T(8,128)S(1)}, f32[2,128,1024]{2,1,0:T(8,128)S(1)}, u32[]{:S(2)}, u32[]{:S(2)}) collective-permute-start(f32[2,128,1024]{2,1,0:T(8,128)S(1)} %gather_fusion), channel_id=1, source_target_pairs={{0,1},{1,2},{2,3},{3,4},{4,5},{5,6},{6,7},{7,8},{8,9},{9,10},{10,1... | collective-permute-start | bytes 3145736 | tf_op jit(solution)/shard_map/ppermute | solution.py:405
  69.5 3.6 %collective-permute-start.2 = (f32[2,1024]{1,0:T(2,128)}, f32[2,1024]{1,0:T(2,128)S(1)}, u32[]{:S(2)}, u32[]{:S(2)}) collective-permute-start(f32[2,1024]{1,0:T(2,128)} %get-tuple-element.21), channel_id=1, source_target_pairs={{0,32},{32,64},{64,96},{96,128},{128,160},{160,192},{192,224},{1,3... | collective-permute-start | bytes 24584 | tf_op jit(solution)/shard_map/ppermute | solution.py:406
  73.1 1.3 collective-permute-start.3
  74.4 0.0 collective-permute-done.2.xlo_ref
  74.4 0.0 copy-start.8
  74.4 3.8 %collective-permute-done.3.xhi_ref = f32[2,1024]{1,0:T(2,128)S(1)} collective-permute-done((f32[2,1024]{1,0:T(2,128)}, f32[2,1024]{1,0:T(2,128)S(1)}, u32[]{:S(2)}, u32[]{:S(2)}) %collective-permute-start.3) | collective-permute-done | bytes 8224 | tf_op jit(solution)/shard_map/ppermute | solution.py:407
  78.2 0.0 copy-start.9
  78.2 1.9 collective-permute-done.above_ref
  80.0 0.0 copy-start.1
  80.0 1.2 collective-permute-done.1.below_ref
  81.2 0.0 copy-done.8
  81.2 0.0 copy-done.9
  81.2 0.0 copy-done.1
  81.2 0.0 copy-start.2
  81.2 1.0 copy-done.2
  82.2 6.5 %setup.1 = (f32[7,128,1024]{2,1,0:T(8,128)}, f32[128,1024]{1,0:T(8,128)}, f32[128,1024]{1,0:T(8,128)}, f32[8,16,128]{2,1,0:T(8,128)}) custom-call(f32[4,128,1024]{2,1,0:T(8,128)} %get-tuple-element.20.fields_ref, f32[2,128,1024]{2,1,0:T(8,128)} %copy-done.1, f32[2,128,1024]{2,1,0:T(8,128)} %copy-done.2, f32[2,1024]{1,0:T(2,128)} %copy-done.8, ...), custom_call_target="tpu_custom_call" | custom-call | tf_op jit(solution)/shard_map/setup/pallas_call | solution.py:408
  88.7 8.2 %all-to-all-start.1 = ((f32[8,16,128]{2,1,0:T(8,128)}), f32[8,16,128]{2,1,0:T(8,128)S(1)}, u32[]{:S(2)}, u32[]{:S(2)}) async-start(f32[8,16,128]{2,1,0:T(8,128)} %get-tuple-element.24), calls=%async_computation.1 | async-start | bytes 131072 | tf_op jit(solution)/shard_map/all_to_all | solution.py:418
  96.9 7.2 %all-to-all-done.1.all_ends_ref = f32[8,16,128]{2,1,0:T(8,128)S(1)} async-done(((f32[8,16,128]{2,1,0:T(8,128)}), f32[8,16,128]{2,1,0:T(8,128)S(1)}, u32[]{:S(2)}, u32[]{:S(2)}) %all-to-all-start.1) | async-done | bytes 65568 | tf_op jit(solution)/shard_map/all_to_all | solution.py:418
  104.2 0.0 copy-start.7
  104.2 0.6 copy-done.7
  104.8 4.6 %update.2 = (f32[128,1024]{1,0:T(8,128)}, f32[8,1024]{1,0:T(8,128)}) custom-call(s32[1]{0:T(128)} %bitcast.slab_ref, f32[128,1024]{1,0:T(8,128)} %get-tuple-element.23.modes_ref, f32[8,16,128]{2,1,0:T(8,128)} %copy-done.7, f32[4,128,1024]{2,1,0:T(8,128)} %get-tuple-element.20.fields_ref, f32[11,8,16,128]{3,2,1,0:T(8,128)} %constant.37.clone.cut_ref, ...), custom_call_target="tpu_custom_call" | custom-call | tf_op jit(solution)/shard_map/update/pallas_call | solution.py:419
  109.4 5.8 %collective-permute-start.5 = (f32[128,1024]{1,0:T(8,128)}, f32[128,1024]{1,0:T(8,128)S(1)}, u32[]{:S(2)}, u32[]{:S(2)}) collective-permute-start(f32[128,1024]{1,0:T(8,128)} %get-tuple-element.25.value_ref.update_ref.u_ref), channel_id=1, source_target_pairs={{0,1},{1,2},{2,3},{3,4},{4,5},{5,6},{6,7},{7,8},{8,9},{9,10},{10,1... | collective-permute-start | bytes 1572872 | tf_op jit(solution)/shard_map/ppermute | solution.py:432
  115.2 1.9 collective-permute-start.4
  117.1 4.5 %collective-permute-done.5.below_ref = f32[128,1024]{1,0:T(8,128)S(1)} collective-permute-done((f32[128,1024]{1,0:T(8,128)}, f32[128,1024]{1,0:T(8,128)S(1)}, u32[]{:S(2)}, u32[]{:S(2)}) %collective-permute-start.5) | collective-permute-done | bytes 524320 | tf_op jit(solution)/shard_map/ppermute | solution.py:432
  121.6 0.0 copy-start.3
  121.6 4.3 %collective-permute-done.4.above_ref = f32[128,1024]{1,0:T(8,128)S(1)} collective-permute-done((f32[128,1024]{1,0:T(8,128)}, f32[128,1024]{1,0:T(8,128)S(1)}, u32[]{:S(2)}, u32[]{:S(2)}) %collective-permute-start.4) | collective-permute-done | bytes 524320 | tf_op jit(solution)/shard_map/ppermute | solution.py:432
  125.9 0.0 copy-start.4
  125.9 0.0 copy-done.3
  125.9 0.8 copy-done.4
  126.7 5.4 %image.1 = (f32[128,1024]{1,0:T(8,128)}, f32[128,1024]{1,0:T(8,128)}, f32[8,16,128]{2,1,0:T(8,128)}) custom-call(f32[128,1024]{1,0:T(8,128)} %get-tuple-element.25.value_ref.update_ref.u_ref, f32[8,1024]{1,0:T(8,128)} %get-tuple-element.26.rim_ref, f32[128,1024]{1,0:T(8,128)} %copy-done.4, f32[128,1024]{1,0:T(8,128)} %copy-done.3, ...), custom_call_target="tpu_custom_call" | custom-call | tf_op jit(solution)/shard_map/image/pallas_call | solution.py:435
  132.1 11.2 %all_to_all.25.all_ends_ref = f32[8,16,128]{2,1,0:T(8,128)} all-to-all(f32[8,16,128]{2,1,0:T(8,128)} %get-tuple-element.29), channel_id=1, replica_groups=mesh['gx'=8,'yz_0'=4,'yz_1'=4,'yz_2'=2] {'gx'}, dimensions={0} | all-to-all | bytes 131072 | tf_op jit(solution)/shard_map/all_to_all | solution.py:418
  143.3 4.6 %update.3 = (f32[128,1024]{1,0:T(8,128)}, f32[8,1024]{1,0:T(8,128)}) custom-call(s32[1]{0:T(128)} %bitcast.slab_ref, f32[128,1024]{1,0:T(8,128)} %get-tuple-element.28.modes_ref, f32[8,16,128]{2,1,0:T(8,128)} %all_to_all.25.all_ends_ref, f32[4,128,1024]{2,1,0:T(8,128)} %get-tuple-element.20.fields_ref, f32[11,8,16,128]{3,2,1,0:T(8,128)} %constant.37.clone.cut_ref, ...), custom_call_target="tpu_custom_call" | custom-call | tf_op jit(solution)/shard_map/update/pallas_call | solution.py:419
  147.8 3.5 %collective-permute-start.7 = (f32[128,1024]{1,0:T(8,128)}, f32[128,1024]{1,0:T(8,128)S(1)}, u32[]{:S(2)}, u32[]{:S(2)}) collective-permute-start(f32[128,1024]{1,0:T(8,128)} %get-tuple-element.30.value_ref.v_ref), channel_id=1, source_target_pairs={{0,1},{1,2},{2,3},{3,4},{4,5},{5,6},{6,7},{7,8},{8,9},{9,10},{10,1... | collective-permute-start | bytes 1572872 | tf_op jit(solution)/shard_map/ppermute | solution.py:432
  151.4 1.9 collective-permute-start.6
  153.3 4.5 %collective-permute-done.7.below_ref = f32[128,1024]{1,0:T(8,128)S(1)} collective-permute-done((f32[128,1024]{1,0:T(8,128)}, f32[128,1024]{1,0:T(8,128)S(1)}, u32[]{:S(2)}, u32[]{:S(2)}) %collective-permute-start.7) | collective-permute-done | bytes 524320 | tf_op jit(solution)/shard_map/ppermute | solution.py:432
  157.8 0.0 copy-start.5
  157.8 4.3 %collective-permute-done.6.above_ref = f32[128,1024]{1,0:T(8,128)S(1)} collective-permute-done((f32[128,1024]{1,0:T(8,128)}, f32[128,1024]{1,0:T(8,128)S(1)}, u32[]{:S(2)}, u32[]{:S(2)}) %collective-permute-start.6) | collective-permute-done | bytes 524320 | tf_op jit(solution)/shard_map/ppermute | solution.py:432
  162.1 0.0 copy-start.6
  162.1 0.0 copy-done.5
  162.1 0.8 copy-done.6
  162.9 4.4 %sums.1 = (f32[128,1024]{1,0:T(8,128)}, f32[32,8,128]{2,1,0:T(8,128)}) custom-call(f32[128,1024]{1,0:T(8,128)} %get-tuple-element.30.value_ref.v_ref, f32[8,1024]{1,0:T(8,128)} %get-tuple-element.31.rim_ref, f32[128,1024]{1,0:T(8,128)} %copy-done.6, f32[128,1024]{1,0:T(8,128)} %copy-done.5, f32[7,128,1024]{2,1,0:T(8,128)} %get-tuple-element.27.faces_ref, ...), custom_call_target="tpu_custom_call" | custom-call | tf_op jit(solution)/shard_map/sums/pallas_call | solution.py:444
  167.3 18.6 %all_to_all.26 = f32[32,8,128]{2,1,0:T(8,128)S(1)} all-to-all(f32[32,8,128]{2,1,0:T(8,128)} %get-tuple-element.34), channel_id=1, replica_groups=mesh['gx'=8,'yz_0'=4,'yz_1'=4,'yz_2'=2] {'yz_0','yz_1','yz_2'}, dimensions={0} | all-to-all | bytes 262144 | tf_op jit(solution)/shard_map/all_to_all | solution.py:452
  185.9 9.9 %all_to_all.27.sums_ref = f32[8,8,128]{2,1,0:T(8,128)} all-to-all(f32[8,8,128]{2,1,0:T(8,128)S(1)} %broadcast_in_dim.16), channel_id=1, replica_groups=mesh['gx'=8,'yz_0'=4,'yz_1'=4,'yz_2'=2] {'gx'}, dimensions={0} | all-to-all | bytes 65536 | tf_op jit(solution)/shard_map/all_to_all | solution.py:454
  195.8 3.0 %final.1 = (f32[128,1024]{1,0:T(8,128)}, f32[128,1024]{1,0:T(8,128)}) custom-call(f32[8,8,128]{2,1,0:T(8,128)} %all_to_all.27.sums_ref, f32[128,1024]{1,0:T(8,128)} %get-tuple-element.32.source_ref, f32[128,1024]{1,0:T(8,128)} %get-tuple-element.25.value_ref.update_ref.u_ref, f32[128,1024]{1,0:T(8,128)} %get-tuple-element.33.first_image_ref.q_ref, ...), custom_call_target="tpu_custom_call" | custom-call | tf_op jit(solution)/shard_map/final/pallas_call | solution.py:455
  (4 shorter events, 0.1 us)
Async XLA Ops:
  5.0 49.7 %all-to-all-start = ((f32[32,200,128]{2,1,0:T(8,128)}), f32[32,200,128]{2,1,0:T(8,128)S(1)}, u32[]{:S(2)}, u32[]{:S(2)}) async-start(f32[32,200,128]{2,1,0:T(8,128)} %pack.1), calls=%async_computation | async-start | bytes 6553600 | tf_op jit(solution)/shard_map/all_to_all | solution.py:393
  54.8 1.7 copy-start
  63.9 16.1 %collective-permute-start = (f32[2,128,1024]{2,1,0:T(8,128)S(1)}, f32[2,128,1024]{2,1,0:T(8,128)S(1)}, u32[]{:S(2)}, u32[]{:S(2)}) collective-permute-start(f32[2,128,1024]{2,1,0:T(8,128)S(1)} %gather_fusion), channel_id=1, source_target_pairs={{1,0},{2,1},{3,2},{4,3},{5,4},{6,5},{7,6},{8,7},{9,8},{10,9},{11,1... | collective-permute-start | bytes 3145736 | tf_op jit(solution)/shard_map/ppermute | solution.py:404
  66.4 14.8 %collective-permute-start.1 = (f32[2,128,1024]{2,1,0:T(8,128)S(1)}, f32[2,128,1024]{2,1,0:T(8,128)S(1)}, u32[]{:S(2)}, u32[]{:S(2)}) collective-permute-start(f32[2,128,1024]{2,1,0:T(8,128)S(1)} %gather_fusion), channel_id=1, source_target_pairs={{0,1},{1,2},{2,3},{3,4},{4,5},{5,6},{6,7},{7,8},{8,9},{9,10},{10,1... | collective-permute-start | bytes 3145736 | tf_op jit(solution)/shard_map/ppermute | solution.py:405
  69.5 4.9 %collective-permute-start.2 = (f32[2,1024]{1,0:T(2,128)}, f32[2,1024]{1,0:T(2,128)S(1)}, u32[]{:S(2)}, u32[]{:S(2)}) collective-permute-start(f32[2,1024]{1,0:T(2,128)} %get-tuple-element.21), channel_id=1, source_target_pairs={{0,32},{32,64},{64,96},{96,128},{128,160},{160,192},{192,224},{1,3... | collective-permute-start | bytes 24584 | tf_op jit(solution)/shard_map/ppermute | solution.py:406
  73.1 5.1 %collective-permute-start.3 = (f32[2,1024]{1,0:T(2,128)}, f32[2,1024]{1,0:T(2,128)S(1)}, u32[]{:S(2)}, u32[]{:S(2)}) collective-permute-start(f32[2,1024]{1,0:T(2,128)} %get-tuple-element.22), channel_id=1, source_target_pairs={{32,0},{64,32},{96,64},{128,96},{160,128},{192,160},{224,192},{33,... | collective-permute-start | bytes 24584 | tf_op jit(solution)/shard_map/ppermute | solution.py:407
  74.4 6.8 %copy-start.8 = (f32[2,1024]{1,0:T(2,128)}, f32[2,1024]{1,0:T(2,128)S(1)}, u32[]{:S(2)}) copy-start(f32[2,1024]{1,0:T(2,128)S(1)} %collective-permute-done.2.xlo_ref) | copy-start | bytes 24580
  78.2 3.1 %copy-start.9 = (f32[2,1024]{1,0:T(2,128)}, f32[2,1024]{1,0:T(2,128)S(1)}, u32[]{:S(2)}) copy-start(f32[2,1024]{1,0:T(2,128)S(1)} %collective-permute-done.3.xhi_ref) | copy-start | bytes 24580
  80.0 1.2 copy-start.1
  81.2 1.0 copy-start.2
  88.7 15.4 %all-to-all-start.1 = ((f32[8,16,128]{2,1,0:T(8,128)}), f32[8,16,128]{2,1,0:T(8,128)S(1)}, u32[]{:S(2)}, u32[]{:S(2)}) async-start(f32[8,16,128]{2,1,0:T(8,128)} %get-tuple-element.24), calls=%async_computation.1 | async-start | bytes 131072 | tf_op jit(solution)/shard_map/all_to_all | solution.py:418
  104.2 0.6 copy-start.7
  109.4 12.2 %collective-permute-start.5 = (f32[128,1024]{1,0:T(8,128)}, f32[128,1024]{1,0:T(8,128)S(1)}, u32[]{:S(2)}, u32[]{:S(2)}) collective-permute-start(f32[128,1024]{1,0:T(8,128)} %get-tuple-element.25.value_ref.update_ref.u_ref), channel_id=1, source_target_pairs={{0,1},{1,2},{2,3},{3,4},{4,5},{5,6},{6,7},{7,8},{8,9},{9,10},{10,1... | collective-permute-start | bytes 1572872 | tf_op jit(solution)/shard_map/ppermute | solution.py:432
  115.2 10.7 %collective-permute-start.4 = (f32[128,1024]{1,0:T(8,128)}, f32[128,1024]{1,0:T(8,128)S(1)}, u32[]{:S(2)}, u32[]{:S(2)}) collective-permute-start(f32[128,1024]{1,0:T(8,128)} %get-tuple-element.25.value_ref.update_ref.u_ref), channel_id=1, source_target_pairs={{1,0},{2,1},{3,2},{4,3},{5,4},{6,5},{7,6},{8,7},{9,8},{10,9},{11,1... | collective-permute-start | bytes 1572872 | tf_op jit(solution)/shard_map/ppermute | solution.py:432
  121.6 4.3 %copy-start.3 = (f32[128,1024]{1,0:T(8,128)}, f32[128,1024]{1,0:T(8,128)S(1)}, u32[]{:S(2)}) copy-start(f32[128,1024]{1,0:T(8,128)S(1)} %collective-permute-done.5.below_ref) | copy-start | bytes 1572868
  125.9 0.8 copy-start.4
  147.8 9.9 %collective-permute-start.7 = (f32[128,1024]{1,0:T(8,128)}, f32[128,1024]{1,0:T(8,128)S(1)}, u32[]{:S(2)}, u32[]{:S(2)}) collective-permute-start(f32[128,1024]{1,0:T(8,128)} %get-tuple-element.30.value_ref.v_ref), channel_id=1, source_target_pairs={{0,1},{1,2},{2,3},{3,4},{4,5},{5,6},{6,7},{7,8},{8,9},{9,10},{10,1... | collective-permute-start | bytes 1572872 | tf_op jit(solution)/shard_map/ppermute | solution.py:432
  151.4 10.7 %collective-permute-start.6 = (f32[128,1024]{1,0:T(8,128)}, f32[128,1024]{1,0:T(8,128)S(1)}, u32[]{:S(2)}, u32[]{:S(2)}) collective-permute-start(f32[128,1024]{1,0:T(8,128)} %get-tuple-element.30.value_ref.v_ref), channel_id=1, source_target_pairs={{1,0},{2,1},{3,2},{4,3},{5,4},{6,5},{7,6},{8,7},{9,8},{10,9},{11,1... | collective-permute-start | bytes 1572872 | tf_op jit(solution)/shard_map/ppermute | solution.py:432
  157.8 4.3 %copy-start.5 = (f32[128,1024]{1,0:T(8,128)}, f32[128,1024]{1,0:T(8,128)S(1)}, u32[]{:S(2)}) copy-start(f32[128,1024]{1,0:T(8,128)S(1)} %collective-permute-done.7.below_ref) | copy-start | bytes 1572868
  162.1 0.8 copy-start.6

commit v2 on v1

--- a/solution.py
+++ b/solution.py
@@ -29,7 +29,7 @@
 BF16 = jnp.bfloat16
 VMEM = pl.BlockSpec(memory_space=pltpu.VMEM)
 SMEM = pl.BlockSpec(memory_space=pltpu.SMEM)
-ANY = pl.BlockSpec(memory_space=pl.ANY)
+HBM = pl.BlockSpec(memory_space=pltpu.HBM)
 
 
 def cosine_rows(length):
@@ -156,19 +156,22 @@
         ends_ref[j, 8:16] = last
 
 
-def pack_kernel(slot_ref, accel_ref, weight_ref, out_ref, count_ref, sem):
+def pack_kernel(place_ref, slot_ref, accel_ref, weight_ref, out_ref, count_ref, sem):
+    del place_ref
     for o in range(OWNERS):
         count_ref[o] = 0
     out_ref[:, PAIR_ROWS:] = jnp.full((OWNERS, 8, 128), -1.0, F32)
+    lane = lax.broadcasted_iota(jnp.int32, (1, 128), 1)
 
     def one(s, carry):
         brick = slot_ref[s]
         owner = brick // PLANE_BRICKS
         place = count_ref[owner]
         count_ref[owner] = place + 1
-        number = jnp.full((1, 128), brick - owner * PLANE_BRICKS, jnp.int32)
-        out_ref[owner, pl.ds(PAIR_ROWS + place, 1), :] = number.astype(F32)
-        at = pl.multiple_of(place * BRICK_ROWS, 16)
+        number = (brick - owner * PLANE_BRICKS).astype(F32)
+        line = out_ref[owner, PAIR_ROWS : PAIR_ROWS + 1, :]
+        out_ref[owner, PAIR_ROWS : PAIR_ROWS + 1, :] = jnp.where(lane == place, number, line)
+        at = pl.multiple_of(place * BRICK_ROWS, BRICK_ROWS)
         pltpu.make_async_copy(accel_ref.at[s], out_ref.at[owner, pl.ds(at, 3 * BR)], sem).start()
         pltpu.make_async_copy(weight_ref.at[s], out_ref.at[owner, pl.ds(at + 3 * BR, BR)], sem).start()
         return carry
@@ -178,78 +181,72 @@
     pltpu.make_async_copy(sent, sent, sem).wait()
 
 
-def place_kernel(ids_ref, solid_ref, got_ref, fields_ref, first_ref, last_ref, sem):
-    def one(s, carry):
-        brick = ids_ref[s]
-
-        @pl.when(brick >= 0)
-        def _():
-            x_at = pl.multiple_of((brick // 8) * BR, BR)
-            y_at = pl.multiple_of((brick % 8) * B, B)
-            source = s // PER_PAIR
-            row = (s % PER_PAIR) * BRICK_ROWS
-            for channel in range(4):
-                at = pl.multiple_of(row + channel * BR, BR)
-                pltpu.make_async_copy(
-                    got_ref.at[source, pl.ds(at, BR)],
-                    fields_ref.at[channel, pl.ds(x_at, BR), pl.ds(y_at, B)],
-                    sem,
-                ).start()
+def place_kernel(solid_ref, got_ref, z_ref, xy_ref, first_ref, last_ref, ids_ref, sem):
+    ids_copy = pltpu.make_async_copy(got_ref.at[:, pl.ds(PAIR_ROWS, 1)], ids_ref, sem)
+    ids_copy.start()
+    ids_copy.wait()
+
+    def one(source, carry):
+        for place in range(PER_PAIR):
+            brick = ids_ref[source, 0, place].astype(jnp.int32)
+
+            @pl.when(brick >= 0)
+            def _():
+                fluid = (1 - solid_ref[brick]).astype(F32)
+                x_at = pl.multiple_of((brick // 8) * BR, BR)
+                y_at = pl.multiple_of((brick % 8) * B, B)
+                for channel, (ref, at) in enumerate(((z_ref, 0), (xy_ref, 0), (xy_ref, 1), (z_ref, 1))):
+                    row = place * BRICK_ROWS + channel * BR
+                    ref[at, pl.ds(x_at, BR), pl.ds(y_at, B)] = got_ref[source, row : row + BR] * fluid
 
         return carry
 
-    lax.fori_loop(0, OWNERS * PER_PAIR, one, 0)
-    pltpu.make_async_copy(fields_ref, fields_ref, sem).wait()
-    for i in range(PLANE_BRICKS):
-        fluid = (1 - solid_ref[i]).astype(F32)
-        rows = pl.ds((i // 8) * BR, BR)
-        cols = pl.ds((i % 8) * B, B)
-        for channel in range(4):
-            fields_ref[channel, rows, cols] = fields_ref[channel, rows, cols] * fluid
+    lax.fori_loop(0, OWNERS, one, 0)
     for ref, row in ((first_ref, 0), (last_ref, XL - 1)):
-        ref[0:1] = fields_ref[3, row : row + 1]
-        ref[1:2] = fields_ref[1, row : row + 1]
+        ref[0:1] = z_ref[1, row : row + 1]
+        ref[1:2] = xy_ref[0, row : row + 1]
 
 
 def setup_kernel(
-    fields_ref, above_ref, below_ref, xlo_ref, xhi_ref, even_ref, odd_ref, small_ref, column_ref, lam_ref,
-    faces_ref, source_ref, modes_ref, ends_ref, wext_ref, aext_ref, fold_ref,
+    place_ref, z_ref, xy_ref, partner_ref, outer_ref, xlo_ref, xhi_ref, even_ref, odd_ref, small_ref, column_ref,
+    lam_ref, faces_ref, source_ref, modes_ref, ends_ref, wext_ref, aext_ref, fold_ref,
 ):
-    for ref, channel, row in ((wext_ref, 3, 0), (aext_ref, 1, 1)):
+    for ref, field, row in ((wext_ref, z_ref[1], 0), (aext_ref, xy_ref[0], 1)):
         ref[7:8] = xlo_ref[row : row + 1]
         ref[XL + 8 : XL + 9] = xhi_ref[row : row + 1]
-        ref[8 : XL + 8] = fields_ref[channel]
+        ref[8 : XL + 8] = field
     inner = lax.broadcasted_iota(jnp.int32, (8, N), 1) < N - 1
-    for i in range(XL // 8):
-        rows = pl.ds(8 * i, 8)
-        weight = fields_ref[3, rows]
-        accel_z = fields_ref[0, rows]
-        accel_x = fields_ref[1, rows]
-        accel_y = fields_ref[2, rows]
-        face_zp = jnp.sqrt(weight * above_ref[1, rows])
-        face_zm = jnp.sqrt(weight * below_ref[1, rows])
+    sign = (2 * place_ref[1] - 1).astype(F32)
+    for i in range(XL // 8):
+        rows = pl.ds(8 * i, 8)
+        accel_z = z_ref[0, rows]
+        weight = z_ref[1, rows]
+        accel_x = xy_ref[0, rows]
+        accel_y = xy_ref[1, rows]
+        face_p = jnp.sqrt(weight * partner_ref[1, rows])
+        face_o = jnp.sqrt(weight * outer_ref[1, rows])
         face_xp = jnp.sqrt(weight * wext_ref[pl.ds(8 * i + 9, 8)])
         face_xm = jnp.sqrt(weight * wext_ref[pl.ds(8 * i + 7, 8)])
         face_yp = jnp.where(inner, jnp.sqrt(weight * pltpu.roll(weight, N - 1, 1)), 0.0)
         face_ym = pltpu.roll(face_yp, 1, 1)
         diagonal = SHIFT_RATE * weight + jnp.where(weight > 0.0, 0.0, 1.0)
-        diagonal = diagonal + face_zp + face_zm + face_xp + face_xm + face_yp + face_ym
-        flux = face_zm * (below_ref[0, rows] + accel_z) - face_zp * (accel_z + above_ref[0, rows])
-        flux = flux + face_xm * (aext_ref[pl.ds(8 * i + 7, 8)] + accel_x)
+        diagonal = diagonal + face_p + face_o + face_xp + face_xm + face_yp + face_ym
+        flux = face_p * (partner_ref[0, rows] + accel_z) - face_o * (accel_z + outer_ref[0, rows])
+        flux = sign * flux + face_xm * (aext_ref[pl.ds(8 * i + 7, 8)] + accel_x)
         flux = flux - face_xp * (accel_x + aext_ref[pl.ds(8 * i + 9, 8)])
         flux_y = face_yp * (accel_y + pltpu.roll(accel_y, N - 1, 1))
         flux = flux + pltpu.roll(flux_y, 1, 1) - flux_y
         source_ref[rows] = 0.5 * flux
-        for k, face in enumerate((face_zp, face_zm, face_xp, face_xm, face_yp, face_ym, diagonal)):
+        for k, face in enumerate((face_p, face_o, face_xp, face_xm, face_yp, face_ym, diagonal)):
             faces_ref[k, rows] = face
     to_modes(source_ref, even_ref, odd_ref, small_ref, column_ref, lam_ref, fold_ref, modes_ref, ends_ref)
 
 
 def update_kernel(
-    slab_ref, modes_ref, all_ends_ref, fields_ref, cut_ref, near_far_ref, even_ref, odd_ref, small_t_ref,
+    place_ref, modes_ref, all_ends_ref, z_ref, cut_ref, near_far_ref, even_ref, odd_ref, small_t_ref,
     column_ref, lam_ref, update_ref, rim_ref, work_ref,
 ):
-    slab = slab_ref[0]
+    slab = place_ref[0]
 
     def jump(m):
         total = jnp.zeros((16, 128), F32)
@@ -278,16 +275,16 @@
         odd = work_ref[rows, H:]
         value = jnp.concatenate([even + odd, mirrored(even - odd)], axis=1)
         if i < XL // 8:
-            update_ref[rows] = jnp.where(fields_ref[3, rows] > 0.0, value, 0.0)
+            update_ref[rows] = jnp.where(z_ref[1, rows] > 0.0, value, 0.0)
         else:
             rim_ref[...] = value
 
 
-def image_rows(i, value_ref, above_ref, below_ref, faces_ref, ext_ref):
+def image_rows(i, value_ref, partner_ref, outer_ref, faces_ref, ext_ref):
     rows = pl.ds(8 * i, 8)
     value = value_ref[rows]
     image = faces_ref[6, rows] * value
-    image = image - (faces_ref[0, rows] * above_ref[rows] + faces_ref[1, rows] * below_ref[rows])
+    image = image - (faces_ref[0, rows] * partner_ref[rows] + faces_ref[1, rows] * outer_ref[rows])
     image = image - (faces_ref[2, rows] * ext_ref[pl.ds(8 * i + 9, 8)] + faces_ref[3, rows] * ext_ref[pl.ds(8 * i + 7, 8)])
     image = image - (faces_ref[4, rows] * pltpu.roll(value, N - 1, 1) + faces_ref[5, rows] * pltpu.roll(value, 1, 1))
     return value, image
@@ -300,24 +297,24 @@
 
 
 def image_kernel(
-    value_ref, rim_ref, above_ref, below_ref, faces_ref, even_ref, odd_ref, small_ref, column_ref, lam_ref,
+    value_ref, rim_ref, partner_ref, outer_ref, faces_ref, even_ref, odd_ref, small_ref, column_ref, lam_ref,
     image_ref, modes_ref, ends_ref, ext_ref, fold_ref,
 ):
     extend(value_ref, rim_ref, ext_ref)
     for i in range(XL // 8):
-        image_ref[pl.ds(8 * i, 8)] = image_rows(i, value_ref, above_ref, below_ref, faces_ref, ext_ref)[1]
+        image_ref[pl.ds(8 * i, 8)] = image_rows(i, value_ref, partner_ref, outer_ref, faces_ref, ext_ref)[1]
     to_modes(image_ref, even_ref, odd_ref, small_ref, column_ref, lam_ref, fold_ref, modes_ref, ends_ref)
 
 
 def sums_kernel(
-    value_ref, rim_ref, above_ref, below_ref, faces_ref, source_ref, update_ref, first_image_ref,
+    value_ref, rim_ref, partner_ref, outer_ref, faces_ref, source_ref, update_ref, first_image_ref,
     image_ref, sums_ref, ext_ref,
 ):
     extend(value_ref, rim_ref, ext_ref)
     totals = [jnp.zeros((8, N), F32) for _ in range(6)]
     for i in range(XL // 8):
         rows = pl.ds(8 * i, 8)
-        v, t = image_rows(i, value_ref, above_ref, below_ref, faces_ref, ext_ref)
+        v, t = image_rows(i, value_ref, partner_ref, outer_ref, faces_ref, ext_ref)
         image_ref[rows] = t
         r, u, q = source_ref[rows], update_ref[rows], first_image_ref[rows]
         for k, (a, b) in enumerate(((r, u), (u, q), (r, v), (q, v), (u, t), (v, t))):
@@ -329,6 +326,14 @@
     lines = jnp.concatenate(lines + [jnp.zeros((2, 128), F32)], axis=0)
     for j in range(OWNERS):
         sums_ref[j] = lines
+
+
+def add_kernel(sums_ref, out_ref):
+    total = sums_ref[0]
+    for j in range(1, OWNERS):
+        total = total + sums_ref[j]
+    for j in range(SLABS):
+        out_ref[j] = total
 
 
 def final_kernel(sums_ref, source_ref, u_ref, q_ref, v_ref, t_ref, solution_ref, residual_ref):
@@ -356,13 +361,25 @@
 
 
 def shape(*dims):
-    return jax.ShapeDtypeStruct(dims, F32)
+    return pltpu.VMEM(dims, F32)
 
 
 def call(kernel, out_shape, in_specs, out_specs, scratch=(), name=None):
-    return pl.pallas_call(
-        kernel, out_shape=out_shape, in_specs=in_specs, out_specs=out_specs, scratch_shapes=list(scratch), name=name
+    run = pl.pallas_call(
+        kernel, out_shape=out_shape, in_specs=in_specs, out_specs=out_specs, scratch_shapes=list(scratch), name=name,
+        compiler_params=pltpu.CompilerParams(vmem_limit_bytes=16 * 2**20),
     )
+
+    def with_spaces(*operands):
+        assert len(operands) == len(in_specs)
+        return run(
+            *(
+                x if spec is SMEM else pltpu.with_memory_space_constraint(x, spec.memory_space)
+                for x, spec in zip(operands, in_specs)
+            )
+        )
+
+    return with_spaces
 
 
 PLANE = (XL, N)
@@ -375,44 +392,45 @@
     dct = (constant["even"], constant["odd"])
     slab_tables = (constant["column"], constant["lam_y"])
     forward = dct + (constant["small"],) + slab_tables
-    slab = lax.axis_index("gx")
+    place = jnp.stack([lax.axis_index("gx"), lax.axis_index("yz_2")])
     slabs, owners = lax.axis_size("gx"), lax.axis_size(YZ)
-    up_z = [(i, i + 1) for i in range(owners - 1)]
-    down_z = [(b, a) for a, b in up_z]
     up_x = [(i, i + 1) for i in range(slabs - 1)]
     down_x = [(b, a) for a, b in up_x]
+    on_chip = [(0, 1), (1, 0)]
+    off_chip = [pair for i in range(1, owners - 1, 2) for pair in ((i, i + 1), (i + 1, i))]
+
+    def neighbours(value):
+        outer = lax.ppermute(value, YZ, off_chip)
+        return lax.ppermute(value, "yz_2", on_chip), outer
 
     send = call(
         pack_kernel,
         shape(OWNERS, SEND_ROWS, 128),
-        [SMEM, ANY, ANY],
+        [SMEM, SMEM, HBM, HBM],
         VMEM,
         [pltpu.SMEM((OWNERS,), jnp.int32), pltpu.SemaphoreType.DMA],
         name="pack",
-    )(brick_slot[0], camera_accel[0].reshape(PLANE_BRICKS, 3 * BR, B), camera_weight[0])
+    )(place, brick_slot[0], camera_accel[0].reshape(PLANE_BRICKS, 3 * BR, B), camera_weight[0])
     got = lax.all_to_all(send, YZ, split_axis=0, concat_axis=0, tiled=True)
-    ids = got[:, PAIR_ROWS : PAIR_ROWS + PER_PAIR, 0].astype(jnp.int32).reshape(-1)
-    fields, first, last = call(
+    z_fields, xy_fields, first, last = call(
         place_kernel,
-        (shape(4, *PLANE), shape(2, N), shape(2, N)),
-        [SMEM, SMEM, ANY],
-        (VMEM, VMEM, VMEM),
-        [pltpu.SemaphoreType.DMA],
+        (shape(2, *PLANE), shape(2, *PLANE), shape(2, N), shape(2, N)),
+        [SMEM, VMEM],
+        (VMEM,) * 4,
+        [pltpu.SMEM((OWNERS, 1, 128), F32), pltpu.SemaphoreType.DMA],
         name="place",
-    )(ids, brick_solid[0], got)
-    beside = fields[jnp.array([0, 3])]
-    above = lax.ppermute(beside, YZ, down_z)
-    below = lax.ppermute(beside, YZ, up_z)
+    )(brick_solid[0], got)
+    partner, outer = neighbours(z_fields)
     xlo = lax.ppermute(last, "gx", up_x)
     xhi = lax.ppermute(first, "gx", down_x)
     faces, source, modes, ends = call(
         setup_kernel,
         (shape(7, *PLANE), shape(*PLANE), shape(*PLANE), shape(SLABS, 16, 128)),
-        [VMEM] * 10,
+        [SMEM] + [VMEM] * 11,
         (VMEM,) * 4,
         [EXT, EXT, FOLD],
         name="setup",
-    )(fields, above, below, xlo, xhi, *forward)
+    )(place, z_fields, xy_fields, partner, outer, xlo, xhi, *forward)
 
     def updated(modes, ends):
         all_ends = lax.all_to_all(ends, "gx", split_axis=0, concat_axis=0, tiled=True)
@@ -424,12 +442,9 @@
             [pltpu.VMEM((XL + 8, N), F32)],
             name="update",
         )(
-            slab.reshape(1), modes, all_ends, fields, constant["cut"], constant["ends"],
+            place, modes, all_ends, z_fields, constant["cut"], constant["ends"],
             *dct, constant["small_t"], *slab_tables,
         )
-
-    def neighbours(value):
-        return lax.ppermute(value, YZ, down_z), lax.ppermute(value, YZ, up_z)
 
     u, rim = updated(modes, ends)
     q, modes, ends = call(
@@ -450,10 +465,10 @@
         name="sums",
     )(v, rim, *neighbours(v), faces, source, u, q)
     sums = lax.all_to_all(sums, YZ, split_axis=0, concat_axis=0, tiled=True)
-    sums = jnp.broadcast_to(jnp.sum(sums, axis=0)[None], (SLABS, 8, 128))
+    sums = call(add_kernel, shape(SLABS, 8, 128), [VMEM], VMEM, name="add")(sums)
     sums = lax.all_to_all(sums, "gx", split_axis=0, concat_axis=0, tiled=True)
     result, residual = call(
-        final_kernel, (shape(*PLANE), shape(*PLANE)), [VMEM] * 6, (VMEM, VMEM), name="final"
+        final_kernel, (jax.ShapeDtypeStruct(PLANE, F32),) * 2, [VMEM] * 6, (VMEM, VMEM), name="final"
     )(sums, source, u, q, v, t)
     return result[None], residual[None]
 

time: 200 us -> 159 us (0.80)
  blocking collectives: 39.6 us -> 102 us
  waiting for transfers between devices: 72.7 us -> 22.2 us
  starting transfers between devices: 40.4 us -> 16.2 us
  Pallas kernels: 38.2 us -> 16.1 us
  local copies, waits for them, and re-layouts: 6.46 us -> 0.7 us
    all_to_all x0 -> x1, blocking collectives: none -> 49.8 us  [on_device(): got = lax.all_to_all(send, YZ, split_axis=0, concat_axis=0, tiled=True)]
    all_to_all x2 -> x0, waiting for transfers between devices: 48.3 us -> none  [the longest x1 41.1 us: on_device(): got = lax.all_to_all(send, YZ, split_axis=0, concat_axis=0, tiled=True)]
    pallas_call x8 -> x9, Pallas kernels: 38.2 us -> 16.1 us  [with_spaces(): run(*(x if spec is SMEM else pltpu.with_memory_space_constraint(x, spec.m...]
    all_to_all x2 -> x0, starting transfers between devices: 16.8 us -> none  [the longest x1 8.59 us: on_device(): got = lax.all_to_all(send, YZ, split_axis=0, concat_axis=0, tiled=True)]
    all_to_all x1 -> x2, blocking collectives: 11.2 us -> 24.8 us  [updated(): lax.all_to_all(ends, 'gx', split_axis=0, concat_axis=0, tiled=True)]
    ppermute x6, starting transfers between devices: 18.7 us -> 11.4 us  [the longest x3 11.1 us: neighbours(): outer = lax.ppermute(value, YZ, off_chip)]
    unnamed x20, local copies, waits for them, and re-layouts: 3.29 us -> 0.7 us
    gather x1 -> x0, local copies, waits for them, and re-layouts: 2.2 us -> none  [on_device(): beside = fields[jnp.array([0, 3])]]
  transfers between devices with their start and end apart: 10 -> 8, of which waited for: 9 -> 4; matrix products, arithmetic and copies ran while one was open for 0% -> 0% of each run, Pallas kernels for 0% -> 0%
where the time goes in v2:
time: 159 us; the launch traced here: 158 us
  blocking collectives  102 us (64%)
  waiting for transfers between devices  22.2 us (14%)
  starting transfers between devices  16.2 us (10%)
  Pallas kernels  16.1 us (10%)
    all_to_all x1, blocking collectives, on_device(): got = lax.all_to_all(send, YZ, split_axis=0, concat_axis=0, tiled=True)  49.8 us
    all_to_all x2, blocking collectives, updated(): lax.all_to_all(ends, 'gx', split_axis=0, concat_axis=0, tiled=True)  24.8 us
    ppermute x3, waiting for transfers between devices, neighbours(): outer = lax.ppermute(value, YZ, off_chip)  18.9 us
    all_to_all x1, blocking collectives, on_device(): sums = lax.all_to_all(sums, YZ, split_axis=0, concat_axis=0, tiled=True)  18.1 us
    pallas_call x9, Pallas kernels, with_spaces(): run(*(x if spec is SMEM else pltpu.with_memory_space_constraint(x, spec.m...  16.1 us
    ppermute x3, starting transfers between devices, neighbours(): outer = lax.ppermute(value, YZ, off_chip)  11.1 us
    all_to_all x1, blocking collectives, on_device(): sums = lax.all_to_all(sums, 'gx', split_axis=0, concat_axis=0, tiled=True)  9.24 us
    ppermute x1, starting transfers between devices, on_device(): xlo = lax.ppermute(last, 'gx', up_x)  3.54 us
  transfers between devices with their start and end apart: 8, of which 4 were waited for; matrix products, arithmetic and copies ran while one was open for 0% of the time, Pallas kernels for 0%

profile of v2, /device:TPU:1, one launch (start us, length us, event | category | flops | bytes accessed | tf_op | source)
XLA Modules:
  0.0 158.1 jit_solution(11460197695957666405)
XLA Ops:
  0.6 0.1 pad_add_fusion.place_ref
  0.7 0.0 copy-start.8
  0.7 0.7 copy-done.8
  1.4 2.6 %pack.1 = f32[32,200,128]{2,1,0:T(8,128)S(1)} custom-call(s32[2]{0:T(128)S(1)} %pad_add_fusion.place_ref, s32[64]{0:T(128)S(1)} %bitcast.8, f32[64,48,128]{2,1,0:T(8,128)} %bitcast.10, f32[64,16,128]{2,1,0:T(8,128)} %bitcast.11), custom_call_target="tpu_custom_call" | custom-call | tf_op jit(solution)/shard_map/pack/pallas_call | solution.py:375
  4.0 0.0 copy-start.9
  4.0 49.8 %all_to_all.25.got_ref = f32[32,200,128]{2,1,0:T(8,128)S(1)} all-to-all(f32[32,200,128]{2,1,0:T(8,128)S(1)} %pack.1), channel_id=1, replica_groups=mesh['gx'=8,'yz_0'=4,'yz_1'=4,'yz_2'=2] {'yz_0','yz_1','yz_2'}, dimensions={0} | all-to-all | bytes 6553600 | tf_op jit(solution)/shard_map/all_to_all | solution.py:414
  53.7 0.0 copy-start
  53.7 0.0 copy-start.1
  53.7 0.0 copy-start.3
  53.7 0.0 copy-start.5
  53.7 0.0 copy-start.6
  53.7 0.0 copy-done.9
  53.8 3.1 %place.1 = (f32[2,128,1024]{2,1,0:T(8,128)S(1)}, f32[2,128,1024]{2,1,0:T(8,128)S(1)}, f32[2,1024]{1,0:T(2,128)S(1)}, f32[2,1024]{1,0:T(2,128)S(1)}) custom-call(s32[64]{0:T(128)S(1)} %bitcast.9, f32[32,200,128]{2,1,0:T(8,128)S(1)} %all_to_all.25.got_ref), custom_call_target="tpu_custom_call" | custom-call | tf_op jit(solution)/shard_map/place/pallas_call | solution.py:375
  56.9 2.4 %collective-permute-start.1 = (f32[2,128,1024]{2,1,0:T(8,128)S(1)}, f32[2,128,1024]{2,1,0:T(8,128)S(1)}, u32[]{:S(2)}, u32[]{:S(2)}) collective-permute-start(f32[2,128,1024]{2,1,0:T(8,128)S(1)} %get-tuple-element.21.z_ref), channel_id=1, source_target_pairs={{1,2},{2,1},{3,4},{4,3},{5,6},{6,5},{7,8},{8,7},{9,10},{10,9},{11,... | collective-permute-start | bytes 3145736 | tf_op jit(solution)/shard_map/ppermute | solution.py:403
  59.3 0.1 collective-permute-start
  59.4 3.5 %collective-permute-start.2 = (f32[2,1024]{1,0:T(2,128)S(1)}, f32[2,1024]{1,0:T(2,128)S(1)}, u32[]{:S(2)}, u32[]{:S(2)}) collective-permute-start(f32[2,1024]{1,0:T(2,128)S(1)} %get-tuple-element.23), channel_id=1, source_target_pairs={{0,32},{32,64},{64,96},{96,128},{128,160},{160,192},{192,224},{1,3... | collective-permute-start | bytes 24584 | tf_op jit(solution)/shard_map/ppermute | solution.py:424
  63.0 1.3 collective-permute-start.3
  64.3 0.0 collective-permute-done.2.xlo_ref
  64.3 3.3 %collective-permute-done.3.xhi_ref = f32[2,1024]{1,0:T(2,128)S(1)} collective-permute-done((f32[2,1024]{1,0:T(2,128)S(1)}, f32[2,1024]{1,0:T(2,128)S(1)}, u32[]{:S(2)}, u32[]{:S(2)}) %collective-permute-start.3) | collective-permute-done | bytes 8224 | tf_op jit(solution)/shard_map/ppermute | solution.py:425
  67.6 5.4 %collective-permute-done.1.outer_ref = f32[2,128,1024]{2,1,0:T(8,128)S(1)} collective-permute-done((f32[2,128,1024]{2,1,0:T(8,128)S(1)}, f32[2,128,1024]{2,1,0:T(8,128)S(1)}, u32[]{:S(2)}, u32[]{:S(2)}) %collective-permute-start.1) | collective-permute-done | bytes 1048608 | tf_op jit(solution)/shard_map/ppermute | solution.py:403
  73.0 0.0 collective-permute-done.partner_ref
  73.0 0.0 copy-done
  73.0 0.0 copy-done.1
  73.0 0.0 copy-done.3
  73.0 0.0 copy-done.5
  73.0 0.0 copy-done.6
  73.0 0.0 copy-start.2
  73.0 0.0 copy-start.4
  73.1 0.0 copy-start.7
  73.1 3.1 %setup.1 = (f32[7,128,1024]{2,1,0:T(8,128)S(1)}, f32[128,1024]{1,0:T(8,128)S(1)}, f32[128,1024]{1,0:T(8,128)S(1)}, f32[8,16,128]{2,1,0:T(8,128)S(1)}) custom-call(s32[2]{0:T(128)S(1)} %pad_add_fusion.place_ref, f32[2,128,1024]{2,1,0:T(8,128)S(1)} %get-tuple-element.21.z_ref, f32[2,128,1024]{2,1,0:T(8,128)S(1)} %get-tuple-element.22.xy_ref, ...), custom_call_target="tpu_custom_call" | custom-call | tf_op jit(solution)/shard_map/setup/pallas_call | solution.py:375
  76.2 15.2 %all_to_all.26.all_ends_ref = f32[8,16,128]{2,1,0:T(8,128)S(1)} all-to-all(f32[8,16,128]{2,1,0:T(8,128)S(1)} %get-tuple-element.26), channel_id=1, replica_groups=mesh['gx'=8,'yz_0'=4,'yz_1'=4,'yz_2'=2] {'gx'}, dimensions={0} | all-to-all | bytes 131072 | tf_op jit(solution)/shard_map/all_to_all | solution.py:436
  91.4 0.0 copy-done.2
  91.4 0.0 copy-done.4
  91.4 0.0 copy-done.7
  91.4 1.7 %update.2 = (f32[128,1024]{1,0:T(8,128)S(1)}, f32[8,1024]{1,0:T(8,128)S(1)}) custom-call(s32[2]{0:T(128)S(1)} %pad_add_fusion.place_ref, f32[128,1024]{1,0:T(8,128)S(1)} %get-tuple-element.25.modes_ref, f32[8,16,128]{2,1,0:T(8,128)S(1)} %all_to_all.26.all_ends_ref, f32[2,128,1024]{2,1,0:T(8,128)S(1)} %get-tuple-element.21.z_ref, ...), custom_call_target="tpu_custom_call" | custom-call | tf_op jit(solution)/shard_map/update/pallas_call | solution.py:375
  93.1 3.9 %collective-permute-start.5 = (f32[128,1024]{1,0:T(8,128)S(1)}, f32[128,1024]{1,0:T(8,128)S(1)}, u32[]{:S(2)}, u32[]{:S(2)}) collective-permute-start(f32[128,1024]{1,0:T(8,128)S(1)} %get-tuple-element.27.value_ref.update_ref.u_ref), channel_id=1, source_target_pairs={{1,2},{2,1},{3,4},{4,3},{5,6},{6,5},{7,8},{8,7},{9,10},{10,9},{11,... | collective-permute-start | bytes 1572872 | tf_op jit(solution)/shard_map/ppermute | solution.py:403
  97.0 0.1 collective-permute-start.4
  97.1 6.7 %collective-permute-done.5.outer_ref = f32[128,1024]{1,0:T(8,128)S(1)} collective-permute-done((f32[128,1024]{1,0:T(8,128)S(1)}, f32[128,1024]{1,0:T(8,128)S(1)}, u32[]{:S(2)}, u32[]{:S(2)}) %collective-permute-start.5) | collective-permute-done | bytes 524320 | tf_op jit(solution)/shard_map/ppermute | solution.py:403
  103.9 0.0 collective-permute-done.4.partner_ref
  103.9 1.6 %image.1 = (f32[128,1024]{1,0:T(8,128)S(1)}, f32[128,1024]{1,0:T(8,128)S(1)}, f32[8,16,128]{2,1,0:T(8,128)S(1)}) custom-call(f32[128,1024]{1,0:T(8,128)S(1)} %get-tuple-element.27.value_ref.update_ref.u_ref, f32[8,1024]{1,0:T(8,128)S(1)} %get-tuple-element.28.rim_ref, f32[128,1024]{1,0:T(8,128)S(1)} %collective-permute-done.4.partner_ref, ...), custom_call_target="tpu_custom_call" | custom-call | tf_op jit(solution)/shard_map/image/pallas_call | solution.py:375
  105.5 9.6 %all_to_all.27.all_ends_ref = f32[8,16,128]{2,1,0:T(8,128)S(1)} all-to-all(f32[8,16,128]{2,1,0:T(8,128)S(1)} %get-tuple-element.31), channel_id=1, replica_groups=mesh['gx'=8,'yz_0'=4,'yz_1'=4,'yz_2'=2] {'gx'}, dimensions={0} | all-to-all | bytes 131072 | tf_op jit(solution)/shard_map/all_to_all | solution.py:436
  115.1 1.7 %update.3 = (f32[128,1024]{1,0:T(8,128)S(1)}, f32[8,1024]{1,0:T(8,128)S(1)}) custom-call(s32[2]{0:T(128)S(1)} %pad_add_fusion.place_ref, f32[128,1024]{1,0:T(8,128)S(1)} %get-tuple-element.30.modes_ref, f32[8,16,128]{2,1,0:T(8,128)S(1)} %all_to_all.27.all_ends_ref, f32[2,128,1024]{2,1,0:T(8,128)S(1)} %get-tuple-element.21.z_ref, ...), custom_call_target="tpu_custom_call" | custom-call | tf_op jit(solution)/shard_map/update/pallas_call | solution.py:375
  116.8 4.8 %collective-permute-start.7 = (f32[128,1024]{1,0:T(8,128)S(1)}, f32[128,1024]{1,0:T(8,128)S(1)}, u32[]{:S(2)}, u32[]{:S(2)}) collective-permute-start(f32[128,1024]{1,0:T(8,128)S(1)} %get-tuple-element.32.value_ref.v_ref), channel_id=1, source_target_pairs={{1,2},{2,1},{3,4},{4,3},{5,6},{6,5},{7,8},{8,7},{9,10},{10,9},{11,... | collective-permute-start | bytes 1572872 | tf_op jit(solution)/shard_map/ppermute | solution.py:403
  121.6 0.1 collective-permute-start.6
  121.7 6.7 %collective-permute-done.7.outer_ref = f32[128,1024]{1,0:T(8,128)S(1)} collective-permute-done((f32[128,1024]{1,0:T(8,128)S(1)}, f32[128,1024]{1,0:T(8,128)S(1)}, u32[]{:S(2)}, u32[]{:S(2)}) %collective-permute-start.7) | collective-permute-done | bytes 524320 | tf_op jit(solution)/shard_map/ppermute | solution.py:403
  128.4 0.0 collective-permute-done.6.partner_ref
  128.4 0.9 sums.1
  129.3 18.1 %all_to_all.28.sums_ref = f32[32,8,128]{2,1,0:T(8,128)S(1)} all-to-all(f32[32,8,128]{2,1,0:T(8,128)S(1)} %get-tuple-element.36), channel_id=1, replica_groups=mesh['gx'=8,'yz_0'=4,'yz_1'=4,'yz_2'=2] {'yz_0','yz_1','yz_2'}, dimensions={0} | all-to-all | bytes 262144 | tf_op jit(solution)/shard_map/all_to_all | solution.py:467
  147.5 9.2 %all_to_all.29.sums_ref = f32[8,8,128]{2,1,0:T(8,128)S(1)} all-to-all(f32[8,8,128]{2,1,0:T(8,128)S(1)} %add.3), channel_id=1, replica_groups=mesh['gx'=8,'yz_0'=4,'yz_1'=4,'yz_2'=2] {'gx'}, dimensions={0} | all-to-all | bytes 65536 | tf_op jit(solution)/shard_map/all_to_all | solution.py:469
  156.7 1.4 final.1
  (1 shorter events, 0.0 us)
Async XLA Ops:
  0.7 0.7 copy-start.8
  4.0 49.8 %copy-start.9 = (s32[1,64]{1,0:T(1,128)S(1)}, s32[1,64]{1,0:T(1,128)}, u32[]{:S(2)}) copy-start(s32[1,64]{1,0:T(1,128)} %param.15) | copy-start | bytes 772
  53.7 19.3 %copy-start = (bf16[2,512,512]{2,1,0:T(8,128)(2,1)S(1)}, bf16[2,512,512]{2,1,0:T(8,128)(2,1)}, u32[]{:S(2)}) copy-start(bf16[2,512,512]{2,1,0:T(8,128)(2,1)} %constant.27.clone.odd_ref) | copy-start | bytes 3145732
  53.7 19.3 %copy-start.1 = (bf16[2,512,512]{2,1,0:T(8,128)(2,1)S(1)}, bf16[2,512,512]{2,1,0:T(8,128)(2,1)}, u32[]{:S(2)}) copy-start(bf16[2,512,512]{2,1,0:T(8,128)(2,1)} %constant.26.clone.even_ref) | copy-start | bytes 3145732
  53.7 19.3 %copy-start.3 = (f32[128,128]{1,0:T(8,128)S(1)}, f32[128,128]{1,0:T(8,128)}, u32[]{:S(2)}) copy-start(f32[128,128]{1,0:T(8,128)} %constant.30.clone.column_ref) | copy-start | bytes 196612
  53.7 19.3 %copy-start.5 = (bf16[256,128]{1,0:T(8,128)(2,1)S(1)}, bf16[256,128]{1,0:T(8,128)(2,1)}, u32[]{:S(2)}) copy-start(bf16[256,128]{1,0:T(8,128)(2,1)} %constant.28.clone.small_ref) | copy-start | bytes 196612
  53.7 19.3 %copy-start.6 = (f32[1,1024]{1,0:T(1,128)S(1)}, f32[1,1024]{1,0:T(1,128)}, u32[]{:S(2)}) copy-start(f32[1,1024]{1,0:T(1,128)} %constant.31.clone.lam_ref) | copy-start | bytes 12292
  56.9 16.1 %collective-permute-start.1 = (f32[2,128,1024]{2,1,0:T(8,128)S(1)}, f32[2,128,1024]{2,1,0:T(8,128)S(1)}, u32[]{:S(2)}, u32[]{:S(2)}) collective-permute-start(f32[2,128,1024]{2,1,0:T(8,128)S(1)} %get-tuple-element.21.z_ref), channel_id=1, source_target_pairs={{1,2},{2,1},{3,4},{4,3},{5,6},{6,5},{7,8},{8,7},{9,10},{10,9},{11,... | collective-permute-start | bytes 3145736 | tf_op jit(solution)/shard_map/ppermute | solution.py:403
  59.3 13.7 %collective-permute-start = (f32[2,128,1024]{2,1,0:T(8,128)S(1)}, f32[2,128,1024]{2,1,0:T(8,128)S(1)}, u32[]{:S(2)}, u32[]{:S(2)}) collective-permute-start(f32[2,128,1024]{2,1,0:T(8,128)S(1)} %get-tuple-element.21.z_ref), channel_id=1, source_target_pairs={{0,1},{1,0},{2,3},{3,2},{4,5},{5,4},{6,7},{7,6},{8,9},{9,8},{10,11... | collective-permute-start | bytes 3145736 | tf_op jit(solution)/shard_map/ppermute | solution.py:404
  59.4 4.9 %collective-permute-start.2 = (f32[2,1024]{1,0:T(2,128)S(1)}, f32[2,1024]{1,0:T(2,128)S(1)}, u32[]{:S(2)}, u32[]{:S(2)}) collective-permute-start(f32[2,1024]{1,0:T(2,128)S(1)} %get-tuple-element.23), channel_id=1, source_target_pairs={{0,32},{32,64},{64,96},{96,128},{128,160},{160,192},{192,224},{1,3... | collective-permute-start | bytes 24584 | tf_op jit(solution)/shard_map/ppermute | solution.py:424
  63.0 4.6 %collective-permute-start.3 = (f32[2,1024]{1,0:T(2,128)S(1)}, f32[2,1024]{1,0:T(2,128)S(1)}, u32[]{:S(2)}, u32[]{:S(2)}) collective-permute-start(f32[2,1024]{1,0:T(2,128)S(1)} %get-tuple-element.24), channel_id=1, source_target_pairs={{32,0},{64,32},{96,64},{128,96},{160,128},{192,160},{224,192},{33,... | collective-permute-start | bytes 24584 | tf_op jit(solution)/shard_map/ppermute | solution.py:425
  73.0 18.4 %copy-start.2 = (f32[11,8,16,128]{3,2,1,0:T(8,128)S(1)}, f32[11,8,16,128]{3,2,1,0:T(8,128)}, u32[]{:S(2)}) copy-start(f32[11,8,16,128]{3,2,1,0:T(8,128)} %constant.32.clone.cut_ref) | copy-start | bytes 2162692
  73.0 18.4 %copy-start.4 = (bf16[256,128]{1,0:T(8,128)(2,1)S(1)}, bf16[256,128]{1,0:T(8,128)(2,1)}, u32[]{:S(2)}) copy-start(bf16[256,128]{1,0:T(8,128)(2,1)} %constant.29.clone.small_t_ref) | copy-start | bytes 196612
  73.1 18.4 %copy-start.7 = (f32[2,8,128]{2,1,0:T(8,128)S(1)}, f32[2,8,128]{2,1,0:T(8,128)}, u32[]{:S(2)}) copy-start(f32[2,8,128]{2,1,0:T(8,128)} %constant.33.clone.near_far_ref) | copy-start | bytes 24580
  93.1 10.7 %collective-permute-start.5 = (f32[128,1024]{1,0:T(8,128)S(1)}, f32[128,1024]{1,0:T(8,128)S(1)}, u32[]{:S(2)}, u32[]{:S(2)}) collective-permute-start(f32[128,1024]{1,0:T(8,128)S(1)} %get-tuple-element.27.value_ref.update_ref.u_ref), channel_id=1, source_target_pairs={{1,2},{2,1},{3,4},{4,3},{5,6},{6,5},{7,8},{8,7},{9,10},{10,9},{11,... | collective-permute-start | bytes 1572872 | tf_op jit(solution)/shard_map/ppermute | solution.py:403
  97.0 6.9 %collective-permute-start.4 = (f32[128,1024]{1,0:T(8,128)S(1)}, f32[128,1024]{1,0:T(8,128)S(1)}, u32[]{:S(2)}, u32[]{:S(2)}) collective-permute-start(f32[128,1024]{1,0:T(8,128)S(1)} %get-tuple-element.27.value_ref.update_ref.u_ref), channel_id=1, source_target_pairs={{0,1},{1,0},{2,3},{3,2},{4,5},{5,4},{6,7},{7,6},{8,9},{9,8},{10,11... | collective-permute-start | bytes 1572872 | tf_op jit(solution)/shard_map/ppermute | solution.py:404
  116.8 11.7 %collective-permute-start.7 = (f32[128,1024]{1,0:T(8,128)S(1)}, f32[128,1024]{1,0:T(8,128)S(1)}, u32[]{:S(2)}, u32[]{:S(2)}) collective-permute-start(f32[128,1024]{1,0:T(8,128)S(1)} %get-tuple-element.32.value_ref.v_ref), channel_id=1, source_target_pairs={{1,2},{2,1},{3,4},{4,3},{5,6},{6,5},{7,8},{8,7},{9,10},{10,9},{11,... | collective-permute-start | bytes 1572872 | tf_op jit(solution)/shard_map/ppermute | solution.py:403
  121.6 6.9 %collective-permute-start.6 = (f32[128,1024]{1,0:T(8,128)S(1)}, f32[128,1024]{1,0:T(8,128)S(1)}, u32[]{:S(2)}, u32[]{:S(2)}) collective-permute-start(f32[128,1024]{1,0:T(8,128)S(1)} %get-tuple-element.32.value_ref.v_ref), channel_id=1, source_target_pairs={{0,1},{1,0},{2,3},{3,2},{4,5},{5,4},{6,7},{7,6},{8,9},{9,8},{10,11... | collective-permute-start | bytes 1572872 | tf_op jit(solution)/shard_map/ppermute | solution.py:404

commit v3 on v2

--- a/solution.py
+++ b/solution.py
@@ -19,9 +19,13 @@
 PLANE_BRICKS = 64
 OWNERS = 32
 PER_PAIR = 3
-BRICK_ROWS = 4 * BR
-PAIR_ROWS = PER_PAIR * BRICK_ROWS
-SEND_ROWS = PAIR_ROWS + 8
+BRICK_ROWS = 3 * BR
+SIDE_ROW = PER_PAIR * BRICK_ROWS
+END_ROW = SIDE_ROW + BR
+SEND_ROWS = END_ROW + 8
+ID_LANE = 64
+CHUNKS = 4
+GROUP = 4
 YZ = ("yz_0", "yz_1", "yz_2")
 SHIFT_RATE = 0.05
 FLOOR = 2.0
@@ -75,12 +79,7 @@
         system[:, j, j + 1] = -far
         system[:, j + 1, j] = -far
     inverse = np.linalg.inv(system)
-    joined = np.zeros((SLABS + 3, SLABS, 2, N))
-    for i in range(cuts):
-        for j in range(cuts):
-            joined[i + 2, j, 1] += inverse[:, i, j]
-            joined[i + 2, j + 1, 0] -= inverse[:, i, j]
-    out["cut"] = joined.astype(np.float32).reshape(SLABS + 3, SLABS, 16, 128)
+    out["cut"] = inverse.transpose(1, 2, 0).astype(np.float32).reshape(cuts, cuts, 8, 128)
     out["ends"] = np.stack([near, far]).astype(np.float32).reshape(2, 8, 128)
     return out
 
@@ -156,89 +155,166 @@
         ends_ref[j, 8:16] = last
 
 
-def pack_kernel(place_ref, slot_ref, accel_ref, weight_ref, out_ref, count_ref, sem):
+def pack_kernel(
+    place_ref, slot_ref, accel_hbm, weight_hbm, out_ref,
+    count_ref, held_ref, number_ref, accel_ref, weight_ref, inner_ref, side_ref, sem,
+):
     del place_ref
+    size = PLANE_BRICKS // CHUNKS
+    copies = []
+    for chunk in range(CHUNKS):
+        bricks = pl.ds(chunk * size, size)
+        copies.append(
+            (
+                pltpu.make_async_copy(accel_hbm.at[bricks], accel_ref.at[bricks], sem.at[0, chunk]),
+                pltpu.make_async_copy(weight_hbm.at[bricks], weight_ref.at[bricks], sem.at[1, chunk]),
+            )
+        )
+        for copy in copies[-1]:
+            copy.start()
     for o in range(OWNERS):
         count_ref[o] = 0
-    out_ref[:, PAIR_ROWS:] = jnp.full((OWNERS, 8, 128), -1.0, F32)
-    lane = lax.broadcasted_iota(jnp.int32, (1, 128), 1)
-
-    def one(s, carry):
+    for k in range(OWNERS * PER_PAIR):
+        held_ref[k] = 0
+        number_ref[k] = -1
+
+    def assign(s, carry):
         brick = slot_ref[s]
         owner = brick // PLANE_BRICKS
         place = count_ref[owner]
         count_ref[owner] = place + 1
-        number = (brick - owner * PLANE_BRICKS).astype(F32)
-        line = out_ref[owner, PAIR_ROWS : PAIR_ROWS + 1, :]
-        out_ref[owner, PAIR_ROWS : PAIR_ROWS + 1, :] = jnp.where(lane == place, number, line)
-        at = pl.multiple_of(place * BRICK_ROWS, BRICK_ROWS)
-        pltpu.make_async_copy(accel_ref.at[s], out_ref.at[owner, pl.ds(at, 3 * BR)], sem).start()
-        pltpu.make_async_copy(weight_ref.at[s], out_ref.at[owner, pl.ds(at + 3 * BR, BR)], sem).start()
+        held_ref[owner * PER_PAIR + place] = s
+        number_ref[owner * PER_PAIR + place] = brick - owner * PLANE_BRICKS
         return carry
 
-    lax.fori_loop(0, PLANE_BRICKS, one, 0)
-    sent = out_ref.at[:, pl.ds(0, PLANE_BRICKS * BRICK_ROWS // OWNERS)]
-    pltpu.make_async_copy(sent, sent, sem).wait()
-
-
-def place_kernel(solid_ref, got_ref, z_ref, xy_ref, first_ref, last_ref, ids_ref, sem):
-    ids_copy = pltpu.make_async_copy(got_ref.at[:, pl.ds(PAIR_ROWS, 1)], ids_ref, sem)
+    lax.fori_loop(0, PLANE_BRICKS, assign, 0, unroll=4)
+    dims = (GROUP, BR, B)
+    lane = lax.broadcasted_iota(jnp.int32, dims, 2)
+    row = lax.broadcasted_iota(jnp.int32, dims, 1)
+
+    def inside(group, carry):
+        bricks = pl.ds(group * GROUP, GROUP)
+        accel_x, accel_y = accel_ref[bricks, BR : 2 * BR], accel_ref[bricks, 2 * BR :]
+        weight = weight_ref[bricks]
+        flux_x = jnp.sqrt(weight * pltpu.roll(weight, BR - 1, 1)) * (accel_x + pltpu.roll(accel_x, BR - 1, 1))
+        flux_y = jnp.sqrt(weight * pltpu.roll(weight, B - 1, 2)) * (accel_y + pltpu.roll(accel_y, B - 1, 2))
+        flux_x = jnp.where(row < BR - 1, flux_x, 0.0)
+        flux_y = jnp.where(lane < B - 1, flux_y, 0.0)
+        inner_ref[bricks] = 0.5 * (pltpu.roll(flux_x, 1, 1) - flux_x + pltpu.roll(flux_y, 1, 2) - flux_y)
+        low = jnp.broadcast_to(accel_y[:, :, :1], dims)
+        high = jnp.broadcast_to(accel_y[:, :, B - 1 :], dims)
+        side_ref[bricks] = jnp.where(lane < ID_LANE, low, high)
+        return carry
+
+    for chunk in range(CHUNKS):
+        for copy in copies[chunk]:
+            copy.wait()
+        lax.fori_loop(chunk * size // GROUP, (chunk + 1) * size // GROUP, inside, 0)
+    lane, row = lane[0], row[0, :8]
+
+    def fill(owner, carry):
+        sides = jnp.zeros((BR, B), F32)
+        ends = jnp.zeros((8, B), F32)
+        for place in range(PER_PAIR):
+            s = held_ref[owner * PER_PAIR + place]
+            number = number_ref[owner * PER_PAIR + place].astype(F32)
+            at = place * BRICK_ROWS
+            out_ref[owner, at : at + BR] = accel_ref[s, :BR]
+            out_ref[owner, at + BR : at + 2 * BR] = inner_ref[s]
+            out_ref[owner, at + 2 * BR : at + 3 * BR] = weight_ref[s]
+            sides = jnp.where((lane == place) | (lane == B - 1 - place), side_ref[s], sides)
+            sides = jnp.where(lane == ID_LANE + place, number, sides)
+            ends = jnp.where(row == 2 * place, accel_ref[s, BR : BR + 1], ends)
+            ends = jnp.where(row == 2 * place + 1, accel_ref[s, 2 * BR - 1 : 2 * BR], ends)
+        out_ref[owner, SIDE_ROW:END_ROW] = sides
+        out_ref[owner, END_ROW:] = ends
+        return carry
+
+    lax.fori_loop(0, OWNERS, fill, 0, unroll=2)
+
+
+def place_kernel(
+    solid_ref, got_ref, z_ref, source_ref, ends_ref, sides_ref, first_ref, last_ref, ids_ref, from_ref, sem
+):
+    ids_copy = pltpu.make_async_copy(got_ref.at[:, pl.ds(SIDE_ROW, 1)], ids_ref, sem)
     ids_copy.start()
     ids_copy.wait()
-
-    def one(source, carry):
+    first_lane = lax.broadcasted_iota(jnp.int32, (BR, B), 1) == 0
+    upper_half = lax.broadcasted_iota(jnp.int32, (BR, B), 0) < BR // 2
+
+    def find(source, carry):
         for place in range(PER_PAIR):
-            brick = ids_ref[source, 0, place].astype(jnp.int32)
-
-            @pl.when(brick >= 0)
-            def _():
-                fluid = (1 - solid_ref[brick]).astype(F32)
-                x_at = pl.multiple_of((brick // 8) * BR, BR)
-                y_at = pl.multiple_of((brick % 8) * B, B)
-                for channel, (ref, at) in enumerate(((z_ref, 0), (xy_ref, 0), (xy_ref, 1), (z_ref, 1))):
-                    row = place * BRICK_ROWS + channel * BR
-                    ref[at, pl.ds(x_at, BR), pl.ds(y_at, B)] = got_ref[source, row : row + BR] * fluid
-
+            brick = ids_ref[source, 0, ID_LANE + place].astype(jnp.int32)
+            from_ref[jnp.where(brick < 0, PLANE_BRICKS, brick)] = source * 4 + place
         return carry
 
-    lax.fori_loop(0, OWNERS, one, 0)
+    lax.fori_loop(0, OWNERS, find, 0, unroll=2)
+
+    def line(x, carry):
+        rows = pl.ds(pl.multiple_of(x * BR, BR), BR)
+        for y in range(N // B):
+            cols = pl.ds(y * B, B)
+            source, place = from_ref[x * (N // B) + y] // 4, from_ref[x * (N // B) + y] % 4
+            fluid = (1 - solid_ref[x * (N // B) + y]).astype(F32)
+            at = pl.multiple_of(place * BRICK_ROWS, BR)
+            z_ref[0, rows, cols] = got_ref[source, pl.ds(at, BR)]
+            source_ref[rows, cols] = got_ref[source, pl.ds(at + BR, BR)] * fluid
+            z_ref[1, rows, cols] = got_ref[source, pl.ds(at + 2 * BR, BR)] * fluid
+            sides = got_ref[source, SIDE_ROW:END_ROW]
+            low = pltpu.roll(sides, (B - place) % B, 1)
+            high = pltpu.roll(sides, place, 1)
+            sides_ref[rows, cols] = jnp.where(first_lane, low, high)
+            first = got_ref[source, pl.ds(END_ROW + 2 * place, 1)]
+            last = got_ref[source, pl.ds(END_ROW + 1 + 2 * place, 1)]
+            ends_ref[rows, cols] = jnp.where(upper_half, first, last)
+        return carry
+
+    lax.fori_loop(0, XL // BR, line, 0)
     for ref, row in ((first_ref, 0), (last_ref, XL - 1)):
         ref[0:1] = z_ref[1, row : row + 1]
-        ref[1:2] = xy_ref[0, row : row + 1]
+        ref[1:2] = ends_ref[row : row + 1]
 
 
 def setup_kernel(
-    place_ref, z_ref, xy_ref, partner_ref, outer_ref, xlo_ref, xhi_ref, even_ref, odd_ref, small_ref, column_ref,
-    lam_ref, faces_ref, source_ref, modes_ref, ends_ref, wext_ref, aext_ref, fold_ref,
+    place_ref, z_ref, inner_ref, x_ends_ref, sides_ref, partner_ref, outer_ref, xlo_ref, xhi_ref,
+    even_ref, odd_ref, small_ref, column_ref, lam_ref,
+    faces_ref, source_ref, modes_ref, ends_ref, wext_ref, fold_ref,
 ):
-    for ref, field, row in ((wext_ref, z_ref[1], 0), (aext_ref, xy_ref[0], 1)):
-        ref[7:8] = xlo_ref[row : row + 1]
-        ref[XL + 8 : XL + 9] = xhi_ref[row : row + 1]
-        ref[8 : XL + 8] = field
-    inner = lax.broadcasted_iota(jnp.int32, (8, N), 1) < N - 1
+    wext_ref[7:8] = xlo_ref[0:1]
+    wext_ref[XL + 8 : XL + 9] = xhi_ref[0:1]
+    wext_ref[8 : XL + 8] = z_ref[1]
+    lane = lax.broadcasted_iota(jnp.int32, (8, N), 1)
+    inside = lane < N - 1
+    brick_end = lane % B == B - 1
     sign = (2 * place_ref[1] - 1).astype(F32)
     for i in range(XL // 8):
         rows = pl.ds(8 * i, 8)
         accel_z = z_ref[0, rows]
         weight = z_ref[1, rows]
-        accel_x = xy_ref[0, rows]
-        accel_y = xy_ref[1, rows]
+        side = sides_ref[rows]
         face_p = jnp.sqrt(weight * partner_ref[1, rows])
         face_o = jnp.sqrt(weight * outer_ref[1, rows])
         face_xp = jnp.sqrt(weight * wext_ref[pl.ds(8 * i + 9, 8)])
         face_xm = jnp.sqrt(weight * wext_ref[pl.ds(8 * i + 7, 8)])
-        face_yp = jnp.where(inner, jnp.sqrt(weight * pltpu.roll(weight, N - 1, 1)), 0.0)
+        face_yp = jnp.where(inside, jnp.sqrt(weight * pltpu.roll(weight, N - 1, 1)), 0.0)
         face_ym = pltpu.roll(face_yp, 1, 1)
         diagonal = SHIFT_RATE * weight + jnp.where(weight > 0.0, 0.0, 1.0)
         diagonal = diagonal + face_p + face_o + face_xp + face_xm + face_yp + face_ym
         flux = face_p * (partner_ref[0, rows] + accel_z) - face_o * (accel_z + outer_ref[0, rows])
-        flux = sign * flux + face_xm * (aext_ref[pl.ds(8 * i + 7, 8)] + accel_x)
-        flux = flux - face_xp * (accel_x + aext_ref[pl.ds(8 * i + 9, 8)])
-        flux_y = face_yp * (accel_y + pltpu.roll(accel_y, N - 1, 1))
-        flux = flux + pltpu.roll(flux_y, 1, 1) - flux_y
-        source_ref[rows] = 0.5 * flux
+        flux_y = jnp.where(brick_end, face_yp * (side + pltpu.roll(side, N - 1, 1)), 0.0)
+        flux = sign * flux + pltpu.roll(flux_y, 1, 1) - flux_y
+        source_ref[rows] = inner_ref[rows] + 0.5 * flux
         for k, face in enumerate((face_p, face_o, face_xp, face_xm, face_yp, face_ym, diagonal)):
             faces_ref[k, rows] = face
+    for x in range(0, XL + 1, BR):
+        face = faces_ref[3, x : x + 1] if x < XL else faces_ref[2, x - 1 : x]
+        before = x_ends_ref[x - 1 : x] if x > 0 else xlo_ref[1:2]
+        after = x_ends_ref[x : x + 1] if x < XL else xhi_ref[1:2]
+        flux = 0.5 * face * (before + after)
+        if x > 0:
+            source_ref[x - 1 : x] = source_ref[x - 1 : x] - flux
+        if x < XL:
+            source_ref[x : x + 1] = source_ref[x : x + 1] + flux
     to_modes(source_ref, even_ref, odd_ref, small_ref, column_ref, lam_ref, fold_ref, modes_ref, ends_ref)
 
 
@@ -248,13 +324,16 @@
 ):
     slab = place_ref[0]
 
-    def jump(m):
-        total = jnp.zeros((16, 128), F32)
-        for j in range(SLABS):
-            total = total + cut_ref[slab + m, j] * all_ends_ref[j]
-        return total[:8] + total[8:]
-
-    farther_low, low, high, farther_high = (jump(m) for m in range(4))
+    steps = [all_ends_ref[j, 8:16] - all_ends_ref[j + 1, 0:8] for j in range(SLABS - 1)]
+
+    def jump(cut):
+        at = jnp.clip(cut, 0, SLABS - 2)
+        total = jnp.zeros((8, 128), F32)
+        for j, step in enumerate(steps):
+            total = total + cut_ref[at, j] * step
+        return jnp.where(at == cut, total, 0.0)
+
+    farther_low, low, high, farther_high = (jump(slab + m) for m in (-2, -1, 0, 1))
     near, far = near_far_ref[0], near_far_ref[1]
     before = all_ends_ref[jnp.maximum(slab - 1, 0), 8:16] - (near * low - far * farther_low)
     after = all_ends_ref[jnp.minimum(slab + 1, SLABS - 1), 0:8] - (far * farther_high - near * high)
@@ -408,16 +487,29 @@
         shape(OWNERS, SEND_ROWS, 128),
         [SMEM, SMEM, HBM, HBM],
         VMEM,
-        [pltpu.SMEM((OWNERS,), jnp.int32), pltpu.SemaphoreType.DMA],
+        [
+            pltpu.SMEM((OWNERS,), jnp.int32),
+            pltpu.SMEM((OWNERS * PER_PAIR,), jnp.int32),
+            pltpu.SMEM((OWNERS * PER_PAIR,), jnp.int32),
+            pltpu.VMEM((PLANE_BRICKS, 3 * BR, B), F32),
+            pltpu.VMEM((PLANE_BRICKS, BR, B), F32),
+            pltpu.VMEM((PLANE_BRICKS, BR, B), F32),
+            pltpu.VMEM((PLANE_BRICKS, BR, B), F32),
+            pltpu.SemaphoreType.DMA((2, CHUNKS)),
+        ],
         name="pack",
     )(place, brick_slot[0], camera_accel[0].reshape(PLANE_BRICKS, 3 * BR, B), camera_weight[0])
     got = lax.all_to_all(send, YZ, split_axis=0, concat_axis=0, tiled=True)
-    z_fields, xy_fields, first, last = call(
+    z_fields, inner, x_ends, sides, first, last = call(
         place_kernel,
-        (shape(2, *PLANE), shape(2, *PLANE), shape(2, N), shape(2, N)),
+        (shape(2, *PLANE), shape(*PLANE), shape(*PLANE), shape(*PLANE), shape(2, N), shape(2, N)),
         [SMEM, VMEM],
-        (VMEM,) * 4,
-        [pltpu.SMEM((OWNERS, 1, 128), F32), pltpu.SemaphoreType.DMA],
+        (VMEM,) * 6,
+        [
+            pltpu.SMEM((OWNERS, 1, B), F32),
+            pltpu.SMEM((PLANE_BRICKS + 1,), jnp.int32),
+            pltpu.SemaphoreType.DMA,
+        ],
         name="place",
     )(brick_solid[0], got)
     partner, outer = neighbours(z_fields)
@@ -426,11 +518,11 @@
     faces, source, modes, ends = call(
         setup_kernel,
         (shape(7, *PLANE), shape(*PLANE), shape(*PLANE), shape(SLABS, 16, 128)),
-        [SMEM] + [VMEM] * 11,
+        [SMEM] + [VMEM] * 13,
         (VMEM,) * 4,
-        [EXT, EXT, FOLD],
+        [EXT, FOLD],
         name="setup",
-    )(place, z_fields, xy_fields, partner, outer, xlo, xhi, *forward)
+    )(place, z_fields, inner, x_ends, sides, partner, outer, xlo, xhi, *forward)
 
     def updated(modes, ends):
         all_ends = lax.all_to_all(ends, "gx", split_axis=0, concat_axis=0, tiled=True)

time: 159 us -> 154 us (0.969)
  blocking collectives: 102 us -> 96.3 us
  Pallas kernels: 16.1 us -> 17.7 us
    all_to_all x1, blocking collectives: 49.8 us -> 43.8 us  [on_device(): got = lax.all_to_all(send, YZ, split_axis=0, concat_axis=0, tiled=True)]
where the time goes in v3:
time: 154 us
  blocking collectives  96.3 us (63%)
  waiting for transfers between devices  22.9 us (15%)
  Pallas kernels  17.7 us (11%)
  starting transfers between devices  15.1 us (10%)
    all_to_all x1, blocking collectives, on_device(): got = lax.all_to_all(send, YZ, split_axis=0, concat_axis=0, tiled=True)  43.8 us
    all_to_all x2, blocking collectives, updated(): lax.all_to_all(ends, 'gx', split_axis=0, concat_axis=0, tiled=True)  24.8 us
    ppermute x3, waiting for transfers between devices, neighbours(): outer = lax.ppermute(value, YZ, off_chip)  19.6 us
    all_to_all x1, blocking collectives, on_device(): sums = lax.all_to_all(sums, YZ, split_axis=0, concat_axis=0, tiled=True)  18.5 us
    pallas_call x9, Pallas kernels, with_spaces(): run(*(x if spec is SMEM else pltpu.with_memory_space_constraint(x, spec.m...  17.7 us
    ppermute x3, starting transfers between devices, neighbours(): outer = lax.ppermute(value, YZ, off_chip)  9.96 us
    all_to_all x1, blocking collectives, on_device(): sums = lax.all_to_all(sums, 'gx', split_axis=0, concat_axis=0, tiled=True)  9.24 us
    ppermute x1, starting transfers between devices, on_device(): xlo = lax.ppermute(last, 'gx', up_x)  3.54 us
  transfers between devices with their start and end apart: 8, of which 4 were waited for; matrix products, arithmetic and copies ran while one was open for 0% of the time, Pallas kernels for 0%

profile of v3, /device:TPU:1, one launch (start us, length us, event | category | flops | bytes accessed | tf_op | source)
XLA Modules:
  0.0 153.6 jit_solution(5137296081753461764)
XLA Ops:
  0.6 0.1 pad_add_fusion.place_ref
  0.7 0.0 copy-start.9
  0.7 0.7 copy-done.9
  1.4 4.6 %pack.1 = f32[32,168,128]{2,1,0:T(8,128)S(1)} custom-call(s32[2]{0:T(128)S(1)} %pad_add_fusion.place_ref, s32[64]{0:T(128)S(1)} %bitcast.9, f32[64,48,128]{2,1,0:T(8,128)} %bitcast.10, f32[64,16,128]{2,1,0:T(8,128)} %bitcast.11), custom_call_target="tpu_custom_call" | custom-call | tf_op jit(solution)/shard_map/pack/pallas_call | solution.py:454
  6.0 0.0 copy-start.8
  6.0 43.8 %all_to_all.25.got_ref = f32[32,168,128]{2,1,0:T(8,128)S(1)} all-to-all(f32[32,168,128]{2,1,0:T(8,128)S(1)} %pack.1), channel_id=1, replica_groups=mesh['gx'=8,'yz_0'=4,'yz_1'=4,'yz_2'=2] {'yz_0','yz_1','yz_2'}, dimensions={0} | all-to-all | bytes 5505024 | tf_op jit(solution)/shard_map/all_to_all | solution.py:502
  49.8 0.0 copy-start
  49.8 0.0 copy-start.1
  49.8 0.0 copy-start.2
  49.8 0.0 copy-start.5
  49.8 0.0 copy-start.6
  49.8 0.0 copy-done.8
  49.8 2.9 %place.1 = (f32[2,128,1024]{2,1,0:T(8,128)S(1)}, f32[128,1024]{1,0:T(8,128)S(1)}, f32[128,1024]{1,0:T(8,128)S(1)}, f32[128,1024]{1,0:T(8,128)S(1)}, f32[2,1024]{1,0:T(2,128)S(1)}, /*index=5*/f32[2,1024]{1,0:T(2,128)S(1)}) custom-call(s32[64]{0:T(128)S(1)} %bitcast.8, f32[32,168,128]{2,1,0:T(8,128)S(1)} %all_to_all.25.got_ref), custom_call_target="tpu_custom_call" | custom-call | tf_op jit(solution)/shard_map/place/pallas_call | solution.py:454
  52.7 2.0 %collective-permute-start.1 = (f32[2,128,1024]{2,1,0:T(8,128)S(1)}, f32[2,128,1024]{2,1,0:T(8,128)S(1)}, u32[]{:S(2)}, u32[]{:S(2)}) collective-permute-start(f32[2,128,1024]{2,1,0:T(8,128)S(1)} %get-tuple-element.23.z_ref), channel_id=1, source_target_pairs={{1,2},{2,1},{3,4},{4,3},{5,6},{6,5},{7,8},{8,7},{9,10},{10,9},{11,... | collective-permute-start | bytes 3145736 | tf_op jit(solution)/shard_map/ppermute | solution.py:482
  54.7 0.1 collective-permute-start
  54.8 3.5 %collective-permute-start.2 = (f32[2,1024]{1,0:T(2,128)S(1)}, f32[2,1024]{1,0:T(2,128)S(1)}, u32[]{:S(2)}, u32[]{:S(2)}) collective-permute-start(f32[2,1024]{1,0:T(2,128)S(1)} %get-tuple-element.27), channel_id=1, source_target_pairs={{0,32},{32,64},{64,96},{96,128},{128,160},{160,192},{192,224},{1,3... | collective-permute-start | bytes 24584 | tf_op jit(solution)/shard_map/ppermute | solution.py:516
  58.3 1.3 collective-permute-start.3
  59.6 0.0 collective-permute-done.2.xlo_ref
  59.7 3.3 %collective-permute-done.3.xhi_ref = f32[2,1024]{1,0:T(2,128)S(1)} collective-permute-done((f32[2,1024]{1,0:T(2,128)S(1)}, f32[2,1024]{1,0:T(2,128)S(1)}, u32[]{:S(2)}, u32[]{:S(2)}) %collective-permute-start.3) | collective-permute-done | bytes 8224 | tf_op jit(solution)/shard_map/ppermute | solution.py:517
  62.9 5.9 %collective-permute-done.1.outer_ref = f32[2,128,1024]{2,1,0:T(8,128)S(1)} collective-permute-done((f32[2,128,1024]{2,1,0:T(8,128)S(1)}, f32[2,128,1024]{2,1,0:T(8,128)S(1)}, u32[]{:S(2)}, u32[]{:S(2)}) %collective-permute-start.1) | collective-permute-done | bytes 1048608 | tf_op jit(solution)/shard_map/ppermute | solution.py:482
  68.8 0.0 collective-permute-done.partner_ref
  68.8 0.0 copy-done
  68.8 0.0 copy-done.1
  68.8 0.0 copy-done.2
  68.8 0.0 copy-done.5
  68.9 0.0 copy-done.6
  68.9 0.0 copy-start.3
  68.9 0.0 copy-start.4
  68.9 0.0 copy-start.7
  68.9 2.9 %setup.1 = (f32[7,128,1024]{2,1,0:T(8,128)S(1)}, f32[128,1024]{1,0:T(8,128)S(1)}, f32[128,1024]{1,0:T(8,128)S(1)}, f32[8,16,128]{2,1,0:T(8,128)S(1)}) custom-call(s32[2]{0:T(128)S(1)} %pad_add_fusion.place_ref, f32[2,128,1024]{2,1,0:T(8,128)S(1)} %get-tuple-element.23.z_ref, f32[128,1024]{1,0:T(8,128)S(1)} %get-tuple-element.24.inner_ref, ...), custom_call_target="tpu_custom_call" | custom-call | tf_op jit(solution)/shard_map/setup/pallas_call | solution.py:454
  71.8 15.2 %all_to_all.26.all_ends_ref = f32[8,16,128]{2,1,0:T(8,128)S(1)} all-to-all(f32[8,16,128]{2,1,0:T(8,128)S(1)} %get-tuple-element.30), channel_id=1, replica_groups=mesh['gx'=8,'yz_0'=4,'yz_1'=4,'yz_2'=2] {'gx'}, dimensions={0} | all-to-all | bytes 131072 | tf_op jit(solution)/shard_map/all_to_all | solution.py:528
  87.0 0.0 copy-done.3
  87.0 0.0 copy-done.4
  87.0 0.0 copy-done.7
  87.0 1.7 %update.2 = (f32[128,1024]{1,0:T(8,128)S(1)}, f32[8,1024]{1,0:T(8,128)S(1)}) custom-call(s32[2]{0:T(128)S(1)} %pad_add_fusion.place_ref, f32[128,1024]{1,0:T(8,128)S(1)} %get-tuple-element.29.modes_ref, f32[8,16,128]{2,1,0:T(8,128)S(1)} %all_to_all.26.all_ends_ref, f32[2,128,1024]{2,1,0:T(8,128)S(1)} %get-tuple-element.23.z_ref, ...), custom_call_target="tpu_custom_call" | custom-call | tf_op jit(solution)/shard_map/update/pallas_call | solution.py:454
  88.7 3.4 %collective-permute-start.5 = (f32[128,1024]{1,0:T(8,128)S(1)}, f32[128,1024]{1,0:T(8,128)S(1)}, u32[]{:S(2)}, u32[]{:S(2)}) collective-permute-start(f32[128,1024]{1,0:T(8,128)S(1)} %get-tuple-element.31.value_ref.update_ref.u_ref), channel_id=1, source_target_pairs={{1,2},{2,1},{3,4},{4,3},{5,6},{6,5},{7,8},{8,7},{9,10},{10,9},{11,... | collective-permute-start | bytes 1572872 | tf_op jit(solution)/shard_map/ppermute | solution.py:482
  92.2 0.1 collective-permute-start.4
  92.3 7.0 %collective-permute-done.5.outer_ref = f32[128,1024]{1,0:T(8,128)S(1)} collective-permute-done((f32[128,1024]{1,0:T(8,128)S(1)}, f32[128,1024]{1,0:T(8,128)S(1)}, u32[]{:S(2)}, u32[]{:S(2)}) %collective-permute-start.5) | collective-permute-done | bytes 524320 | tf_op jit(solution)/shard_map/ppermute | solution.py:482
  99.2 0.0 collective-permute-done.4.partner_ref
  99.2 1.6 %image.1 = (f32[128,1024]{1,0:T(8,128)S(1)}, f32[128,1024]{1,0:T(8,128)S(1)}, f32[8,16,128]{2,1,0:T(8,128)S(1)}) custom-call(f32[128,1024]{1,0:T(8,128)S(1)} %get-tuple-element.31.value_ref.update_ref.u_ref, f32[8,1024]{1,0:T(8,128)S(1)} %get-tuple-element.32.rim_ref, f32[128,1024]{1,0:T(8,128)S(1)} %collective-permute-done.4.partner_ref, ...), custom_call_target="tpu_custom_call" | custom-call | tf_op jit(solution)/shard_map/image/pallas_call | solution.py:454
  100.9 9.6 %all_to_all.27.all_ends_ref = f32[8,16,128]{2,1,0:T(8,128)S(1)} all-to-all(f32[8,16,128]{2,1,0:T(8,128)S(1)} %get-tuple-element.35), channel_id=1, replica_groups=mesh['gx'=8,'yz_0'=4,'yz_1'=4,'yz_2'=2] {'gx'}, dimensions={0} | all-to-all | bytes 131072 | tf_op jit(solution)/shard_map/all_to_all | solution.py:528
  110.5 1.7 %update.3 = (f32[128,1024]{1,0:T(8,128)S(1)}, f32[8,1024]{1,0:T(8,128)S(1)}) custom-call(s32[2]{0:T(128)S(1)} %pad_add_fusion.place_ref, f32[128,1024]{1,0:T(8,128)S(1)} %get-tuple-element.34.modes_ref, f32[8,16,128]{2,1,0:T(8,128)S(1)} %all_to_all.27.all_ends_ref, f32[2,128,1024]{2,1,0:T(8,128)S(1)} %get-tuple-element.23.z_ref, ...), custom_call_target="tpu_custom_call" | custom-call | tf_op jit(solution)/shard_map/update/pallas_call | solution.py:454
  112.1 4.6 %collective-permute-start.7 = (f32[128,1024]{1,0:T(8,128)S(1)}, f32[128,1024]{1,0:T(8,128)S(1)}, u32[]{:S(2)}, u32[]{:S(2)}) collective-permute-start(f32[128,1024]{1,0:T(8,128)S(1)} %get-tuple-element.36.value_ref.v_ref), channel_id=1, source_target_pairs={{1,2},{2,1},{3,4},{4,3},{5,6},{6,5},{7,8},{8,7},{9,10},{10,9},{11,... | collective-permute-start | bytes 1572872 | tf_op jit(solution)/shard_map/ppermute | solution.py:482
  116.7 0.1 collective-permute-start.6
  116.8 6.7 %collective-permute-done.7.outer_ref = f32[128,1024]{1,0:T(8,128)S(1)} collective-permute-done((f32[128,1024]{1,0:T(8,128)S(1)}, f32[128,1024]{1,0:T(8,128)S(1)}, u32[]{:S(2)}, u32[]{:S(2)}) %collective-permute-start.7) | collective-permute-done | bytes 524320 | tf_op jit(solution)/shard_map/ppermute | solution.py:482
  123.6 0.0 collective-permute-done.6.partner_ref
  123.6 0.9 sums.1
  124.5 18.5 %all_to_all.28.sums_ref = f32[32,8,128]{2,1,0:T(8,128)S(1)} all-to-all(f32[32,8,128]{2,1,0:T(8,128)S(1)} %get-tuple-element.40), channel_id=1, replica_groups=mesh['gx'=8,'yz_0'=4,'yz_1'=4,'yz_2'=2] {'yz_0','yz_1','yz_2'}, dimensions={0} | all-to-all | bytes 262144 | tf_op jit(solution)/shard_map/all_to_all | solution.py:559
  143.0 9.2 %all_to_all.29.sums_ref = f32[8,8,128]{2,1,0:T(8,128)S(1)} all-to-all(f32[8,8,128]{2,1,0:T(8,128)S(1)} %add.3), channel_id=1, replica_groups=mesh['gx'=8,'yz_0'=4,'yz_1'=4,'yz_2'=2] {'gx'}, dimensions={0} | all-to-all | bytes 65536 | tf_op jit(solution)/shard_map/all_to_all | solution.py:561
  152.2 1.4 final.1
  (1 shorter events, 0.0 us)
Async XLA Ops:
  0.7 0.7 copy-start.9
  6.0 43.8 %copy-start.8 = (s32[1,64]{1,0:T(1,128)S(1)}, s32[1,64]{1,0:T(1,128)}, u32[]{:S(2)}) copy-start(s32[1,64]{1,0:T(1,128)} %param.15) | copy-start | bytes 772
  49.8 19.1 %copy-start = (bf16[2,512,512]{2,1,0:T(8,128)(2,1)S(1)}, bf16[2,512,512]{2,1,0:T(8,128)(2,1)}, u32[]{:S(2)}) copy-start(bf16[2,512,512]{2,1,0:T(8,128)(2,1)} %constant.27.clone.odd_ref) | copy-start | bytes 3145732
  49.8 19.1 %copy-start.1 = (bf16[2,512,512]{2,1,0:T(8,128)(2,1)S(1)}, bf16[2,512,512]{2,1,0:T(8,128)(2,1)}, u32[]{:S(2)}) copy-start(bf16[2,512,512]{2,1,0:T(8,128)(2,1)} %constant.26.clone.even_ref) | copy-start | bytes 3145732
  49.8 19.1 %copy-start.2 = (f32[128,128]{1,0:T(8,128)S(1)}, f32[128,128]{1,0:T(8,128)}, u32[]{:S(2)}) copy-start(f32[128,128]{1,0:T(8,128)} %constant.30.clone.column_ref) | copy-start | bytes 196612
  49.8 19.1 %copy-start.5 = (bf16[256,128]{1,0:T(8,128)(2,1)S(1)}, bf16[256,128]{1,0:T(8,128)(2,1)}, u32[]{:S(2)}) copy-start(bf16[256,128]{1,0:T(8,128)(2,1)} %constant.28.clone.small_ref) | copy-start | bytes 196612
  49.8 19.1 %copy-start.6 = (f32[1,1024]{1,0:T(1,128)S(1)}, f32[1,1024]{1,0:T(1,128)}, u32[]{:S(2)}) copy-start(f32[1,1024]{1,0:T(1,128)} %constant.31.clone.lam_ref) | copy-start | bytes 12292
  52.7 16.1 %collective-permute-start.1 = (f32[2,128,1024]{2,1,0:T(8,128)S(1)}, f32[2,128,1024]{2,1,0:T(8,128)S(1)}, u32[]{:S(2)}, u32[]{:S(2)}) collective-permute-start(f32[2,128,1024]{2,1,0:T(8,128)S(1)} %get-tuple-element.23.z_ref), channel_id=1, source_target_pairs={{1,2},{2,1},{3,4},{4,3},{5,6},{6,5},{7,8},{8,7},{9,10},{10,9},{11,... | collective-permute-start | bytes 3145736 | tf_op jit(solution)/shard_map/ppermute | solution.py:482
  54.7 14.1 %collective-permute-start = (f32[2,128,1024]{2,1,0:T(8,128)S(1)}, f32[2,128,1024]{2,1,0:T(8,128)S(1)}, u32[]{:S(2)}, u32[]{:S(2)}) collective-permute-start(f32[2,128,1024]{2,1,0:T(8,128)S(1)} %get-tuple-element.23.z_ref), channel_id=1, source_target_pairs={{0,1},{1,0},{2,3},{3,2},{4,5},{5,4},{6,7},{7,6},{8,9},{9,8},{10,11... | collective-permute-start | bytes 3145736 | tf_op jit(solution)/shard_map/ppermute | solution.py:483
  54.8 4.9 %collective-permute-start.2 = (f32[2,1024]{1,0:T(2,128)S(1)}, f32[2,1024]{1,0:T(2,128)S(1)}, u32[]{:S(2)}, u32[]{:S(2)}) collective-permute-start(f32[2,1024]{1,0:T(2,128)S(1)} %get-tuple-element.27), channel_id=1, source_target_pairs={{0,32},{32,64},{64,96},{96,128},{128,160},{160,192},{192,224},{1,3... | collective-permute-start | bytes 24584 | tf_op jit(solution)/shard_map/ppermute | solution.py:516
  58.3 4.6 %collective-permute-start.3 = (f32[2,1024]{1,0:T(2,128)S(1)}, f32[2,1024]{1,0:T(2,128)S(1)}, u32[]{:S(2)}, u32[]{:S(2)}) collective-permute-start(f32[2,1024]{1,0:T(2,128)S(1)} %get-tuple-element.28), channel_id=1, source_target_pairs={{32,0},{64,32},{96,64},{128,96},{160,128},{192,160},{224,192},{33,... | collective-permute-start | bytes 24584 | tf_op jit(solution)/shard_map/ppermute | solution.py:517
  68.9 18.2 %copy-start.3 = (f32[7,7,8,128]{3,2,1,0:T(8,128)S(1)}, f32[7,7,8,128]{3,2,1,0:T(8,128)}, u32[]{:S(2)}) copy-start(f32[7,7,8,128]{3,2,1,0:T(8,128)} %constant.32.clone.cut_ref) | copy-start | bytes 602116
  68.9 18.2 %copy-start.4 = (bf16[256,128]{1,0:T(8,128)(2,1)S(1)}, bf16[256,128]{1,0:T(8,128)(2,1)}, u32[]{:S(2)}) copy-start(bf16[256,128]{1,0:T(8,128)(2,1)} %constant.29.clone.small_t_ref) | copy-start | bytes 196612
  68.9 18.2 %copy-start.7 = (f32[2,8,128]{2,1,0:T(8,128)S(1)}, f32[2,8,128]{2,1,0:T(8,128)}, u32[]{:S(2)}) copy-start(f32[2,8,128]{2,1,0:T(8,128)} %constant.33.clone.near_far_ref) | copy-start | bytes 24580
  88.7 10.5 %collective-permute-start.5 = (f32[128,1024]{1,0:T(8,128)S(1)}, f32[128,1024]{1,0:T(8,128)S(1)}, u32[]{:S(2)}, u32[]{:S(2)}) collective-permute-start(f32[128,1024]{1,0:T(8,128)S(1)} %get-tuple-element.31.value_ref.update_ref.u_ref), channel_id=1, source_target_pairs={{1,2},{2,1},{3,4},{4,3},{5,6},{6,5},{7,8},{8,7},{9,10},{10,9},{11,... | collective-permute-start | bytes 1572872 | tf_op jit(solution)/shard_map/ppermute | solution.py:482
  92.2 7.1 %collective-permute-start.4 = (f32[128,1024]{1,0:T(8,128)S(1)}, f32[128,1024]{1,0:T(8,128)S(1)}, u32[]{:S(2)}, u32[]{:S(2)}) collective-permute-start(f32[128,1024]{1,0:T(8,128)S(1)} %get-tuple-element.31.value_ref.update_ref.u_ref), channel_id=1, source_target_pairs={{0,1},{1,0},{2,3},{3,2},{4,5},{5,4},{6,7},{7,6},{8,9},{9,8},{10,11... | collective-permute-start | bytes 1572872 | tf_op jit(solution)/shard_map/ppermute | solution.py:483
  112.1 11.4 %collective-permute-start.7 = (f32[128,1024]{1,0:T(8,128)S(1)}, f32[128,1024]{1,0:T(8,128)S(1)}, u32[]{:S(2)}, u32[]{:S(2)}) collective-permute-start(f32[128,1024]{1,0:T(8,128)S(1)} %get-tuple-element.36.value_ref.v_ref), channel_id=1, source_target_pairs={{1,2},{2,1},{3,4},{4,3},{5,6},{6,5},{7,8},{8,7},{9,10},{10,9},{11,... | collective-permute-start | bytes 1572872 | tf_op jit(solution)/shard_map/ppermute | solution.py:482
  116.7 6.9 %collective-permute-start.6 = (f32[128,1024]{1,0:T(8,128)S(1)}, f32[128,1024]{1,0:T(8,128)S(1)}, u32[]{:S(2)}, u32[]{:S(2)}) collective-permute-start(f32[128,1024]{1,0:T(8,128)S(1)} %get-tuple-element.36.value_ref.v_ref), channel_id=1, source_target_pairs={{0,1},{1,0},{2,3},{3,2},{4,5},{5,4},{6,7},{7,6},{8,9},{9,8},{10,11... | collective-permute-start | bytes 1572872 | tf_op jit(solution)/shard_map/ppermute | solution.py:483

commit v4 on v3

--- a/solution.py
+++ b/solution.py
@@ -20,12 +20,12 @@
 OWNERS = 32
 PER_PAIR = 3
 BRICK_ROWS = 3 * BR
-SIDE_ROW = PER_PAIR * BRICK_ROWS
-END_ROW = SIDE_ROW + BR
+END_ROW = PER_PAIR * BRICK_ROWS
+SIDE_ROW = END_ROW + 2 * PER_PAIR
+ID_ROW = SIDE_ROW + 1
 SEND_ROWS = END_ROW + 8
-ID_LANE = 64
 CHUNKS = 4
-GROUP = 4
+GROUP = 8
 YZ = ("yz_0", "yz_1", "yz_2")
 SHIFT_RATE = 0.05
 FLOOR = 2.0
@@ -156,10 +156,12 @@
 
 
 def pack_kernel(
-    place_ref, slot_ref, accel_hbm, weight_hbm, out_ref,
-    count_ref, held_ref, number_ref, accel_ref, weight_ref, inner_ref, side_ref, sem,
+    place_ref, slot_hbm, accel_hbm, weight_hbm, out_ref,
+    slot_ref, count_ref, held_ref, number_ref, accel_ref, weight_ref, inner_ref, side_ref, sem, slot_sem,
 ):
     del place_ref
+    slot_copy = pltpu.make_async_copy(slot_hbm, slot_ref, slot_sem)
+    slot_copy.start()
     size = PLANE_BRICKS // CHUNKS
     copies = []
     for chunk in range(CHUNKS):
@@ -177,9 +179,10 @@
     for k in range(OWNERS * PER_PAIR):
         held_ref[k] = 0
         number_ref[k] = -1
+    slot_copy.wait()
 
     def assign(s, carry):
-        brick = slot_ref[s]
+        brick = slot_ref[0, s]
         owner = brick // PLANE_BRICKS
         place = count_ref[owner]
         count_ref[owner] = place + 1
@@ -187,33 +190,39 @@
         number_ref[owner * PER_PAIR + place] = brick - owner * PLANE_BRICKS
         return carry
 
-    lax.fori_loop(0, PLANE_BRICKS, assign, 0, unroll=4)
+    lax.fori_loop(0, PLANE_BRICKS, assign, 0, unroll=8)
     dims = (GROUP, BR, B)
     lane = lax.broadcasted_iota(jnp.int32, dims, 2)
     row = lax.broadcasted_iota(jnp.int32, dims, 1)
+    few_lanes, few_rows = lane[0, :8], row[0, :8]
+    edge = jnp.where((few_rows == 0) & (few_lanes == 0), 1.0, 0.0)
+    edge = jnp.where((few_rows == 1) & (few_lanes == B - 1), 1.0, edge)
 
     def inside(group, carry):
         bricks = pl.ds(group * GROUP, GROUP)
-        accel_x, accel_y = accel_ref[bricks, BR : 2 * BR], accel_ref[bricks, 2 * BR :]
-        weight = weight_ref[bricks]
-        flux_x = jnp.sqrt(weight * pltpu.roll(weight, BR - 1, 1)) * (accel_x + pltpu.roll(accel_x, BR - 1, 1))
-        flux_y = jnp.sqrt(weight * pltpu.roll(weight, B - 1, 2)) * (accel_y + pltpu.roll(accel_y, B - 1, 2))
+        root = jnp.sqrt(weight_ref[bricks])
+        weight_ref[bricks] = root
+        accel_x = accel_ref[bricks, BR : 2 * BR]
+        flux_x = root * pltpu.roll(root, BR - 1, 1) * (accel_x + pltpu.roll(accel_x, BR - 1, 1))
         flux_x = jnp.where(row < BR - 1, flux_x, 0.0)
+        inner = pltpu.roll(flux_x, 1, 1) - flux_x
+        accel_y = accel_ref[bricks, 2 * BR :]
+        flux_y = root * pltpu.roll(root, B - 1, 2) * (accel_y + pltpu.roll(accel_y, B - 1, 2))
         flux_y = jnp.where(lane < B - 1, flux_y, 0.0)
-        inner_ref[bricks] = 0.5 * (pltpu.roll(flux_x, 1, 1) - flux_x + pltpu.roll(flux_y, 1, 2) - flux_y)
-        low = jnp.broadcast_to(accel_y[:, :, :1], dims)
-        high = jnp.broadcast_to(accel_y[:, :, B - 1 :], dims)
-        side_ref[bricks] = jnp.where(lane < ID_LANE, low, high)
+        inner_ref[bricks] = 0.5 * (inner + pltpu.roll(flux_y, 1, 2) - flux_y)
+        sides = lax.dot_general(
+            edge, accel_y.reshape(GROUP * BR, B), (((1,), (1,)), ((), ())),
+            precision=lax.Precision.HIGHEST, preferred_element_type=F32,
+        )
+        side_ref[group] = jnp.where(few_rows == 1, pltpu.roll(sides, BR, 1), sides)
         return carry
 
     for chunk in range(CHUNKS):
         for copy in copies[chunk]:
             copy.wait()
-        lax.fori_loop(chunk * size // GROUP, (chunk + 1) * size // GROUP, inside, 0)
-    lane, row = lane[0], row[0, :8]
+        lax.fori_loop(chunk * size // GROUP, (chunk + 1) * size // GROUP, inside, 0, unroll=2)
 
     def fill(owner, carry):
-        sides = jnp.zeros((BR, B), F32)
         ends = jnp.zeros((8, B), F32)
         for place in range(PER_PAIR):
             s = held_ref[owner * PER_PAIR + place]
@@ -222,33 +231,34 @@
             out_ref[owner, at : at + BR] = accel_ref[s, :BR]
             out_ref[owner, at + BR : at + 2 * BR] = inner_ref[s]
             out_ref[owner, at + 2 * BR : at + 3 * BR] = weight_ref[s]
-            sides = jnp.where((lane == place) | (lane == B - 1 - place), side_ref[s], sides)
-            sides = jnp.where(lane == ID_LANE + place, number, sides)
-            ends = jnp.where(row == 2 * place, accel_ref[s, BR : BR + 1], ends)
-            ends = jnp.where(row == 2 * place + 1, accel_ref[s, 2 * BR - 1 : 2 * BR], ends)
-        out_ref[owner, SIDE_ROW:END_ROW] = sides
+            ends = jnp.where(few_rows == 2 * place, accel_ref[s, BR : BR + 1], ends)
+            ends = jnp.where(few_rows == 2 * place + 1, accel_ref[s, 2 * BR - 1 : 2 * BR], ends)
+            sides = pltpu.roll(side_ref[s // GROUP], (B + 2 * BR * place - BR * (s % GROUP)) % B, 1)
+            sides = jnp.where(few_lanes < 2 * BR * place + BR, sides[0:1], sides[1:2])
+            ends = jnp.where((few_rows == SIDE_ROW - END_ROW) & (few_lanes >= 2 * BR * place), sides, ends)
+            ends = jnp.where((few_rows == ID_ROW - END_ROW) & (few_lanes == place), number, ends)
         out_ref[owner, END_ROW:] = ends
         return carry
 
-    lax.fori_loop(0, OWNERS, fill, 0, unroll=2)
+    lax.fori_loop(0, OWNERS, fill, 0, unroll=4)
 
 
 def place_kernel(
     solid_ref, got_ref, z_ref, source_ref, ends_ref, sides_ref, first_ref, last_ref, ids_ref, from_ref, sem
 ):
-    ids_copy = pltpu.make_async_copy(got_ref.at[:, pl.ds(SIDE_ROW, 1)], ids_ref, sem)
+    ids_copy = pltpu.make_async_copy(got_ref.at[:, pl.ds(ID_ROW, 1)], ids_ref, sem)
     ids_copy.start()
     ids_copy.wait()
-    first_lane = lax.broadcasted_iota(jnp.int32, (BR, B), 1) == 0
-    upper_half = lax.broadcasted_iota(jnp.int32, (BR, B), 0) < BR // 2
+    lane = lax.broadcasted_iota(jnp.int32, (BR, B), 1)
+    row = lax.broadcasted_iota(jnp.int32, (BR, B), 0)
 
     def find(source, carry):
         for place in range(PER_PAIR):
-            brick = ids_ref[source, 0, ID_LANE + place].astype(jnp.int32)
+            brick = ids_ref[source, 0, place].astype(jnp.int32)
             from_ref[jnp.where(brick < 0, PLANE_BRICKS, brick)] = source * 4 + place
         return carry
 
-    lax.fori_loop(0, OWNERS, find, 0, unroll=2)
+    lax.fori_loop(0, OWNERS, find, 0, unroll=4)
 
     def line(x, carry):
         rows = pl.ds(pl.multiple_of(x * BR, BR), BR)
@@ -260,13 +270,14 @@
             z_ref[0, rows, cols] = got_ref[source, pl.ds(at, BR)]
             source_ref[rows, cols] = got_ref[source, pl.ds(at + BR, BR)] * fluid
             z_ref[1, rows, cols] = got_ref[source, pl.ds(at + 2 * BR, BR)] * fluid
-            sides = got_ref[source, SIDE_ROW:END_ROW]
-            low = pltpu.roll(sides, (B - place) % B, 1)
-            high = pltpu.roll(sides, place, 1)
-            sides_ref[rows, cols] = jnp.where(first_lane, low, high)
+            sides = jnp.broadcast_to(got_ref[source, SIDE_ROW : SIDE_ROW + 1], (BR, B))
+            own = lane - row - 2 * BR * place
+            low = jnp.sum(jnp.where(own == 0, sides, 0.0), axis=1, keepdims=True)
+            high = jnp.sum(jnp.where(own == BR, sides, 0.0), axis=1, keepdims=True)
+            sides_ref[rows, cols] = jnp.where(lane == 0, low, high)
             first = got_ref[source, pl.ds(END_ROW + 2 * place, 1)]
             last = got_ref[source, pl.ds(END_ROW + 1 + 2 * place, 1)]
-            ends_ref[rows, cols] = jnp.where(upper_half, first, last)
+            ends_ref[rows, cols] = jnp.where(row < BR // 2, first, last)
         return carry
 
     lax.fori_loop(0, XL // BR, line, 0)
@@ -278,39 +289,29 @@
 def setup_kernel(
     place_ref, z_ref, inner_ref, x_ends_ref, sides_ref, partner_ref, outer_ref, xlo_ref, xhi_ref,
     even_ref, odd_ref, small_ref, column_ref, lam_ref,
-    faces_ref, source_ref, modes_ref, ends_ref, wext_ref, fold_ref,
+    diagonal_ref, source_ref, modes_ref, ends_ref, ext_ref, fold_ref,
 ):
-    wext_ref[7:8] = xlo_ref[0:1]
-    wext_ref[XL + 8 : XL + 9] = xhi_ref[0:1]
-    wext_ref[8 : XL + 8] = z_ref[1]
+    ext_ref[7:8] = xlo_ref[0:1]
+    ext_ref[XL + 8 : XL + 9] = xhi_ref[0:1]
+    ext_ref[8 : XL + 8] = z_ref[1]
     lane = lax.broadcasted_iota(jnp.int32, (8, N), 1)
-    inside = lane < N - 1
-    brick_end = lane % B == B - 1
+    brick_end = (lane % B == B - 1) & (lane < N - 1)
     sign = (2 * place_ref[1] - 1).astype(F32)
     for i in range(XL // 8):
         rows = pl.ds(8 * i, 8)
-        accel_z = z_ref[0, rows]
-        weight = z_ref[1, rows]
-        side = sides_ref[rows]
-        face_p = jnp.sqrt(weight * partner_ref[1, rows])
-        face_o = jnp.sqrt(weight * outer_ref[1, rows])
-        face_xp = jnp.sqrt(weight * wext_ref[pl.ds(8 * i + 9, 8)])
-        face_xm = jnp.sqrt(weight * wext_ref[pl.ds(8 * i + 7, 8)])
-        face_yp = jnp.where(inside, jnp.sqrt(weight * pltpu.roll(weight, N - 1, 1)), 0.0)
-        face_ym = pltpu.roll(face_yp, 1, 1)
-        diagonal = SHIFT_RATE * weight + jnp.where(weight > 0.0, 0.0, 1.0)
-        diagonal = diagonal + face_p + face_o + face_xp + face_xm + face_yp + face_ym
-        flux = face_p * (partner_ref[0, rows] + accel_z) - face_o * (accel_z + outer_ref[0, rows])
-        flux_y = jnp.where(brick_end, face_yp * (side + pltpu.roll(side, N - 1, 1)), 0.0)
-        flux = sign * flux + pltpu.roll(flux_y, 1, 1) - flux_y
-        source_ref[rows] = inner_ref[rows] + 0.5 * flux
-        for k, face in enumerate((face_p, face_o, face_xp, face_xm, face_yp, face_ym, diagonal)):
-            faces_ref[k, rows] = face
+        accel_z, root, side = z_ref[0, rows], z_ref[1, rows], sides_ref[rows]
+        root_p, root_o = partner_ref[1, rows], outer_ref[1, rows]
+        after = pltpu.roll(root, N - 1, 1)
+        beside = root_p + root_o + ext_ref[pl.ds(8 * i + 9, 8)] + ext_ref[pl.ds(8 * i + 7, 8)]
+        beside = beside + jnp.where(lane < N - 1, after, 0.0) + jnp.where(lane > 0, pltpu.roll(root, 1, 1), 0.0)
+        diagonal_ref[rows] = root * (SHIFT_RATE * root + beside) + jnp.where(root > 0.0, 0.0, 1.0)
+        flux = sign * (root_p * (partner_ref[0, rows] + accel_z) - root_o * (accel_z + outer_ref[0, rows]))
+        flux_y = jnp.where(brick_end, root * after * (side + pltpu.roll(side, N - 1, 1)), 0.0)
+        source_ref[rows] = inner_ref[rows] + 0.5 * (root * flux + pltpu.roll(flux_y, 1, 1) - flux_y)
     for x in range(0, XL + 1, BR):
-        face = faces_ref[3, x : x + 1] if x < XL else faces_ref[2, x - 1 : x]
         before = x_ends_ref[x - 1 : x] if x > 0 else xlo_ref[1:2]
         after = x_ends_ref[x : x + 1] if x < XL else xhi_ref[1:2]
-        flux = 0.5 * face * (before + after)
+        flux = 0.5 * ext_ref[x + 7 : x + 8] * ext_ref[x + 8 : x + 9] * (before + after)
         if x > 0:
             source_ref[x - 1 : x] = source_ref[x - 1 : x] - flux
         if x < XL:
@@ -319,8 +320,8 @@
 
 
 def update_kernel(
-    place_ref, modes_ref, all_ends_ref, z_ref, cut_ref, near_far_ref, even_ref, odd_ref, small_t_ref,
-    column_ref, lam_ref, update_ref, rim_ref, work_ref,
+    place_ref, modes_ref, all_ends_ref, z_ref, xlo_ref, xhi_ref, cut_ref, near_far_ref, even_ref, odd_ref,
+    small_t_ref, column_ref, lam_ref, update_ref, scaled_ref, rim_ref, work_ref,
 ):
     slab = place_ref[0]
 
@@ -354,46 +355,51 @@
         odd = work_ref[rows, H:]
         value = jnp.concatenate([even + odd, mirrored(even - odd)], axis=1)
         if i < XL // 8:
-            update_ref[rows] = jnp.where(z_ref[1, rows] > 0.0, value, 0.0)
+            root = z_ref[1, rows]
+            update_ref[rows] = jnp.where(root > 0.0, value, 0.0)
+            scaled_ref[rows] = root * value
         else:
-            rim_ref[...] = value
-
-
-def image_rows(i, value_ref, partner_ref, outer_ref, faces_ref, ext_ref):
+            rim_ref[0:1] = value[0:1] * xlo_ref[0:1]
+            rim_ref[1:2] = value[1:2] * xhi_ref[0:1]
+
+
+def image_rows(i, value_ref, scaled_ref, partner_ref, outer_ref, z_ref, diagonal_ref, ext_ref):
     rows = pl.ds(8 * i, 8)
-    value = value_ref[rows]
-    image = faces_ref[6, rows] * value
-    image = image - (faces_ref[0, rows] * partner_ref[rows] + faces_ref[1, rows] * outer_ref[rows])
-    image = image - (faces_ref[2, rows] * ext_ref[pl.ds(8 * i + 9, 8)] + faces_ref[3, rows] * ext_ref[pl.ds(8 * i + 7, 8)])
-    image = image - (faces_ref[4, rows] * pltpu.roll(value, N - 1, 1) + faces_ref[5, rows] * pltpu.roll(value, 1, 1))
-    return value, image
-
-
-def extend(value_ref, rim_ref, ext_ref):
+    value, scaled = value_ref[rows], scaled_ref[rows]
+    lane = lax.broadcasted_iota(jnp.int32, (8, N), 1)
+    beside = partner_ref[rows] + outer_ref[rows] + ext_ref[pl.ds(8 * i + 9, 8)] + ext_ref[pl.ds(8 * i + 7, 8)]
+    beside = beside + jnp.where(lane < N - 1, pltpu.roll(scaled, N - 1, 1), 0.0)
+    beside = beside + jnp.where(lane > 0, pltpu.roll(scaled, 1, 1), 0.0)
+    return value, diagonal_ref[rows] * value - z_ref[1, rows] * beside
+
+
+def extend(scaled_ref, rim_ref, ext_ref):
     ext_ref[7:8] = rim_ref[0:1]
     ext_ref[XL + 8 : XL + 9] = rim_ref[1:2]
-    ext_ref[8 : XL + 8] = value_ref[...]
+    ext_ref[8 : XL + 8] = scaled_ref[...]
 
 
 def image_kernel(
-    value_ref, rim_ref, partner_ref, outer_ref, faces_ref, even_ref, odd_ref, small_ref, column_ref, lam_ref,
+    value_ref, scaled_ref, rim_ref, partner_ref, outer_ref, z_ref, diagonal_ref,
+    even_ref, odd_ref, small_ref, column_ref, lam_ref,
     image_ref, modes_ref, ends_ref, ext_ref, fold_ref,
 ):
-    extend(value_ref, rim_ref, ext_ref)
-    for i in range(XL // 8):
-        image_ref[pl.ds(8 * i, 8)] = image_rows(i, value_ref, partner_ref, outer_ref, faces_ref, ext_ref)[1]
+    extend(scaled_ref, rim_ref, ext_ref)
+    for i in range(XL // 8):
+        _, image = image_rows(i, value_ref, scaled_ref, partner_ref, outer_ref, z_ref, diagonal_ref, ext_ref)
+        image_ref[pl.ds(8 * i, 8)] = image
     to_modes(image_ref, even_ref, odd_ref, small_ref, column_ref, lam_ref, fold_ref, modes_ref, ends_ref)
 
 
 def sums_kernel(
-    value_ref, rim_ref, partner_ref, outer_ref, faces_ref, source_ref, update_ref, first_image_ref,
-    image_ref, sums_ref, ext_ref,
+    value_ref, scaled_ref, rim_ref, partner_ref, outer_ref, z_ref, diagonal_ref, source_ref, update_ref,
+    first_image_ref, image_ref, sums_ref, ext_ref,
 ):
-    extend(value_ref, rim_ref, ext_ref)
+    extend(scaled_ref, rim_ref, ext_ref)
     totals = [jnp.zeros((8, N), F32) for _ in range(6)]
     for i in range(XL // 8):
         rows = pl.ds(8 * i, 8)
-        v, t = image_rows(i, value_ref, partner_ref, outer_ref, faces_ref, ext_ref)
+        v, t = image_rows(i, value_ref, scaled_ref, partner_ref, outer_ref, z_ref, diagonal_ref, ext_ref)
         image_ref[rows] = t
         r, u, q = source_ref[rows], update_ref[rows], first_image_ref[rows]
         for k, (a, b) in enumerate(((r, u), (u, q), (r, v), (q, v), (u, t), (v, t))):
@@ -485,20 +491,22 @@
     send = call(
         pack_kernel,
         shape(OWNERS, SEND_ROWS, 128),
-        [SMEM, SMEM, HBM, HBM],
+        [SMEM, HBM, HBM, HBM],
         VMEM,
         [
+            pltpu.SMEM((1, PLANE_BRICKS), jnp.int32),
             pltpu.SMEM((OWNERS,), jnp.int32),
             pltpu.SMEM((OWNERS * PER_PAIR,), jnp.int32),
             pltpu.SMEM((OWNERS * PER_PAIR,), jnp.int32),
             pltpu.VMEM((PLANE_BRICKS, 3 * BR, B), F32),
             pltpu.VMEM((PLANE_BRICKS, BR, B), F32),
             pltpu.VMEM((PLANE_BRICKS, BR, B), F32),
-            pltpu.VMEM((PLANE_BRICKS, BR, B), F32),
+            pltpu.VMEM((PLANE_BRICKS // GROUP, 8, B), F32),
             pltpu.SemaphoreType.DMA((2, CHUNKS)),
+            pltpu.SemaphoreType.DMA,
         ],
         name="pack",
-    )(place, brick_slot[0], camera_accel[0].reshape(PLANE_BRICKS, 3 * BR, B), camera_weight[0])
+    )(place, brick_slot, camera_accel[0].reshape(PLANE_BRICKS, 3 * BR, B), camera_weight[0])
     got = lax.all_to_all(send, YZ, split_axis=0, concat_axis=0, tiled=True)
     z_fields, inner, x_ends, sides, first, last = call(
         place_kernel,
@@ -515,9 +523,9 @@
     partner, outer = neighbours(z_fields)
     xlo = lax.ppermute(last, "gx", up_x)
     xhi = lax.ppermute(first, "gx", down_x)
-    faces, source, modes, ends = call(
+    diagonal, source, modes, ends = call(
         setup_kernel,
-        (shape(7, *PLANE), shape(*PLANE), shape(*PLANE), shape(SLABS, 16, 128)),
+        (shape(*PLANE), shape(*PLANE), shape(*PLANE), shape(SLABS, 16, 128)),
         [SMEM] + [VMEM] * 13,
         (VMEM,) * 4,
         [EXT, FOLD],
@@ -528,34 +536,34 @@
         all_ends = lax.all_to_all(ends, "gx", split_axis=0, concat_axis=0, tiled=True)
         return call(
             update_kernel,
-            (shape(*PLANE), shape(8, N)),
-            [SMEM] + [VMEM] * 10,
-            (VMEM, VMEM),
+            (shape(*PLANE), shape(*PLANE), shape(2, N)),
+            [SMEM] + [VMEM] * 12,
+            (VMEM,) * 3,
             [pltpu.VMEM((XL + 8, N), F32)],
             name="update",
         )(
-            place, modes, all_ends, z_fields, constant["cut"], constant["ends"],
+            place, modes, all_ends, z_fields, xlo, xhi, constant["cut"], constant["ends"],
             *dct, constant["small_t"], *slab_tables,
         )
 
-    u, rim = updated(modes, ends)
+    u, scaled, rim = updated(modes, ends)
     q, modes, ends = call(
         image_kernel,
         (shape(*PLANE), shape(*PLANE), shape(SLABS, 16, 128)),
-        [VMEM] * 10,
+        [VMEM] * 12,
         (VMEM,) * 3,
         [EXT, FOLD],
         name="image",
-    )(u, rim, *neighbours(u), faces, *forward)
-    v, rim = updated(modes, ends)
+    )(u, scaled, rim, *neighbours(scaled), z_fields, diagonal, *forward)
+    v, scaled, rim = updated(modes, ends)
     t, sums = call(
         sums_kernel,
         (shape(*PLANE), shape(OWNERS, 8, 128)),
-        [VMEM] * 8,
+        [VMEM] * 10,
         (VMEM, VMEM),
         [EXT],
         name="sums",
-    )(v, rim, *neighbours(v), faces, source, u, q)
+    )(v, scaled, rim, *neighbours(scaled), z_fields, diagonal, source, u, q)
     sums = lax.all_to_all(sums, YZ, split_axis=0, concat_axis=0, tiled=True)
     sums = call(add_kernel, shape(SLABS, 8, 128), [VMEM], VMEM, name="add")(sums)
     sums = lax.all_to_all(sums, "gx", split_axis=0, concat_axis=0, tiled=True)

time: 154 us -> 150 us (0.974)
  blocking collectives: 96.3 us -> 93.6 us
    all_to_all x1, blocking collectives: 43.8 us -> 41.1 us  [on_device(): got = lax.all_to_all(send, YZ, split_axis=0, concat_axis=0, tiled=True)]
where the time goes in v4:
time: 150 us
  blocking collectives  93.6 us (62%)
  waiting for transfers between devices  23 us (15%)
  Pallas kernels  17.5 us (12%)
  starting transfers between devices  15 us (10%)
    all_to_all x1, blocking collectives, on_device(): got = lax.all_to_all(send, YZ, split_axis=0, concat_axis=0, tiled=True)  41.1 us
    all_to_all x2, blocking collectives, updated(): lax.all_to_all(ends, 'gx', split_axis=0, concat_axis=0, tiled=True)  24.8 us
    ppermute x3, waiting for transfers between devices, neighbours(): outer = lax.ppermute(value, YZ, off_chip)  19.7 us
    all_to_all x1, blocking collectives, on_device(): sums = lax.all_to_all(sums, YZ, split_axis=0, concat_axis=0, tiled=True)  18.4 us
    pallas_call x9, Pallas kernels, with_spaces(): run(*(x if spec is SMEM else pltpu.with_memory_space_constraint(x, spec.m...  17.5 us
    ppermute x3, starting transfers between devices, neighbours(): outer = lax.ppermute(value, YZ, off_chip)  9.93 us
    all_to_all x1, blocking collectives, on_device(): sums = lax.all_to_all(sums, 'gx', split_axis=0, concat_axis=0, tiled=True)  9.24 us
    ppermute x1, starting transfers between devices, on_device(): xlo = lax.ppermute(last, 'gx', up_x)  3.54 us
  transfers between devices with their start and end apart: 8, of which 4 were waited for; matrix products, arithmetic and copies ran while one was open for 0% of the time, Pallas kernels for 0%

profile of v4, /device:TPU:1, one launch (start us, length us, event | category | flops | bytes accessed | tf_op | source)
XLA Modules:
  0.0 150.0 jit_solution(2495268801256271337)
XLA Ops:
  0.6 0.1 pad_add_fusion.place_ref
  0.7 5.0 %pack.1 = f32[32,152,128]{2,1,0:T(8,128)S(1)} custom-call(s32[2]{0:T(128)S(1)} %pad_add_fusion.place_ref, s32[1,64]{1,0:T(1,128)} %slot_hbm.1, f32[64,48,128]{2,1,0:T(8,128)} %bitcast.8, f32[64,16,128]{2,1,0:T(8,128)} %bitcast.9), custom_call_target="tpu_custom_call" | custom-call | tf_op jit(solution)/shard_map/pack/pallas_call | solution.py:460
  5.7 0.0 copy-start.8
  5.7 41.1 %all_to_all.25.got_ref = f32[32,152,128]{2,1,0:T(8,128)S(1)} all-to-all(f32[32,152,128]{2,1,0:T(8,128)S(1)} %pack.1), channel_id=1, replica_groups=mesh['gx'=8,'yz_0'=4,'yz_1'=4,'yz_2'=2] {'yz_0','yz_1','yz_2'}, dimensions={0} | all-to-all | bytes 4980736 | tf_op jit(solution)/shard_map/all_to_all | solution.py:510
  46.8 0.0 copy-start
  46.8 0.0 copy-start.1
  46.8 0.0 copy-start.2
  46.8 0.0 copy-start.5
  46.8 0.0 copy-start.6
  46.8 0.0 copy-done.8
  46.9 2.8 %place.1 = (f32[2,128,1024]{2,1,0:T(8,128)S(1)}, f32[128,1024]{1,0:T(8,128)S(1)}, f32[128,1024]{1,0:T(8,128)S(1)}, f32[128,1024]{1,0:T(8,128)S(1)}, f32[2,1024]{1,0:T(2,128)S(1)}, /*index=5*/f32[2,1024]{1,0:T(2,128)S(1)}) custom-call(s32[64]{0:T(128)S(1)} %bitcast.7, f32[32,152,128]{2,1,0:T(8,128)S(1)} %all_to_all.25.got_ref), custom_call_target="tpu_custom_call" | custom-call | tf_op jit(solution)/shard_map/place/pallas_call | solution.py:460
  49.7 1.9 %collective-permute-start.1 = (f32[2,128,1024]{2,1,0:T(8,128)S(1)}, f32[2,128,1024]{2,1,0:T(8,128)S(1)}, u32[]{:S(2)}, u32[]{:S(2)}) collective-permute-start(f32[2,128,1024]{2,1,0:T(8,128)S(1)} %get-tuple-element.25.z_ref), channel_id=1, source_target_pairs={{1,2},{2,1},{3,4},{4,3},{5,6},{6,5},{7,8},{8,7},{9,10},{10,9},{11,... | collective-permute-start | bytes 3145736 | tf_op jit(solution)/shard_map/ppermute | solution.py:488
  51.6 0.1 collective-permute-start
  51.7 3.5 %collective-permute-start.2 = (f32[2,1024]{1,0:T(2,128)S(1)}, f32[2,1024]{1,0:T(2,128)S(1)}, u32[]{:S(2)}, u32[]{:S(2)}) collective-permute-start(f32[2,1024]{1,0:T(2,128)S(1)} %get-tuple-element.29), channel_id=1, source_target_pairs={{0,32},{32,64},{64,96},{96,128},{128,160},{160,192},{192,224},{1,3... | collective-permute-start | bytes 24584 | tf_op jit(solution)/shard_map/ppermute | solution.py:524
  55.3 1.3 collective-permute-start.3
  56.6 0.0 collective-permute-done.2.xlo_ref
  56.6 3.3 %collective-permute-done.3.xhi_ref = f32[2,1024]{1,0:T(2,128)S(1)} collective-permute-done((f32[2,1024]{1,0:T(2,128)S(1)}, f32[2,1024]{1,0:T(2,128)S(1)}, u32[]{:S(2)}, u32[]{:S(2)}) %collective-permute-start.3) | collective-permute-done | bytes 8224 | tf_op jit(solution)/shard_map/ppermute | solution.py:525
  59.8 6.0 %collective-permute-done.1.outer_ref = f32[2,128,1024]{2,1,0:T(8,128)S(1)} collective-permute-done((f32[2,128,1024]{2,1,0:T(8,128)S(1)}, f32[2,128,1024]{2,1,0:T(8,128)S(1)}, u32[]{:S(2)}, u32[]{:S(2)}) %collective-permute-start.1) | collective-permute-done | bytes 1048608 | tf_op jit(solution)/shard_map/ppermute | solution.py:488
  65.8 0.0 collective-permute-done.partner_ref
  65.8 0.0 copy-done
  65.8 0.0 copy-done.1
  65.8 0.0 copy-done.2
  65.8 0.0 copy-done.5
  65.8 0.0 copy-done.6
  65.8 0.0 copy-start.3
  65.8 0.0 copy-start.4
  65.9 0.0 copy-start.7
  65.9 2.6 %setup.1 = (f32[128,1024]{1,0:T(8,128)S(1)}, f32[128,1024]{1,0:T(8,128)S(1)}, f32[128,1024]{1,0:T(8,128)S(1)}, f32[8,16,128]{2,1,0:T(8,128)S(1)}) custom-call(s32[2]{0:T(128)S(1)} %pad_add_fusion.place_ref, f32[2,128,1024]{2,1,0:T(8,128)S(1)} %get-tuple-element.25.z_ref, f32[128,1024]{1,0:T(8,128)S(1)} %get-tuple-element.26.inner_ref, ...), custom_call_target="tpu_custom_call" | custom-call | tf_op jit(solution)/shard_map/setup/pallas_call | solution.py:460
  68.5 15.2 %all_to_all.26.all_ends_ref = f32[8,16,128]{2,1,0:T(8,128)S(1)} all-to-all(f32[8,16,128]{2,1,0:T(8,128)S(1)} %get-tuple-element.32), channel_id=1, replica_groups=mesh['gx'=8,'yz_0'=4,'yz_1'=4,'yz_2'=2] {'gx'}, dimensions={0} | all-to-all | bytes 131072 | tf_op jit(solution)/shard_map/all_to_all | solution.py:536
  83.7 0.0 copy-done.3
  83.7 0.0 copy-done.4
  83.7 0.0 copy-done.7
  83.7 1.7 %update.2 = (f32[128,1024]{1,0:T(8,128)S(1)}, f32[128,1024]{1,0:T(8,128)S(1)}, f32[2,1024]{1,0:T(2,128)S(1)}) custom-call(s32[2]{0:T(128)S(1)} %pad_add_fusion.place_ref, f32[128,1024]{1,0:T(8,128)S(1)} %get-tuple-element.31.modes_ref, f32[8,16,128]{2,1,0:T(8,128)S(1)} %all_to_all.26.all_ends_ref, f32[2,128,1024]{2,1,0:T(8,128)S(1)} %get-tuple-element.25.z_ref, ...), custom_call_target="tpu_custom_call" | custom-call | tf_op jit(solution)/shard_map/update/pallas_call | solution.py:460
  85.4 3.4 %collective-permute-start.5 = (f32[128,1024]{1,0:T(8,128)S(1)}, f32[128,1024]{1,0:T(8,128)S(1)}, u32[]{:S(2)}, u32[]{:S(2)}) collective-permute-start(f32[128,1024]{1,0:T(8,128)S(1)} %get-tuple-element.34.scaled_ref), channel_id=1, source_target_pairs={{1,2},{2,1},{3,4},{4,3},{5,6},{6,5},{7,8},{8,7},{9,10},{10,9},{11,... | collective-permute-start | bytes 1572872 | tf_op jit(solution)/shard_map/ppermute | solution.py:488
  88.9 0.1 collective-permute-start.4
  89.0 7.0 %collective-permute-done.5.outer_ref = f32[128,1024]{1,0:T(8,128)S(1)} collective-permute-done((f32[128,1024]{1,0:T(8,128)S(1)}, f32[128,1024]{1,0:T(8,128)S(1)}, u32[]{:S(2)}, u32[]{:S(2)}) %collective-permute-start.5) | collective-permute-done | bytes 524320 | tf_op jit(solution)/shard_map/ppermute | solution.py:488
  95.9 0.0 collective-permute-done.4.partner_ref
  95.9 1.5 %image.1 = (f32[128,1024]{1,0:T(8,128)S(1)}, f32[128,1024]{1,0:T(8,128)S(1)}, f32[8,16,128]{2,1,0:T(8,128)S(1)}) custom-call(f32[128,1024]{1,0:T(8,128)S(1)} %get-tuple-element.33.value_ref.update_ref.u_ref, f32[128,1024]{1,0:T(8,128)S(1)} %get-tuple-element.34.scaled_ref, f32[2,1024]{1,0:T(2,128)S(1)} %get-tuple-element.35.rim_ref, ...), custom_call_target="tpu_custom_call" | custom-call | tf_op jit(solution)/shard_map/image/pallas_call | solution.py:460
  97.5 9.6 %all_to_all.27.all_ends_ref = f32[8,16,128]{2,1,0:T(8,128)S(1)} all-to-all(f32[8,16,128]{2,1,0:T(8,128)S(1)} %get-tuple-element.38), channel_id=1, replica_groups=mesh['gx'=8,'yz_0'=4,'yz_1'=4,'yz_2'=2] {'gx'}, dimensions={0} | all-to-all | bytes 131072 | tf_op jit(solution)/shard_map/all_to_all | solution.py:536
  107.1 1.7 %update.3 = (f32[128,1024]{1,0:T(8,128)S(1)}, f32[128,1024]{1,0:T(8,128)S(1)}, f32[2,1024]{1,0:T(2,128)S(1)}) custom-call(s32[2]{0:T(128)S(1)} %pad_add_fusion.place_ref, f32[128,1024]{1,0:T(8,128)S(1)} %get-tuple-element.37.modes_ref, f32[8,16,128]{2,1,0:T(8,128)S(1)} %all_to_all.27.all_ends_ref, f32[2,128,1024]{2,1,0:T(8,128)S(1)} %get-tuple-element.25.z_ref, ...), custom_call_target="tpu_custom_call" | custom-call | tf_op jit(solution)/shard_map/update/pallas_call | solution.py:460
  108.8 4.6 %collective-permute-start.7 = (f32[128,1024]{1,0:T(8,128)S(1)}, f32[128,1024]{1,0:T(8,128)S(1)}, u32[]{:S(2)}, u32[]{:S(2)}) collective-permute-start(f32[128,1024]{1,0:T(8,128)S(1)} %get-tuple-element.40.scaled_ref), channel_id=1, source_target_pairs={{1,2},{2,1},{3,4},{4,3},{5,6},{6,5},{7,8},{8,7},{9,10},{10,9},{11,... | collective-permute-start | bytes 1572872 | tf_op jit(solution)/shard_map/ppermute | solution.py:488
  113.4 0.1 collective-permute-start.6
  113.5 6.7 %collective-permute-done.7.outer_ref = f32[128,1024]{1,0:T(8,128)S(1)} collective-permute-done((f32[128,1024]{1,0:T(8,128)S(1)}, f32[128,1024]{1,0:T(8,128)S(1)}, u32[]{:S(2)}, u32[]{:S(2)}) %collective-permute-start.7) | collective-permute-done | bytes 524320 | tf_op jit(solution)/shard_map/ppermute | solution.py:488
  120.2 0.0 collective-permute-done.6.partner_ref
  120.2 0.8 sums.1
  121.0 18.4 %all_to_all.28.sums_ref = f32[32,8,128]{2,1,0:T(8,128)S(1)} all-to-all(f32[32,8,128]{2,1,0:T(8,128)S(1)} %get-tuple-element.44), channel_id=1, replica_groups=mesh['gx'=8,'yz_0'=4,'yz_1'=4,'yz_2'=2] {'yz_0','yz_1','yz_2'}, dimensions={0} | all-to-all | bytes 262144 | tf_op jit(solution)/shard_map/all_to_all | solution.py:567
  139.4 9.2 %all_to_all.29.sums_ref = f32[8,8,128]{2,1,0:T(8,128)S(1)} all-to-all(f32[8,8,128]{2,1,0:T(8,128)S(1)} %add.3), channel_id=1, replica_groups=mesh['gx'=8,'yz_0'=4,'yz_1'=4,'yz_2'=2] {'gx'}, dimensions={0} | all-to-all | bytes 65536 | tf_op jit(solution)/shard_map/all_to_all | solution.py:569
  148.6 1.4 final.1
  (1 shorter events, 0.0 us)
Async XLA Ops:
  5.7 41.2 %copy-start.8 = (s32[1,64]{1,0:T(1,128)S(1)}, s32[1,64]{1,0:T(1,128)}, u32[]{:S(2)}) copy-start(s32[1,64]{1,0:T(1,128)} %param.15) | copy-start | bytes 772
  46.8 19.0 %copy-start = (bf16[2,512,512]{2,1,0:T(8,128)(2,1)S(1)}, bf16[2,512,512]{2,1,0:T(8,128)(2,1)}, u32[]{:S(2)}) copy-start(bf16[2,512,512]{2,1,0:T(8,128)(2,1)} %constant.27.clone.odd_ref) | copy-start | bytes 3145732
  46.8 19.0 %copy-start.1 = (bf16[2,512,512]{2,1,0:T(8,128)(2,1)S(1)}, bf16[2,512,512]{2,1,0:T(8,128)(2,1)}, u32[]{:S(2)}) copy-start(bf16[2,512,512]{2,1,0:T(8,128)(2,1)} %constant.26.clone.even_ref) | copy-start | bytes 3145732
  46.8 19.0 %copy-start.2 = (f32[128,128]{1,0:T(8,128)S(1)}, f32[128,128]{1,0:T(8,128)}, u32[]{:S(2)}) copy-start(f32[128,128]{1,0:T(8,128)} %constant.30.clone.column_ref) | copy-start | bytes 196612
  46.8 19.0 %copy-start.5 = (bf16[256,128]{1,0:T(8,128)(2,1)S(1)}, bf16[256,128]{1,0:T(8,128)(2,1)}, u32[]{:S(2)}) copy-start(bf16[256,128]{1,0:T(8,128)(2,1)} %constant.28.clone.small_ref) | copy-start | bytes 196612
  46.8 19.0 %copy-start.6 = (f32[1,1024]{1,0:T(1,128)S(1)}, f32[1,1024]{1,0:T(1,128)}, u32[]{:S(2)}) copy-start(f32[1,1024]{1,0:T(1,128)} %constant.31.clone.lam_ref) | copy-start | bytes 12292
  49.7 16.1 %collective-permute-start.1 = (f32[2,128,1024]{2,1,0:T(8,128)S(1)}, f32[2,128,1024]{2,1,0:T(8,128)S(1)}, u32[]{:S(2)}, u32[]{:S(2)}) collective-permute-start(f32[2,128,1024]{2,1,0:T(8,128)S(1)} %get-tuple-element.25.z_ref), channel_id=1, source_target_pairs={{1,2},{2,1},{3,4},{4,3},{5,6},{6,5},{7,8},{8,7},{9,10},{10,9},{11,... | collective-permute-start | bytes 3145736 | tf_op jit(solution)/shard_map/ppermute | solution.py:488
  51.6 14.2 %collective-permute-start = (f32[2,128,1024]{2,1,0:T(8,128)S(1)}, f32[2,128,1024]{2,1,0:T(8,128)S(1)}, u32[]{:S(2)}, u32[]{:S(2)}) collective-permute-start(f32[2,128,1024]{2,1,0:T(8,128)S(1)} %get-tuple-element.25.z_ref), channel_id=1, source_target_pairs={{0,1},{1,0},{2,3},{3,2},{4,5},{5,4},{6,7},{7,6},{8,9},{9,8},{10,11... | collective-permute-start | bytes 3145736 | tf_op jit(solution)/shard_map/ppermute | solution.py:489
  51.7 4.9 %collective-permute-start.2 = (f32[2,1024]{1,0:T(2,128)S(1)}, f32[2,1024]{1,0:T(2,128)S(1)}, u32[]{:S(2)}, u32[]{:S(2)}) collective-permute-start(f32[2,1024]{1,0:T(2,128)S(1)} %get-tuple-element.29), channel_id=1, source_target_pairs={{0,32},{32,64},{64,96},{96,128},{128,160},{160,192},{192,224},{1,3... | collective-permute-start | bytes 24584 | tf_op jit(solution)/shard_map/ppermute | solution.py:524
  55.3 4.6 %collective-permute-start.3 = (f32[2,1024]{1,0:T(2,128)S(1)}, f32[2,1024]{1,0:T(2,128)S(1)}, u32[]{:S(2)}, u32[]{:S(2)}) collective-permute-start(f32[2,1024]{1,0:T(2,128)S(1)} %get-tuple-element.30), channel_id=1, source_target_pairs={{32,0},{64,32},{96,64},{128,96},{160,128},{192,160},{224,192},{33,... | collective-permute-start | bytes 24584 | tf_op jit(solution)/shard_map/ppermute | solution.py:525
  65.8 17.9 %copy-start.3 = (f32[7,7,8,128]{3,2,1,0:T(8,128)S(1)}, f32[7,7,8,128]{3,2,1,0:T(8,128)}, u32[]{:S(2)}) copy-start(f32[7,7,8,128]{3,2,1,0:T(8,128)} %constant.32.clone.cut_ref) | copy-start | bytes 602116
  65.8 17.9 %copy-start.4 = (bf16[256,128]{1,0:T(8,128)(2,1)S(1)}, bf16[256,128]{1,0:T(8,128)(2,1)}, u32[]{:S(2)}) copy-start(bf16[256,128]{1,0:T(8,128)(2,1)} %constant.29.clone.small_t_ref) | copy-start | bytes 196612
  65.9 17.9 %copy-start.7 = (f32[2,8,128]{2,1,0:T(8,128)S(1)}, f32[2,8,128]{2,1,0:T(8,128)}, u32[]{:S(2)}) copy-start(f32[2,8,128]{2,1,0:T(8,128)} %constant.33.clone.near_far_ref) | copy-start | bytes 24580
  85.4 10.5 %collective-permute-start.5 = (f32[128,1024]{1,0:T(8,128)S(1)}, f32[128,1024]{1,0:T(8,128)S(1)}, u32[]{:S(2)}, u32[]{:S(2)}) collective-permute-start(f32[128,1024]{1,0:T(8,128)S(1)} %get-tuple-element.34.scaled_ref), channel_id=1, source_target_pairs={{1,2},{2,1},{3,4},{4,3},{5,6},{6,5},{7,8},{8,7},{9,10},{10,9},{11,... | collective-permute-start | bytes 1572872 | tf_op jit(solution)/shard_map/ppermute | solution.py:488
  88.9 7.1 %collective-permute-start.4 = (f32[128,1024]{1,0:T(8,128)S(1)}, f32[128,1024]{1,0:T(8,128)S(1)}, u32[]{:S(2)}, u32[]{:S(2)}) collective-permute-start(f32[128,1024]{1,0:T(8,128)S(1)} %get-tuple-element.34.scaled_ref), channel_id=1, source_target_pairs={{0,1},{1,0},{2,3},{3,2},{4,5},{5,4},{6,7},{7,6},{8,9},{9,8},{10,11... | collective-permute-start | bytes 1572872 | tf_op jit(solution)/shard_map/ppermute | solution.py:489
  108.8 11.4 %collective-permute-start.7 = (f32[128,1024]{1,0:T(8,128)S(1)}, f32[128,1024]{1,0:T(8,128)S(1)}, u32[]{:S(2)}, u32[]{:S(2)}) collective-permute-start(f32[128,1024]{1,0:T(8,128)S(1)} %get-tuple-element.40.scaled_ref), channel_id=1, source_target_pairs={{1,2},{2,1},{3,4},{4,3},{5,6},{6,5},{7,8},{8,7},{9,10},{10,9},{11,... | collective-permute-start | bytes 1572872 | tf_op jit(solution)/shard_map/ppermute | solution.py:488
  113.4 6.9 %collective-permute-start.6 = (f32[128,1024]{1,0:T(8,128)S(1)}, f32[128,1024]{1,0:T(8,128)S(1)}, u32[]{:S(2)}, u32[]{:S(2)}) collective-permute-start(f32[128,1024]{1,0:T(8,128)S(1)} %get-tuple-element.40.scaled_ref), channel_id=1, source_target_pairs={{0,1},{1,0},{2,3},{3,2},{4,5},{5,4},{6,7},{7,6},{8,9},{9,8},{10,11... | collective-permute-start | bytes 1572872 | tf_op jit(solution)/shard_map/ppermute | solution.py:489

commit v5 on v4

--- a/solution.py
+++ b/solution.py
@@ -16,7 +16,8 @@
 SLABS = 8
 BR = 16
 B = 128
-PLANE_BRICKS = 64
+PLANE_SHIFT = 6
+PLANE_BRICKS = 1 << PLANE_SHIFT
 OWNERS = 32
 PER_PAIR = 3
 BRICK_ROWS = 3 * BR
@@ -25,7 +26,8 @@
 ID_ROW = SIDE_ROW + 1
 SEND_ROWS = END_ROW + 8
 CHUNKS = 4
-GROUP = 8
+GROUP_SHIFT = 3
+GROUP = 1 << GROUP_SHIFT
 YZ = ("yz_0", "yz_1", "yz_2")
 SHIFT_RATE = 0.05
 FLOOR = 2.0
@@ -125,7 +127,7 @@
     return jnp.concatenate([tile[t : t + 1] for t in range(8)], axis=1)
 
 
-def to_modes(field_ref, even_ref, odd_ref, small_ref, column_ref, lam_ref, fold_ref, modes_ref, ends_ref):
+def to_modes(field_ref, even_ref, odd_ref, small_ref, column_ref, inverse_ref, fold_ref, modes_ref, ends_ref):
     for i in range(XL // 8):
         rows = pl.ds(8 * i, 8)
         low = field_ref[rows, :H]
@@ -144,7 +146,7 @@
     last = jnp.zeros((8, N), F32)
     for i in range(XL // 8):
         rows = pl.ds(8 * i, 8)
-        modes = modes_ref[rows, :] / (column_ref[rows, 0:1] + lam_ref[...])
+        modes = modes_ref[rows, :] * inverse_ref[rows]
         modes_ref[rows, :] = modes
         first = first + modes * column_ref[rows, 1:2]
         last = last + modes * column_ref[rows, 2:3]
@@ -183,11 +185,11 @@
 
     def assign(s, carry):
         brick = slot_ref[0, s]
-        owner = brick // PLANE_BRICKS
+        owner = brick >> PLANE_SHIFT
         place = count_ref[owner]
         count_ref[owner] = place + 1
         held_ref[owner * PER_PAIR + place] = s
-        number_ref[owner * PER_PAIR + place] = brick - owner * PLANE_BRICKS
+        number_ref[owner * PER_PAIR + place] = brick & (PLANE_BRICKS - 1)
         return carry
 
     lax.fori_loop(0, PLANE_BRICKS, assign, 0, unroll=8)
@@ -233,7 +235,7 @@
             out_ref[owner, at + 2 * BR : at + 3 * BR] = weight_ref[s]
             ends = jnp.where(few_rows == 2 * place, accel_ref[s, BR : BR + 1], ends)
             ends = jnp.where(few_rows == 2 * place + 1, accel_ref[s, 2 * BR - 1 : 2 * BR], ends)
-            sides = pltpu.roll(side_ref[s // GROUP], (B + 2 * BR * place - BR * (s % GROUP)) % B, 1)
+            sides = pltpu.roll(side_ref[s >> GROUP_SHIFT], (2 * BR * place - BR * (s & (GROUP - 1))) & (B - 1), 1)
             sides = jnp.where(few_lanes < 2 * BR * place + BR, sides[0:1], sides[1:2])
             ends = jnp.where((few_rows == SIDE_ROW - END_ROW) & (few_lanes >= 2 * BR * place), sides, ends)
             ends = jnp.where((few_rows == ID_ROW - END_ROW) & (few_lanes == place), number, ends)
@@ -264,7 +266,8 @@
         rows = pl.ds(pl.multiple_of(x * BR, BR), BR)
         for y in range(N // B):
             cols = pl.ds(y * B, B)
-            source, place = from_ref[x * (N // B) + y] // 4, from_ref[x * (N // B) + y] % 4
+            held = from_ref[x * (N // B) + y]
+            source, place = held >> 2, held & 3
             fluid = (1 - solid_ref[x * (N // B) + y]).astype(F32)
             at = pl.multiple_of(place * BRICK_ROWS, BR)
             z_ref[0, rows, cols] = got_ref[source, pl.ds(at, BR)]
@@ -286,42 +289,54 @@
         ref[1:2] = ends_ref[row : row + 1]
 
 
-def setup_kernel(
-    place_ref, z_ref, inner_ref, x_ends_ref, sides_ref, partner_ref, outer_ref, xlo_ref, xhi_ref,
-    even_ref, odd_ref, small_ref, column_ref, lam_ref,
-    diagonal_ref, source_ref, modes_ref, ends_ref, ext_ref, fold_ref,
-):
-    ext_ref[7:8] = xlo_ref[0:1]
-    ext_ref[XL + 8 : XL + 9] = xhi_ref[0:1]
+def prepare_kernel(
+    z_ref, inner_ref, x_ends_ref, sides_ref, column_ref, lam_ref, beside_ref, source_ref, inverse_ref, ext_ref
+):
+    ext_ref[7:8] = jnp.zeros((1, N), F32)
+    ext_ref[XL + 8 : XL + 9] = jnp.zeros((1, N), F32)
     ext_ref[8 : XL + 8] = z_ref[1]
     lane = lax.broadcasted_iota(jnp.int32, (8, N), 1)
-    brick_end = (lane % B == B - 1) & (lane < N - 1)
+    brick_end = ((lane & (B - 1)) == B - 1) & (lane < N - 1)
+    for i in range(XL // 8):
+        rows = pl.ds(8 * i, 8)
+        root, side = z_ref[1, rows], sides_ref[rows]
+        after = pltpu.roll(root, N - 1, 1)
+        beside = SHIFT_RATE * root + ext_ref[pl.ds(8 * i + 9, 8)] + ext_ref[pl.ds(8 * i + 7, 8)]
+        beside = beside + jnp.where(lane < N - 1, after, 0.0) + jnp.where(lane > 0, pltpu.roll(root, 1, 1), 0.0)
+        beside_ref[rows] = beside
+        flux_y = jnp.where(brick_end, 0.5 * root * after * (side + pltpu.roll(side, N - 1, 1)), 0.0)
+        source_ref[rows] = inner_ref[rows] + pltpu.roll(flux_y, 1, 1) - flux_y
+        inverse_ref[rows] = 1.0 / (column_ref[rows, 0:1] + lam_ref[...])
+    for x in range(BR, XL, BR):
+        flux = 0.5 * ext_ref[x + 7 : x + 8] * ext_ref[x + 8 : x + 9] * (x_ends_ref[x - 1 : x] + x_ends_ref[x : x + 1])
+        source_ref[x - 1 : x] = source_ref[x - 1 : x] - flux
+        source_ref[x : x + 1] = source_ref[x : x + 1] + flux
+
+
+def setup_kernel(
+    place_ref, z_ref, beside_ref, inner_ref, x_ends_ref, partner_ref, outer_ref, xlo_ref, xhi_ref,
+    even_ref, odd_ref, small_ref, column_ref, inverse_ref,
+    diagonal_ref, source_ref, modes_ref, ends_ref, fold_ref,
+):
     sign = (2 * place_ref[1] - 1).astype(F32)
     for i in range(XL // 8):
         rows = pl.ds(8 * i, 8)
-        accel_z, root, side = z_ref[0, rows], z_ref[1, rows], sides_ref[rows]
+        accel_z, root = z_ref[0, rows], z_ref[1, rows]
         root_p, root_o = partner_ref[1, rows], outer_ref[1, rows]
-        after = pltpu.roll(root, N - 1, 1)
-        beside = root_p + root_o + ext_ref[pl.ds(8 * i + 9, 8)] + ext_ref[pl.ds(8 * i + 7, 8)]
-        beside = beside + jnp.where(lane < N - 1, after, 0.0) + jnp.where(lane > 0, pltpu.roll(root, 1, 1), 0.0)
-        diagonal_ref[rows] = root * (SHIFT_RATE * root + beside) + jnp.where(root > 0.0, 0.0, 1.0)
-        flux = sign * (root_p * (partner_ref[0, rows] + accel_z) - root_o * (accel_z + outer_ref[0, rows]))
-        flux_y = jnp.where(brick_end, root * after * (side + pltpu.roll(side, N - 1, 1)), 0.0)
-        source_ref[rows] = inner_ref[rows] + 0.5 * (root * flux + pltpu.roll(flux_y, 1, 1) - flux_y)
-    for x in range(0, XL + 1, BR):
-        before = x_ends_ref[x - 1 : x] if x > 0 else xlo_ref[1:2]
-        after = x_ends_ref[x : x + 1] if x < XL else xhi_ref[1:2]
-        flux = 0.5 * ext_ref[x + 7 : x + 8] * ext_ref[x + 8 : x + 9] * (before + after)
-        if x > 0:
-            source_ref[x - 1 : x] = source_ref[x - 1 : x] - flux
-        if x < XL:
-            source_ref[x : x + 1] = source_ref[x : x + 1] + flux
-    to_modes(source_ref, even_ref, odd_ref, small_ref, column_ref, lam_ref, fold_ref, modes_ref, ends_ref)
+        diagonal_ref[rows] = root * (beside_ref[rows] + root_p + root_o) + jnp.where(root > 0.0, 0.0, 1.0)
+        flux = root_p * (partner_ref[0, rows] + accel_z) - root_o * (accel_z + outer_ref[0, rows])
+        source_ref[rows] = inner_ref[rows] + (0.5 * sign) * (root * flux)
+    for at, rim_ref, sign in ((0, xlo_ref, 1.0), (XL - 1, xhi_ref, -1.0)):
+        row = pl.ds(at, 1)
+        face = z_ref[1, row] * rim_ref[0:1]
+        diagonal_ref[row] = diagonal_ref[row] + face
+        source_ref[row] = source_ref[row] + (0.5 * sign) * face * (x_ends_ref[row] + rim_ref[1:2])
+    to_modes(source_ref, even_ref, odd_ref, small_ref, column_ref, inverse_ref, fold_ref, modes_ref, ends_ref)
 
 
 def update_kernel(
     place_ref, modes_ref, all_ends_ref, z_ref, xlo_ref, xhi_ref, cut_ref, near_far_ref, even_ref, odd_ref,
-    small_t_ref, column_ref, lam_ref, update_ref, scaled_ref, rim_ref, work_ref,
+    small_t_ref, column_ref, inverse_ref, update_ref, scaled_ref, rim_ref, work_ref,
 ):
     slab = place_ref[0]
 
@@ -342,7 +357,7 @@
     for i in range(XL // 8):
         rows = pl.ds(8 * i, 8)
         change = column_ref[rows, 2:3] * high_row - column_ref[rows, 1:2] * low_row
-        work_ref[rows] = modes_ref[rows] - change / (column_ref[rows, 0:1] + lam_ref[...])
+        work_ref[rows] = modes_ref[rows] - change * inverse_ref[rows]
     work_ref[0:XL] = of_table(small_t_ref, work_ref[0:XL])
     work_ref[XL : XL + 8] = jnp.concatenate([as_row(before), as_row(after), jnp.zeros((6, N), F32)], axis=0)
     even = by_table(work_ref[:, :H], even_ref, False)
@@ -363,52 +378,64 @@
             rim_ref[1:2] = value[1:2] * xhi_ref[0:1]
 
 
-def image_rows(i, value_ref, scaled_ref, partner_ref, outer_ref, z_ref, diagonal_ref, ext_ref):
-    rows = pl.ds(8 * i, 8)
-    value, scaled = value_ref[rows], scaled_ref[rows]
-    lane = lax.broadcasted_iota(jnp.int32, (8, N), 1)
-    beside = partner_ref[rows] + outer_ref[rows] + ext_ref[pl.ds(8 * i + 9, 8)] + ext_ref[pl.ds(8 * i + 7, 8)]
-    beside = beside + jnp.where(lane < N - 1, pltpu.roll(scaled, N - 1, 1), 0.0)
-    beside = beside + jnp.where(lane > 0, pltpu.roll(scaled, 1, 1), 0.0)
-    return value, diagonal_ref[rows] * value - z_ref[1, rows] * beside
-
-
-def extend(scaled_ref, rim_ref, ext_ref):
+def own_image(value_ref, scaled_ref, rim_ref, z_ref, diagonal_ref, ext_ref):
     ext_ref[7:8] = rim_ref[0:1]
     ext_ref[XL + 8 : XL + 9] = rim_ref[1:2]
     ext_ref[8 : XL + 8] = scaled_ref[...]
+    lane = lax.broadcasted_iota(jnp.int32, (8, N), 1)
+    for i in range(XL // 8):
+        rows = pl.ds(8 * i, 8)
+        scaled = scaled_ref[rows]
+        beside = ext_ref[pl.ds(8 * i + 9, 8)] + ext_ref[pl.ds(8 * i + 7, 8)]
+        beside = beside + jnp.where(lane < N - 1, pltpu.roll(scaled, N - 1, 1), 0.0)
+        beside = beside + jnp.where(lane > 0, pltpu.roll(scaled, 1, 1), 0.0)
+        yield rows, diagonal_ref[rows] * value_ref[rows] - z_ref[1, rows] * beside
+
+
+def own_kernel(value_ref, scaled_ref, rim_ref, z_ref, diagonal_ref, own_ref, ext_ref):
+    for rows, image in own_image(value_ref, scaled_ref, rim_ref, z_ref, diagonal_ref, ext_ref):
+        own_ref[rows] = image
 
 
 def image_kernel(
-    value_ref, scaled_ref, rim_ref, partner_ref, outer_ref, z_ref, diagonal_ref,
-    even_ref, odd_ref, small_ref, column_ref, lam_ref,
-    image_ref, modes_ref, ends_ref, ext_ref, fold_ref,
-):
-    extend(scaled_ref, rim_ref, ext_ref)
-    for i in range(XL // 8):
-        _, image = image_rows(i, value_ref, scaled_ref, partner_ref, outer_ref, z_ref, diagonal_ref, ext_ref)
-        image_ref[pl.ds(8 * i, 8)] = image
-    to_modes(image_ref, even_ref, odd_ref, small_ref, column_ref, lam_ref, fold_ref, modes_ref, ends_ref)
+    own_ref, partner_ref, outer_ref, z_ref, even_ref, odd_ref, small_ref, column_ref, inverse_ref,
+    image_ref, modes_ref, ends_ref, fold_ref,
+):
+    for i in range(XL // 8):
+        rows = pl.ds(8 * i, 8)
+        image_ref[rows] = own_ref[rows] - z_ref[1, rows] * (partner_ref[rows] + outer_ref[rows])
+    to_modes(image_ref, even_ref, odd_ref, small_ref, column_ref, inverse_ref, fold_ref, modes_ref, ends_ref)
+
+
+def one_line(total):
+    line = jnp.sum(total, axis=0, keepdims=True)
+    return sum(line[:, t * 128 : (t + 1) * 128] for t in range(8))
+
+
+def own_sums_kernel(
+    value_ref, scaled_ref, rim_ref, z_ref, diagonal_ref, source_ref, update_ref, first_image_ref,
+    own_ref, lines_ref, ext_ref,
+):
+    totals = [jnp.zeros((8, N), F32) for _ in range(4)]
+    for rows, image in own_image(value_ref, scaled_ref, rim_ref, z_ref, diagonal_ref, ext_ref):
+        own_ref[rows] = image
+        v, r, u, q = value_ref[rows], source_ref[rows], update_ref[rows], first_image_ref[rows]
+        for k, (a, b) in enumerate(((r, u), (u, q), (r, v), (q, v))):
+            totals[k] = totals[k] + a * b
+    lines_ref[...] = jnp.concatenate([one_line(total) for total in totals] + [jnp.zeros((4, 128), F32)], axis=0)
 
 
 def sums_kernel(
-    value_ref, scaled_ref, rim_ref, partner_ref, outer_ref, z_ref, diagonal_ref, source_ref, update_ref,
-    first_image_ref, image_ref, sums_ref, ext_ref,
-):
-    extend(scaled_ref, rim_ref, ext_ref)
-    totals = [jnp.zeros((8, N), F32) for _ in range(6)]
-    for i in range(XL // 8):
-        rows = pl.ds(8 * i, 8)
-        v, t = image_rows(i, value_ref, scaled_ref, partner_ref, outer_ref, z_ref, diagonal_ref, ext_ref)
+    value_ref, own_ref, lines_ref, partner_ref, outer_ref, z_ref, update_ref, image_ref, sums_ref
+):
+    totals = [jnp.zeros((8, N), F32) for _ in range(2)]
+    for i in range(XL // 8):
+        rows = pl.ds(8 * i, 8)
+        t = own_ref[rows] - z_ref[1, rows] * (partner_ref[rows] + outer_ref[rows])
         image_ref[rows] = t
-        r, u, q = source_ref[rows], update_ref[rows], first_image_ref[rows]
-        for k, (a, b) in enumerate(((r, u), (u, q), (r, v), (q, v), (u, t), (v, t))):
-            totals[k] = totals[k] + a * b
-    lines = []
-    for total in totals:
-        line = jnp.sum(total, axis=0, keepdims=True)
-        lines.append(sum(line[:, t * 128 : (t + 1) * 128] for t in range(8)))
-    lines = jnp.concatenate(lines + [jnp.zeros((2, 128), F32)], axis=0)
+        totals[0] = totals[0] + update_ref[rows] * t
+        totals[1] = totals[1] + value_ref[rows] * t
+    lines = jnp.concatenate([lines_ref[0:4]] + [one_line(total) for total in totals] + [jnp.zeros((2, 128), F32)], axis=0)
     for j in range(OWNERS):
         sums_ref[j] = lines
 
@@ -421,7 +448,9 @@
         out_ref[j] = total
 
 
-def final_kernel(sums_ref, source_ref, u_ref, q_ref, v_ref, t_ref, solution_ref, residual_ref):
+def final_kernel(
+    sums_ref, source_ref, u_ref, q_ref, v_ref, t_ref, solution_hbm, residual_hbm, solution_ref, residual_ref, sem
+):
     total = sums_ref[0]
     for j in range(1, SLABS):
         total = total + sums_ref[j]
@@ -436,6 +465,8 @@
     second = energy / curve
     spread = lambda s: jnp.broadcast_to(s, (8, N))
     step, beta, second = spread(step), spread(beta), spread(second)
+    copies = []
+    size = XL // CHUNKS
     for i in range(XL // 8):
         rows = pl.ds(8 * i, 8)
         u, q = u_ref[rows], q_ref[rows]
@@ -443,6 +474,14 @@
         along = q - step * t_ref[rows] + beta * q
         solution_ref[rows] = step * u + second * direction
         residual_ref[rows] = source_ref[rows] - step * q - second * along
+        if (8 * i + 8) % size == 0:
+            done = pl.ds(8 * i + 8 - size, size)
+            for k, (ref, hbm) in enumerate(((solution_ref, solution_hbm), (residual_ref, residual_hbm))):
+                copy = pltpu.make_async_copy(ref.at[done], hbm.at[done], sem.at[k, 8 * i // size])
+                copy.start()
+                copies.append(copy)
+    for copy in copies:
+        copy.wait()
 
 
 def shape(*dims):
@@ -475,8 +514,6 @@
 def on_device(camera_accel, camera_weight, brick_slot, brick_solid):
     constant = {name: jnp.asarray(value) for name, value in tables().items()}
     dct = (constant["even"], constant["odd"])
-    slab_tables = (constant["column"], constant["lam_y"])
-    forward = dct + (constant["small"],) + slab_tables
     place = jnp.stack([lax.axis_index("gx"), lax.axis_index("yz_2")])
     slabs, owners = lax.axis_size("gx"), lax.axis_size(YZ)
     up_x = [(i, i + 1) for i in range(slabs - 1)]
@@ -523,14 +560,19 @@
     partner, outer = neighbours(z_fields)
     xlo = lax.ppermute(last, "gx", up_x)
     xhi = lax.ppermute(first, "gx", down_x)
+    beside, inner, inverse = call(
+        prepare_kernel, (shape(*PLANE),) * 3, [VMEM] * 6, (VMEM,) * 3, [EXT], name="prepare"
+    )(z_fields, inner, x_ends, sides, constant["column"], constant["lam_y"])
+    slab_tables = (constant["column"], inverse)
+    forward = dct + (constant["small"],) + slab_tables
     diagonal, source, modes, ends = call(
         setup_kernel,
         (shape(*PLANE), shape(*PLANE), shape(*PLANE), shape(SLABS, 16, 128)),
         [SMEM] + [VMEM] * 13,
         (VMEM,) * 4,
-        [EXT, FOLD],
+        [FOLD],
         name="setup",
-    )(place, z_fields, inner, x_ends, sides, partner, outer, xlo, xhi, *forward)
+    )(place, z_fields, beside, inner, x_ends, partner, outer, xlo, xhi, *forward)
 
     def updated(modes, ends):
         all_ends = lax.all_to_all(ends, "gx", split_axis=0, concat_axis=0, tiled=True)
@@ -547,28 +589,38 @@
         )
 
     u, scaled, rim = updated(modes, ends)
+    planes = neighbours(scaled)
+    own = call(own_kernel, shape(*PLANE), [VMEM] * 5, VMEM, [EXT], name="own")(u, scaled, rim, z_fields, diagonal)
     q, modes, ends = call(
         image_kernel,
         (shape(*PLANE), shape(*PLANE), shape(SLABS, 16, 128)),
-        [VMEM] * 12,
+        [VMEM] * 9,
         (VMEM,) * 3,
-        [EXT, FOLD],
+        [FOLD],
         name="image",
-    )(u, scaled, rim, *neighbours(scaled), z_fields, diagonal, *forward)
+    )(own, *planes, z_fields, *forward)
     v, scaled, rim = updated(modes, ends)
+    planes = neighbours(scaled)
+    own, lines = call(
+        own_sums_kernel, (shape(*PLANE), shape(8, 128)), [VMEM] * 8, (VMEM, VMEM), [EXT], name="own_sums"
+    )(v, scaled, rim, z_fields, diagonal, source, u, q)
     t, sums = call(
         sums_kernel,
         (shape(*PLANE), shape(OWNERS, 8, 128)),
-        [VMEM] * 10,
+        [VMEM] * 7,
         (VMEM, VMEM),
-        [EXT],
         name="sums",
-    )(v, scaled, rim, *neighbours(scaled), z_fields, diagonal, source, u, q)
+    )(v, own, lines, *planes, z_fields, u)
     sums = lax.all_to_all(sums, YZ, split_axis=0, concat_axis=0, tiled=True)
     sums = call(add_kernel, shape(SLABS, 8, 128), [VMEM], VMEM, name="add")(sums)
     sums = lax.all_to_all(sums, "gx", split_axis=0, concat_axis=0, tiled=True)
     result, residual = call(
-        final_kernel, (jax.ShapeDtypeStruct(PLANE, F32),) * 2, [VMEM] * 6, (VMEM, VMEM), name="final"
+        final_kernel,
+        (jax.ShapeDtypeStruct(PLANE, F32),) * 2,
+        [VMEM] * 6,
+        (HBM, HBM),
+        [FOLD, FOLD, pltpu.SemaphoreType.DMA((2, CHUNKS))],
+        name="final",
     )(sums, source, u, q, v, t)
     return result[None], residual[None]
 

time: 150 us -> 148 us (0.987)
  waiting for transfers between devices: 23 us -> 20.3 us
    ppermute x1, waiting for transfers between devices: 3.27 us -> 1.72 us  [on_device(): xhi = lax.ppermute(first, 'gx', down_x)]
    pallas_call x9 -> x12, Pallas kernels: 17.5 us -> 17.4 us  [with_spaces(): run(*(x if spec is SMEM else pltpu.with_memory_space_constraint(x, spec.m...]
  transfers between devices with their start and end apart: 8 -> 8, of which waited for: 4 -> 4; matrix products, arithmetic and copies ran while one was open for 0% -> 0% of each run, Pallas kernels for 0% -> 2%
where the time goes in v5:
time: 148 us; the launch traced here: 147 us
  blocking collectives  93.6 us (63%)
  waiting for transfers between devices  20.3 us (14%)
  Pallas kernels  17.4 us (12%)
  starting transfers between devices  15 us (10%)
    all_to_all x1, blocking collectives, on_device(): got = lax.all_to_all(send, YZ, split_axis=0, concat_axis=0, tiled=True)  41.1 us
    all_to_all x2, blocking collectives, updated(): lax.all_to_all(ends, 'gx', split_axis=0, concat_axis=0, tiled=True)  24.8 us
    ppermute x3, waiting for transfers between devices, neighbours(): outer = lax.ppermute(value, YZ, off_chip)  18.6 us
    all_to_all x1, blocking collectives, on_device(): sums = lax.all_to_all(sums, YZ, split_axis=0, concat_axis=0, tiled=True)  18.4 us
    pallas_call x12, Pallas kernels, with_spaces(): run(*(x if spec is SMEM else pltpu.with_memory_space_constraint(x, spec.m...  17.4 us
    ppermute x3, starting transfers between devices, neighbours(): outer = lax.ppermute(value, YZ, off_chip)  9.93 us
    all_to_all x1, blocking collectives, on_device(): sums = lax.all_to_all(sums, 'gx', split_axis=0, concat_axis=0, tiled=True)  9.24 us
    ppermute x1, starting transfers between devices, on_device(): xlo = lax.ppermute(last, 'gx', up_x)  3.54 us
  transfers between devices with their start and end apart: 8, of which 4 were waited for; matrix products, arithmetic and copies ran while one was open for 0% of the time, Pallas kernels for 2%

profile of v5, /device:TPU:1, one launch (start us, length us, event | category | flops | bytes accessed | tf_op | source)
XLA Modules:
  0.0 147.3 jit_solution(17874680524028023621)
XLA Ops:
  0.6 0.1 pad_add_fusion.place_ref
  0.7 4.2 %pack.1 = f32[32,152,128]{2,1,0:T(8,128)S(1)} custom-call(s32[2]{0:T(128)S(1)} %pad_add_fusion.place_ref, s32[1,64]{1,0:T(1,128)} %slot_hbm.1, f32[64,48,128]{2,1,0:T(8,128)} %bitcast.8, f32[64,16,128]{2,1,0:T(8,128)} %bitcast.9), custom_call_target="tpu_custom_call" | custom-call | tf_op jit(solution)/shard_map/pack/pallas_call | solution.py:499
  4.9 0.0 copy-start.8
  4.9 41.1 %all_to_all.25.got_ref = f32[32,152,128]{2,1,0:T(8,128)S(1)} all-to-all(f32[32,152,128]{2,1,0:T(8,128)S(1)} %pack.1), channel_id=1, replica_groups=mesh['gx'=8,'yz_0'=4,'yz_1'=4,'yz_2'=2] {'yz_0','yz_1','yz_2'}, dimensions={0} | all-to-all | bytes 4980736 | tf_op jit(solution)/shard_map/all_to_all | solution.py:547
  46.0 0.0 copy-start.2
  46.0 0.0 copy-start.7
  46.1 0.0 copy-done.8
  46.1 0.0 copy-start
  46.1 0.0 copy-start.1
  46.1 0.0 copy-start.5
  46.1 2.6 %place.1 = (f32[2,128,1024]{2,1,0:T(8,128)S(1)}, f32[128,1024]{1,0:T(8,128)S(1)}, f32[128,1024]{1,0:T(8,128)S(1)}, f32[128,1024]{1,0:T(8,128)S(1)}, f32[2,1024]{1,0:T(2,128)S(1)}, /*index=5*/f32[2,1024]{1,0:T(2,128)S(1)}) custom-call(s32[64]{0:T(128)S(1)} %bitcast.7, f32[32,152,128]{2,1,0:T(8,128)S(1)} %all_to_all.25.got_ref), custom_call_target="tpu_custom_call" | custom-call | tf_op jit(solution)/shard_map/place/pallas_call | solution.py:499
  48.7 1.9 %collective-permute-start.1 = (f32[2,128,1024]{2,1,0:T(8,128)S(1)}, f32[2,128,1024]{2,1,0:T(8,128)S(1)}, u32[]{:S(2)}, u32[]{:S(2)}) collective-permute-start(f32[2,128,1024]{2,1,0:T(8,128)S(1)} %get-tuple-element.30.z_ref), channel_id=1, source_target_pairs={{1,2},{2,1},{3,4},{4,3},{5,6},{6,5},{7,8},{8,7},{9,10},{10,9},{11,... | collective-permute-start | bytes 3145736 | tf_op jit(solution)/shard_map/ppermute | solution.py:525
  50.7 0.1 collective-permute-start
  50.8 3.5 %collective-permute-start.2 = (f32[2,1024]{1,0:T(2,128)S(1)}, f32[2,1024]{1,0:T(2,128)S(1)}, u32[]{:S(2)}, u32[]{:S(2)}) collective-permute-start(f32[2,1024]{1,0:T(2,128)S(1)} %get-tuple-element.36), channel_id=1, source_target_pairs={{0,32},{32,64},{64,96},{96,128},{128,160},{160,192},{192,224},{1,3... | collective-permute-start | bytes 24584 | tf_op jit(solution)/shard_map/ppermute | solution.py:561
  54.3 1.3 collective-permute-start.3
  55.6 0.0 copy-done.2
  55.6 0.0 copy-done.7
  55.6 1.5 %prepare.1 = (f32[128,1024]{1,0:T(8,128)S(1)}, f32[128,1024]{1,0:T(8,128)S(1)}, f32[128,1024]{1,0:T(8,128)S(1)}) custom-call(f32[2,128,1024]{2,1,0:T(8,128)S(1)} %get-tuple-element.30.z_ref, f32[128,1024]{1,0:T(8,128)S(1)} %get-tuple-element.31.inner_ref, f32[128,1024]{1,0:T(8,128)S(1)} %get-tuple-element.32.x_ends_ref, ...), custom_call_target="tpu_custom_call" | custom-call | tf_op jit(solution)/shard_map/prepare/pallas_call | solution.py:499
  57.2 0.0 collective-permute-done.2.xlo_ref
  57.2 1.7 %collective-permute-done.3.xhi_ref = f32[2,1024]{1,0:T(2,128)S(1)} collective-permute-done((f32[2,1024]{1,0:T(2,128)S(1)}, f32[2,1024]{1,0:T(2,128)S(1)}, u32[]{:S(2)}, u32[]{:S(2)}) %collective-permute-start.3) | collective-permute-done | bytes 8224 | tf_op jit(solution)/shard_map/ppermute | solution.py:562
  58.9 6.0 %collective-permute-done.1.outer_ref = f32[2,128,1024]{2,1,0:T(8,128)S(1)} collective-permute-done((f32[2,128,1024]{2,1,0:T(8,128)S(1)}, f32[2,128,1024]{2,1,0:T(8,128)S(1)}, u32[]{:S(2)}, u32[]{:S(2)}) %collective-permute-start.1) | collective-permute-done | bytes 1048608 | tf_op jit(solution)/shard_map/ppermute | solution.py:525
  64.8 0.0 collective-permute-done.partner_ref
  64.8 0.0 copy-done
  64.9 0.0 copy-done.1
  64.9 0.0 copy-done.5
  64.9 0.0 copy-start.3
  64.9 0.0 copy-start.4
  64.9 0.0 copy-start.6
  64.9 1.9 %setup.1 = (f32[128,1024]{1,0:T(8,128)S(1)}, f32[128,1024]{1,0:T(8,128)S(1)}, f32[128,1024]{1,0:T(8,128)S(1)}, f32[8,16,128]{2,1,0:T(8,128)S(1)}) custom-call(s32[2]{0:T(128)S(1)} %pad_add_fusion.place_ref, f32[2,128,1024]{2,1,0:T(8,128)S(1)} %get-tuple-element.30.z_ref, f32[128,1024]{1,0:T(8,128)S(1)} %get-tuple-element.34.beside_ref, ...), custom_call_target="tpu_custom_call" | custom-call | tf_op jit(solution)/shard_map/setup/pallas_call | solution.py:499
  66.8 15.2 %all_to_all.26.all_ends_ref = f32[8,16,128]{2,1,0:T(8,128)S(1)} all-to-all(f32[8,16,128]{2,1,0:T(8,128)S(1)} %get-tuple-element.40), channel_id=1, replica_groups=mesh['gx'=8,'yz_0'=4,'yz_1'=4,'yz_2'=2] {'gx'}, dimensions={0} | all-to-all | bytes 131072 | tf_op jit(solution)/shard_map/all_to_all | solution.py:578
  82.0 0.0 copy-done.3
  82.0 0.0 copy-done.4
  82.0 0.0 copy-done.6
  82.0 1.7 %update.2 = (f32[128,1024]{1,0:T(8,128)S(1)}, f32[128,1024]{1,0:T(8,128)S(1)}, f32[2,1024]{1,0:T(2,128)S(1)}) custom-call(s32[2]{0:T(128)S(1)} %pad_add_fusion.place_ref, f32[128,1024]{1,0:T(8,128)S(1)} %get-tuple-element.39.modes_ref, f32[8,16,128]{2,1,0:T(8,128)S(1)} %all_to_all.26.all_ends_ref, f32[2,128,1024]{2,1,0:T(8,128)S(1)} %get-tuple-element.30.z_ref, ...), custom_call_target="tpu_custom_call" | custom-call | tf_op jit(solution)/shard_map/update/pallas_call | solution.py:499
  83.7 3.4 %collective-permute-start.5 = (f32[128,1024]{1,0:T(8,128)S(1)}, f32[128,1024]{1,0:T(8,128)S(1)}, u32[]{:S(2)}, u32[]{:S(2)}) collective-permute-start(f32[128,1024]{1,0:T(8,128)S(1)} %get-tuple-element.42.scaled_ref), channel_id=1, source_target_pairs={{1,2},{2,1},{3,4},{4,3},{5,6},{6,5},{7,8},{8,7},{9,10},{10,9},{11,... | collective-permute-start | bytes 1572872 | tf_op jit(solution)/shard_map/ppermute | solution.py:525
  87.2 0.1 collective-permute-start.4
  87.3 0.4 own.1.own_ref
  87.7 6.5 %collective-permute-done.5.outer_ref = f32[128,1024]{1,0:T(8,128)S(1)} collective-permute-done((f32[128,1024]{1,0:T(8,128)S(1)}, f32[128,1024]{1,0:T(8,128)S(1)}, u32[]{:S(2)}, u32[]{:S(2)}) %collective-permute-start.5) | collective-permute-done | bytes 524320 | tf_op jit(solution)/shard_map/ppermute | solution.py:525
  94.2 0.0 collective-permute-done.4.partner_ref
  94.2 1.2 image.1
  95.4 9.6 %all_to_all.27.all_ends_ref = f32[8,16,128]{2,1,0:T(8,128)S(1)} all-to-all(f32[8,16,128]{2,1,0:T(8,128)S(1)} %get-tuple-element.46), channel_id=1, replica_groups=mesh['gx'=8,'yz_0'=4,'yz_1'=4,'yz_2'=2] {'gx'}, dimensions={0} | all-to-all | bytes 131072 | tf_op jit(solution)/shard_map/all_to_all | solution.py:578
  105.0 1.7 %update.3 = (f32[128,1024]{1,0:T(8,128)S(1)}, f32[128,1024]{1,0:T(8,128)S(1)}, f32[2,1024]{1,0:T(2,128)S(1)}) custom-call(s32[2]{0:T(128)S(1)} %pad_add_fusion.place_ref, f32[128,1024]{1,0:T(8,128)S(1)} %get-tuple-element.45.modes_ref, f32[8,16,128]{2,1,0:T(8,128)S(1)} %all_to_all.27.all_ends_ref, f32[2,128,1024]{2,1,0:T(8,128)S(1)} %get-tuple-element.30.z_ref, ...), custom_call_target="tpu_custom_call" | custom-call | tf_op jit(solution)/shard_map/update/pallas_call | solution.py:499
  106.7 4.6 %collective-permute-start.7 = (f32[128,1024]{1,0:T(8,128)S(1)}, f32[128,1024]{1,0:T(8,128)S(1)}, u32[]{:S(2)}, u32[]{:S(2)}) collective-permute-start(f32[128,1024]{1,0:T(8,128)S(1)} %get-tuple-element.48.scaled_ref), channel_id=1, source_target_pairs={{1,2},{2,1},{3,4},{4,3},{5,6},{6,5},{7,8},{8,7},{9,10},{10,9},{11,... | collective-permute-start | bytes 1572872 | tf_op jit(solution)/shard_map/ppermute | solution.py:525
  111.3 0.1 collective-permute-start.6
  111.4 0.7 own_sums.1
  112.1 6.1 %collective-permute-done.7.outer_ref = f32[128,1024]{1,0:T(8,128)S(1)} collective-permute-done((f32[128,1024]{1,0:T(8,128)S(1)}, f32[128,1024]{1,0:T(8,128)S(1)}, u32[]{:S(2)}, u32[]{:S(2)}) %collective-permute-start.7) | collective-permute-done | bytes 524320 | tf_op jit(solution)/shard_map/ppermute | solution.py:525
  118.2 0.0 collective-permute-done.6.partner_ref
  118.2 0.2 sums.1
  118.4 18.4 %all_to_all.28.sums_ref = f32[32,8,128]{2,1,0:T(8,128)S(1)} all-to-all(f32[32,8,128]{2,1,0:T(8,128)S(1)} %get-tuple-element.54), channel_id=1, replica_groups=mesh['gx'=8,'yz_0'=4,'yz_1'=4,'yz_2'=2] {'yz_0','yz_1','yz_2'}, dimensions={0} | all-to-all | bytes 262144 | tf_op jit(solution)/shard_map/all_to_all | solution.py:614
  136.8 9.2 %all_to_all.29.sums_ref = f32[8,8,128]{2,1,0:T(8,128)S(1)} all-to-all(f32[8,8,128]{2,1,0:T(8,128)S(1)} %add.3), channel_id=1, replica_groups=mesh['gx'=8,'yz_0'=4,'yz_1'=4,'yz_2'=2] {'gx'}, dimensions={0} | all-to-all | bytes 65536 | tf_op jit(solution)/shard_map/all_to_all | solution.py:616
  146.1 1.2 final.1
  (1 shorter events, 0.0 us)
Async XLA Ops:
  4.9 41.1 %copy-start.8 = (s32[1,64]{1,0:T(1,128)S(1)}, s32[1,64]{1,0:T(1,128)}, u32[]{:S(2)}) copy-start(s32[1,64]{1,0:T(1,128)} %param.15) | copy-start | bytes 772
  46.0 9.6 %copy-start.2 = (f32[128,128]{1,0:T(8,128)S(1)}, f32[128,128]{1,0:T(8,128)}, u32[]{:S(2)}) copy-start(f32[128,128]{1,0:T(8,128)} %constant.30.clone.column_ref) | copy-start | bytes 196612
  46.0 9.6 %copy-start.7 = (f32[1,1024]{1,0:T(1,128)S(1)}, f32[1,1024]{1,0:T(1,128)}, u32[]{:S(2)}) copy-start(f32[1,1024]{1,0:T(1,128)} %constant.31.clone.lam_ref) | copy-start | bytes 12292
  46.1 18.8 %copy-start = (bf16[2,512,512]{2,1,0:T(8,128)(2,1)S(1)}, bf16[2,512,512]{2,1,0:T(8,128)(2,1)}, u32[]{:S(2)}) copy-start(bf16[2,512,512]{2,1,0:T(8,128)(2,1)} %constant.27.clone.odd_ref) | copy-start | bytes 3145732
  46.1 18.8 %copy-start.1 = (bf16[2,512,512]{2,1,0:T(8,128)(2,1)S(1)}, bf16[2,512,512]{2,1,0:T(8,128)(2,1)}, u32[]{:S(2)}) copy-start(bf16[2,512,512]{2,1,0:T(8,128)(2,1)} %constant.26.clone.even_ref) | copy-start | bytes 3145732
  46.1 18.8 %copy-start.5 = (bf16[256,128]{1,0:T(8,128)(2,1)S(1)}, bf16[256,128]{1,0:T(8,128)(2,1)}, u32[]{:S(2)}) copy-start(bf16[256,128]{1,0:T(8,128)(2,1)} %constant.28.clone.small_ref) | copy-start | bytes 196612
  48.7 16.1 %collective-permute-start.1 = (f32[2,128,1024]{2,1,0:T(8,128)S(1)}, f32[2,128,1024]{2,1,0:T(8,128)S(1)}, u32[]{:S(2)}, u32[]{:S(2)}) collective-permute-start(f32[2,128,1024]{2,1,0:T(8,128)S(1)} %get-tuple-element.30.z_ref), channel_id=1, source_target_pairs={{1,2},{2,1},{3,4},{4,3},{5,6},{6,5},{7,8},{8,7},{9,10},{10,9},{11,... | collective-permute-start | bytes 3145736 | tf_op jit(solution)/shard_map/ppermute | solution.py:525
  50.7 14.2 %collective-permute-start = (f32[2,128,1024]{2,1,0:T(8,128)S(1)}, f32[2,128,1024]{2,1,0:T(8,128)S(1)}, u32[]{:S(2)}, u32[]{:S(2)}) collective-permute-start(f32[2,128,1024]{2,1,0:T(8,128)S(1)} %get-tuple-element.30.z_ref), channel_id=1, source_target_pairs={{0,1},{1,0},{2,3},{3,2},{4,5},{5,4},{6,7},{7,6},{8,9},{9,8},{10,11... | collective-permute-start | bytes 3145736 | tf_op jit(solution)/shard_map/ppermute | solution.py:526
  50.8 6.4 %collective-permute-start.2 = (f32[2,1024]{1,0:T(2,128)S(1)}, f32[2,1024]{1,0:T(2,128)S(1)}, u32[]{:S(2)}, u32[]{:S(2)}) collective-permute-start(f32[2,1024]{1,0:T(2,128)S(1)} %get-tuple-element.36), channel_id=1, source_target_pairs={{0,32},{32,64},{64,96},{96,128},{128,160},{160,192},{192,224},{1,3... | collective-permute-start | bytes 24584 | tf_op jit(solution)/shard_map/ppermute | solution.py:561
  54.3 4.6 %collective-permute-start.3 = (f32[2,1024]{1,0:T(2,128)S(1)}, f32[2,1024]{1,0:T(2,128)S(1)}, u32[]{:S(2)}, u32[]{:S(2)}) collective-permute-start(f32[2,1024]{1,0:T(2,128)S(1)} %get-tuple-element.37), channel_id=1, source_target_pairs={{32,0},{64,32},{96,64},{128,96},{160,128},{192,160},{224,192},{33,... | collective-permute-start | bytes 24584 | tf_op jit(solution)/shard_map/ppermute | solution.py:562
  64.9 17.1 %copy-start.3 = (f32[7,7,8,128]{3,2,1,0:T(8,128)S(1)}, f32[7,7,8,128]{3,2,1,0:T(8,128)}, u32[]{:S(2)}) copy-start(f32[7,7,8,128]{3,2,1,0:T(8,128)} %constant.32.clone.cut_ref) | copy-start | bytes 602116
  64.9 17.1 %copy-start.4 = (bf16[256,128]{1,0:T(8,128)(2,1)S(1)}, bf16[256,128]{1,0:T(8,128)(2,1)}, u32[]{:S(2)}) copy-start(bf16[256,128]{1,0:T(8,128)(2,1)} %constant.29.clone.small_t_ref) | copy-start | bytes 196612
  64.9 17.1 %copy-start.6 = (f32[2,8,128]{2,1,0:T(8,128)S(1)}, f32[2,8,128]{2,1,0:T(8,128)}, u32[]{:S(2)}) copy-start(f32[2,8,128]{2,1,0:T(8,128)} %constant.33.clone.near_far_ref) | copy-start | bytes 24580
  83.7 10.5 %collective-permute-start.5 = (f32[128,1024]{1,0:T(8,128)S(1)}, f32[128,1024]{1,0:T(8,128)S(1)}, u32[]{:S(2)}, u32[]{:S(2)}) collective-permute-start(f32[128,1024]{1,0:T(8,128)S(1)} %get-tuple-element.42.scaled_ref), channel_id=1, source_target_pairs={{1,2},{2,1},{3,4},{4,3},{5,6},{6,5},{7,8},{8,7},{9,10},{10,9},{11,... | collective-permute-start | bytes 1572872 | tf_op jit(solution)/shard_map/ppermute | solution.py:525
  87.2 7.1 %collective-permute-start.4 = (f32[128,1024]{1,0:T(8,128)S(1)}, f32[128,1024]{1,0:T(8,128)S(1)}, u32[]{:S(2)}, u32[]{:S(2)}) collective-permute-start(f32[128,1024]{1,0:T(8,128)S(1)} %get-tuple-element.42.scaled_ref), channel_id=1, source_target_pairs={{0,1},{1,0},{2,3},{3,2},{4,5},{5,4},{6,7},{7,6},{8,9},{9,8},{10,11... | collective-permute-start | bytes 1572872 | tf_op jit(solution)/shard_map/ppermute | solution.py:526
  106.7 11.4 %collective-permute-start.7 = (f32[128,1024]{1,0:T(8,128)S(1)}, f32[128,1024]{1,0:T(8,128)S(1)}, u32[]{:S(2)}, u32[]{:S(2)}) collective-permute-start(f32[128,1024]{1,0:T(8,128)S(1)} %get-tuple-element.48.scaled_ref), channel_id=1, source_target_pairs={{1,2},{2,1},{3,4},{4,3},{5,6},{6,5},{7,8},{8,7},{9,10},{10,9},{11,... | collective-permute-start | bytes 1572872 | tf_op jit(solution)/shard_map/ppermute | solution.py:525
  111.3 6.9 %collective-permute-start.6 = (f32[128,1024]{1,0:T(8,128)S(1)}, f32[128,1024]{1,0:T(8,128)S(1)}, u32[]{:S(2)}, u32[]{:S(2)}) collective-permute-start(f32[128,1024]{1,0:T(8,128)S(1)} %get-tuple-element.48.scaled_ref), channel_id=1, source_target_pairs={{0,1},{1,0},{2,3},{3,2},{4,5},{5,4},{6,7},{7,6},{8,9},{9,8},{10,11... | collective-permute-start | bytes 1572872 | tf_op jit(solution)/shard_map/ppermute | solution.py:526

commit v6 on v5

--- a/solution.py
+++ b/solution.py
@@ -19,6 +19,7 @@
 PLANE_SHIFT = 6
 PLANE_BRICKS = 1 << PLANE_SHIFT
 OWNERS = 32
+PEERS = 16
 PER_PAIR = 3
 BRICK_ROWS = 3 * BR
 END_ROW = PER_PAIR * BRICK_ROWS
@@ -245,34 +246,51 @@
     lax.fori_loop(0, OWNERS, fill, 0, unroll=4)
 
 
-def place_kernel(
-    solid_ref, got_ref, z_ref, source_ref, ends_ref, sides_ref, first_ref, last_ref, ids_ref, from_ref, sem
-):
-    ids_copy = pltpu.make_async_copy(got_ref.at[:, pl.ds(ID_ROW, 1)], ids_ref, sem)
-    ids_copy.start()
-    ids_copy.wait()
-    lane = lax.broadcasted_iota(jnp.int32, (BR, B), 1)
-    row = lax.broadcasted_iota(jnp.int32, (BR, B), 0)
-
-    def find(source, carry):
-        for place in range(PER_PAIR):
-            brick = ids_ref[source, 0, place].astype(jnp.int32)
-            from_ref[jnp.where(brick < 0, PLANE_BRICKS, brick)] = source * 4 + place
-        return carry
-
-    lax.fori_loop(0, OWNERS, find, 0, unroll=4)
+def place_kernel(solid_ref, got_ref, z_ref, first_ref, last_ref, from_ref, origin_ref, sem):
+    lane = lax.broadcasted_iota(jnp.int32, (OWNERS, B), 1)
+    slot = (lax.broadcasted_iota(jnp.int32, (OWNERS, B), 0) << 2).astype(F32)
+    numbers = got_ref[:, ID_ROW, :].astype(jnp.int32)
+    origin = jnp.zeros((OWNERS, B), F32)
+    for place in range(PER_PAIR):
+        origin = origin + jnp.where(numbers[:, place : place + 1] == lane, slot + place, 0.0)
+    origin_ref[...] = jnp.broadcast_to(jnp.sum(origin, axis=0, keepdims=True), (8, B)).astype(jnp.int32)
+    copy = pltpu.make_async_copy(origin_ref.at[pl.ds(0, 1)], from_ref, sem)
+    copy.start()
+    copy.wait()
 
     def line(x, carry):
         rows = pl.ds(pl.multiple_of(x * BR, BR), BR)
         for y in range(N // B):
             cols = pl.ds(y * B, B)
-            held = from_ref[x * (N // B) + y]
+            held = from_ref[0, x * (N // B) + y]
             source, place = held >> 2, held & 3
             fluid = (1 - solid_ref[x * (N // B) + y]).astype(F32)
             at = pl.multiple_of(place * BRICK_ROWS, BR)
             z_ref[0, rows, cols] = got_ref[source, pl.ds(at, BR)]
+            z_ref[1, rows, cols] = got_ref[source, pl.ds(at + 2 * BR, BR)] * fluid
+        return carry
+
+    lax.fori_loop(0, XL // BR, line, 0)
+    for ref, row, end in ((first_ref, 0, 0), (last_ref, XL - 1, 1)):
+        ref[0:1] = z_ref[1, row : row + 1]
+        for y in range(N // B):
+            held = from_ref[0, row // BR * (N // B) + y]
+            ref[1:2, y * B : (y + 1) * B] = got_ref[held >> 2, pl.ds(END_ROW + end + 2 * (held & 3), 1)]
+
+
+def place_rest_kernel(solid_ref, from_ref, got_ref, source_ref, ends_ref, sides_ref):
+    lane = lax.broadcasted_iota(jnp.int32, (BR, B), 1)
+    row = lax.broadcasted_iota(jnp.int32, (BR, B), 0)
+
+    def line(x, carry):
+        rows = pl.ds(pl.multiple_of(x * BR, BR), BR)
+        for y in range(N // B):
+            cols = pl.ds(y * B, B)
+            held = from_ref[0, x * (N // B) + y]
+            source, place = held >> 2, held & 3
+            fluid = (1 - solid_ref[x * (N // B) + y]).astype(F32)
+            at = pl.multiple_of(place * BRICK_ROWS, BR)
             source_ref[rows, cols] = got_ref[source, pl.ds(at + BR, BR)] * fluid
-            z_ref[1, rows, cols] = got_ref[source, pl.ds(at + 2 * BR, BR)] * fluid
             sides = jnp.broadcast_to(got_ref[source, SIDE_ROW : SIDE_ROW + 1], (BR, B))
             own = lane - row - 2 * BR * place
             low = jnp.sum(jnp.where(own == 0, sides, 0.0), axis=1, keepdims=True)
@@ -284,9 +302,6 @@
         return carry
 
     lax.fori_loop(0, XL // BR, line, 0)
-    for ref, row in ((first_ref, 0), (last_ref, XL - 1)):
-        ref[0:1] = z_ref[1, row : row + 1]
-        ref[1:2] = ends_ref[row : row + 1]
 
 
 def prepare_kernel(
@@ -436,15 +451,18 @@
         totals[0] = totals[0] + update_ref[rows] * t
         totals[1] = totals[1] + value_ref[rows] * t
     lines = jnp.concatenate([lines_ref[0:4]] + [one_line(total) for total in totals] + [jnp.zeros((2, 128), F32)], axis=0)
-    for j in range(OWNERS):
-        sums_ref[j] = lines
+    index = [lax.broadcasted_iota(jnp.int32, (8, 128), k) for k in range(2)]
+    line = jnp.where(index[0] == index[1], jnp.sum(lines, axis=1, keepdims=True), 0.0)
+    line = jnp.sum(line, axis=0, keepdims=True)
+    for j in range(PEERS):
+        sums_ref[j] = line
 
 
 def add_kernel(sums_ref, out_ref):
     total = sums_ref[0]
-    for j in range(1, OWNERS):
+    for j in range(1, PEERS):
         total = total + sums_ref[j]
-    for j in range(SLABS):
+    for j in range(PEERS):
         out_ref[j] = total
 
 
@@ -452,8 +470,10 @@
     sums_ref, source_ref, u_ref, q_ref, v_ref, t_ref, solution_hbm, residual_hbm, solution_ref, residual_ref, sem
 ):
     total = sums_ref[0]
-    for j in range(1, SLABS):
+    for j in range(1, PEERS):
         total = total + sums_ref[j]
+    index = [lax.broadcasted_iota(jnp.int32, (8, 128), k) for k in range(2)]
+    total = jnp.where(index[0] == index[1], jnp.broadcast_to(total, (8, 128)), 0.0)
     total = jnp.sum(total, axis=1, keepdims=True)
     ru, uq, rv, qv, ut, vt = (total[k : k + 1] for k in range(6))
     step = ru / uq
@@ -545,21 +565,20 @@
         name="pack",
     )(place, brick_slot, camera_accel[0].reshape(PLANE_BRICKS, 3 * BR, B), camera_weight[0])
     got = lax.all_to_all(send, YZ, split_axis=0, concat_axis=0, tiled=True)
-    z_fields, inner, x_ends, sides, first, last = call(
+    z_fields, first, last, origin = call(
         place_kernel,
-        (shape(2, *PLANE), shape(*PLANE), shape(*PLANE), shape(*PLANE), shape(2, N), shape(2, N)),
+        (shape(2, *PLANE), shape(2, N), shape(2, N), jax.ShapeDtypeStruct((1, B), jnp.int32)),
         [SMEM, VMEM],
-        (VMEM,) * 6,
-        [
-            pltpu.SMEM((OWNERS, 1, B), F32),
-            pltpu.SMEM((PLANE_BRICKS + 1,), jnp.int32),
-            pltpu.SemaphoreType.DMA,
-        ],
+        (VMEM,) * 3 + (SMEM,),
+        [pltpu.VMEM((8, B), jnp.int32), pltpu.SemaphoreType.DMA],
         name="place",
     )(brick_solid[0], got)
     partner, outer = neighbours(z_fields)
     xlo = lax.ppermute(last, "gx", up_x)
     xhi = lax.ppermute(first, "gx", down_x)
+    inner, x_ends, sides = call(
+        place_rest_kernel, (shape(*PLANE),) * 3, [SMEM, SMEM, VMEM], (VMEM,) * 3, name="place_rest"
+    )(brick_solid[0], origin, got)
     beside, inner, inverse = call(
         prepare_kernel, (shape(*PLANE),) * 3, [VMEM] * 6, (VMEM,) * 3, [EXT], name="prepare"
     )(z_fields, inner, x_ends, sides, constant["column"], constant["lam_y"])
@@ -606,14 +625,14 @@
     )(v, scaled, rim, z_fields, diagonal, source, u, q)
     t, sums = call(
         sums_kernel,
-        (shape(*PLANE), shape(OWNERS, 8, 128)),
+        (shape(*PLANE), shape(PEERS, 1, 128)),
         [VMEM] * 7,
         (VMEM, VMEM),
         name="sums",
     )(v, own, lines, *planes, z_fields, u)
-    sums = lax.all_to_all(sums, YZ, split_axis=0, concat_axis=0, tiled=True)
-    sums = call(add_kernel, shape(SLABS, 8, 128), [VMEM], VMEM, name="add")(sums)
-    sums = lax.all_to_all(sums, "gx", split_axis=0, concat_axis=0, tiled=True)
+    sums = lax.all_to_all(sums, ("gx", "yz_2"), split_axis=0, concat_axis=0, tiled=True)
+    sums = call(add_kernel, shape(PEERS, 1, 128), [VMEM], VMEM, name="add")(sums)
+    sums = lax.all_to_all(sums, ("yz_0", "yz_1"), split_axis=0, concat_axis=0, tiled=True)
     result, residual = call(
         final_kernel,
         (jax.ShapeDtypeStruct(PLANE, F32),) * 2,

time: 148 us -> 146 us (0.986)
  waiting for transfers between devices: 20.3 us -> 18.8 us
    ppermute x1, waiting for transfers between devices: 1.72 us -> 0.21 us  [on_device(): xhi = lax.ppermute(first, 'gx', down_x)]
    pallas_call x12 -> x13, Pallas kernels: 17.4 us -> 18.4 us  [with_spaces(): run(*(x if spec is SMEM else pltpu.with_memory_space_constraint(x, spec.m...]
  transfers between devices with their start and end apart: 8 -> 8, of which waited for: 4 -> 4; matrix products, arithmetic and copies ran while one was open for 0% -> 0% of each run, Pallas kernels for 2% -> 3%
where the time goes in v6:
time: 146 us; the launch traced here: 145 us
  blocking collectives  92.2 us (63%)
  waiting for transfers between devices  18.8 us (13%)
  Pallas kernels  18.4 us (13%)
  starting transfers between devices  15 us (10%)
    all_to_all x1, blocking collectives, on_device(): got = lax.all_to_all(send, YZ, split_axis=0, concat_axis=0, tiled=True)  41.1 us
    all_to_all x2, blocking collectives, updated(): lax.all_to_all(ends, 'gx', split_axis=0, concat_axis=0, tiled=True)  24.8 us
    ppermute x3, waiting for transfers between devices, neighbours(): outer = lax.ppermute(value, YZ, off_chip)  18.6 us
    pallas_call x13, Pallas kernels, with_spaces(): run(*(x if spec is SMEM else pltpu.with_memory_space_constraint(x, spec.m...  18.4 us
    all_to_all x1, blocking collectives, on_device(): lax.all_to_all(sums, ('yz_0', 'yz_1'), split_axis=0, concat_axis=0, tiled...  17.5 us
    ppermute x3, starting transfers between devices, neighbours(): outer = lax.ppermute(value, YZ, off_chip)  9.93 us
    all_to_all x1, blocking collectives, on_device(): lax.all_to_all(sums, ('gx', 'yz_2'), split_axis=0, concat_axis=0, tiled=T...  8.8 us
    ppermute x1, starting transfers between devices, on_device(): xlo = lax.ppermute(last, 'gx', up_x)  3.54 us
  transfers between devices with their start and end apart: 8, of which 4 were waited for; matrix products, arithmetic and copies ran while one was open for 0% of the time, Pallas kernels for 3%

profile of v6, /device:TPU:1, one launch (start us, length us, event | category | flops | bytes accessed | tf_op | source)
XLA Modules:
  0.0 145.5 jit_solution(13007097759546254314)
XLA Ops:
  0.6 0.1 pad_add_fusion.place_ref
  0.7 4.2 %pack.1 = f32[32,152,128]{2,1,0:T(8,128)S(1)} custom-call(s32[2]{0:T(128)S(1)} %pad_add_fusion.place_ref, s32[1,64]{1,0:T(1,128)} %slot_hbm.1, f32[64,48,128]{2,1,0:T(8,128)} %bitcast.9, f32[64,16,128]{2,1,0:T(8,128)} %bitcast.10), custom_call_target="tpu_custom_call" | custom-call | tf_op jit(solution)/shard_map/pack/pallas_call | solution.py:519
  4.9 0.0 copy-start.8
  4.9 41.1 %all_to_all.25.got_ref = f32[32,152,128]{2,1,0:T(8,128)S(1)} all-to-all(f32[32,152,128]{2,1,0:T(8,128)S(1)} %pack.1), channel_id=1, replica_groups=mesh['gx'=8,'yz_0'=4,'yz_1'=4,'yz_2'=2] {'yz_0','yz_1','yz_2'}, dimensions={0} | all-to-all | bytes 4980736 | tf_op jit(solution)/shard_map/all_to_all | solution.py:567
  46.0 0.0 copy-done.8
  46.0 0.0 copy-start.2
  46.1 0.0 copy-start.7
  46.1 2.1 %place.1 = (f32[2,128,1024]{2,1,0:T(8,128)S(1)}, f32[2,1024]{1,0:T(2,128)S(1)}, f32[2,1024]{1,0:T(2,128)S(1)}, s32[1,128]{1,0:T(1,128)S(1)}) custom-call(s32[64]{0:T(128)S(1)} %bitcast.7, f32[32,152,128]{2,1,0:T(8,128)S(1)} %all_to_all.25.got_ref), custom_call_target="tpu_custom_call" | custom-call | tf_op jit(solution)/shard_map/place/pallas_call | solution.py:519
  48.2 1.9 %collective-permute-start.1 = (f32[2,128,1024]{2,1,0:T(8,128)S(1)}, f32[2,128,1024]{2,1,0:T(8,128)S(1)}, u32[]{:S(2)}, u32[]{:S(2)}) collective-permute-start(f32[2,128,1024]{2,1,0:T(8,128)S(1)} %get-tuple-element.31.z_ref), channel_id=1, source_target_pairs={{1,2},{2,1},{3,4},{4,3},{5,6},{6,5},{7,8},{8,7},{9,10},{10,9},{11,... | collective-permute-start | bytes 3145736 | tf_op jit(solution)/shard_map/ppermute | solution.py:545
  50.1 0.1 collective-permute-start
  50.2 3.5 %collective-permute-start.2 = (f32[2,1024]{1,0:T(2,128)S(1)}, f32[2,1024]{1,0:T(2,128)S(1)}, u32[]{:S(2)}, u32[]{:S(2)}) collective-permute-start(f32[2,1024]{1,0:T(2,128)S(1)} %get-tuple-element.38), channel_id=1, source_target_pairs={{0,32},{32,64},{64,96},{96,128},{128,160},{160,192},{192,224},{1,3... | collective-permute-start | bytes 24584 | tf_op jit(solution)/shard_map/ppermute | solution.py:577
  53.8 1.3 collective-permute-start.3
  55.1 0.0 copy-start
  55.1 0.0 copy-start.1
  55.1 0.0 copy-start.5
  55.1 1.5 %place_rest.1 = (f32[128,1024]{1,0:T(8,128)S(1)}, f32[128,1024]{1,0:T(8,128)S(1)}, f32[128,1024]{1,0:T(8,128)S(1)}) custom-call(s32[64]{0:T(128)S(1)} %bitcast.8, s32[1,128]{1,0:T(1,128)S(1)} %get-tuple-element.32.from_ref, f32[32,152,128]{2,1,0:T(8,128)S(1)} %all_to_all.25.got_ref), custom_call_target="tpu_custom_call" | custom-call | tf_op jit(solution)/shard_map/place_rest/pallas_call | solution.py:519
  56.6 0.0 copy-done.2
  56.6 0.0 copy-done.7
  56.6 1.5 %prepare.1 = (f32[128,1024]{1,0:T(8,128)S(1)}, f32[128,1024]{1,0:T(8,128)S(1)}, f32[128,1024]{1,0:T(8,128)S(1)}) custom-call(f32[2,128,1024]{2,1,0:T(8,128)S(1)} %get-tuple-element.31.z_ref, f32[128,1024]{1,0:T(8,128)S(1)} %get-tuple-element.33.inner_ref, f32[128,1024]{1,0:T(8,128)S(1)} %get-tuple-element.34.x_ends_ref, ...), custom_call_target="tpu_custom_call" | custom-call | tf_op jit(solution)/shard_map/prepare/pallas_call | solution.py:519
  58.1 0.0 collective-permute-done.2.xlo_ref
  58.1 0.2 collective-permute-done.3.xhi_ref
  58.3 6.0 %collective-permute-done.1.outer_ref = f32[2,128,1024]{2,1,0:T(8,128)S(1)} collective-permute-done((f32[2,128,1024]{2,1,0:T(8,128)S(1)}, f32[2,128,1024]{2,1,0:T(8,128)S(1)}, u32[]{:S(2)}, u32[]{:S(2)}) %collective-permute-start.1) | collective-permute-done | bytes 1048608 | tf_op jit(solution)/shard_map/ppermute | solution.py:545
  64.3 0.0 collective-permute-done.partner_ref
  64.3 0.0 copy-done
  64.3 0.0 copy-done.1
  64.3 0.0 copy-done.5
  64.3 0.0 copy-start.3
  64.3 0.0 copy-start.4
  64.3 0.0 copy-start.6
  64.4 1.9 %setup.1 = (f32[128,1024]{1,0:T(8,128)S(1)}, f32[128,1024]{1,0:T(8,128)S(1)}, f32[128,1024]{1,0:T(8,128)S(1)}, f32[8,16,128]{2,1,0:T(8,128)S(1)}) custom-call(s32[2]{0:T(128)S(1)} %pad_add_fusion.place_ref, f32[2,128,1024]{2,1,0:T(8,128)S(1)} %get-tuple-element.31.z_ref, f32[128,1024]{1,0:T(8,128)S(1)} %get-tuple-element.36.beside_ref, ...), custom_call_target="tpu_custom_call" | custom-call | tf_op jit(solution)/shard_map/setup/pallas_call | solution.py:519
  66.2 15.2 %all_to_all.26.all_ends_ref = f32[8,16,128]{2,1,0:T(8,128)S(1)} all-to-all(f32[8,16,128]{2,1,0:T(8,128)S(1)} %get-tuple-element.42), channel_id=1, replica_groups=mesh['gx'=8,'yz_0'=4,'yz_1'=4,'yz_2'=2] {'gx'}, dimensions={0} | all-to-all | bytes 131072 | tf_op jit(solution)/shard_map/all_to_all | solution.py:597
  81.5 0.0 copy-done.3
  81.5 0.0 copy-done.4
  81.5 0.0 copy-done.6
  81.5 1.7 %update.2 = (f32[128,1024]{1,0:T(8,128)S(1)}, f32[128,1024]{1,0:T(8,128)S(1)}, f32[2,1024]{1,0:T(2,128)S(1)}) custom-call(s32[2]{0:T(128)S(1)} %pad_add_fusion.place_ref, f32[128,1024]{1,0:T(8,128)S(1)} %get-tuple-element.41.modes_ref, f32[8,16,128]{2,1,0:T(8,128)S(1)} %all_to_all.26.all_ends_ref, f32[2,128,1024]{2,1,0:T(8,128)S(1)} %get-tuple-element.31.z_ref, ...), custom_call_target="tpu_custom_call" | custom-call | tf_op jit(solution)/shard_map/update/pallas_call | solution.py:519
  83.2 3.4 %collective-permute-start.5 = (f32[128,1024]{1,0:T(8,128)S(1)}, f32[128,1024]{1,0:T(8,128)S(1)}, u32[]{:S(2)}, u32[]{:S(2)}) collective-permute-start(f32[128,1024]{1,0:T(8,128)S(1)} %get-tuple-element.44.scaled_ref), channel_id=1, source_target_pairs={{1,2},{2,1},{3,4},{4,3},{5,6},{6,5},{7,8},{8,7},{9,10},{10,9},{11,... | collective-permute-start | bytes 1572872 | tf_op jit(solution)/shard_map/ppermute | solution.py:545
  86.6 0.1 collective-permute-start.4
  86.7 0.4 own.1.own_ref
  87.2 6.5 %collective-permute-done.5.outer_ref = f32[128,1024]{1,0:T(8,128)S(1)} collective-permute-done((f32[128,1024]{1,0:T(8,128)S(1)}, f32[128,1024]{1,0:T(8,128)S(1)}, u32[]{:S(2)}, u32[]{:S(2)}) %collective-permute-start.5) | collective-permute-done | bytes 524320 | tf_op jit(solution)/shard_map/ppermute | solution.py:545
  93.7 0.0 collective-permute-done.4.partner_ref
  93.7 1.2 image.1
  94.9 9.6 %all_to_all.27.all_ends_ref = f32[8,16,128]{2,1,0:T(8,128)S(1)} all-to-all(f32[8,16,128]{2,1,0:T(8,128)S(1)} %get-tuple-element.48), channel_id=1, replica_groups=mesh['gx'=8,'yz_0'=4,'yz_1'=4,'yz_2'=2] {'gx'}, dimensions={0} | all-to-all | bytes 131072 | tf_op jit(solution)/shard_map/all_to_all | solution.py:597
  104.5 1.7 %update.3 = (f32[128,1024]{1,0:T(8,128)S(1)}, f32[128,1024]{1,0:T(8,128)S(1)}, f32[2,1024]{1,0:T(2,128)S(1)}) custom-call(s32[2]{0:T(128)S(1)} %pad_add_fusion.place_ref, f32[128,1024]{1,0:T(8,128)S(1)} %get-tuple-element.47.modes_ref, f32[8,16,128]{2,1,0:T(8,128)S(1)} %all_to_all.27.all_ends_ref, f32[2,128,1024]{2,1,0:T(8,128)S(1)} %get-tuple-element.31.z_ref, ...), custom_call_target="tpu_custom_call" | custom-call | tf_op jit(solution)/shard_map/update/pallas_call | solution.py:519
  106.2 4.6 %collective-permute-start.7 = (f32[128,1024]{1,0:T(8,128)S(1)}, f32[128,1024]{1,0:T(8,128)S(1)}, u32[]{:S(2)}, u32[]{:S(2)}) collective-permute-start(f32[128,1024]{1,0:T(8,128)S(1)} %get-tuple-element.50.scaled_ref), channel_id=1, source_target_pairs={{1,2},{2,1},{3,4},{4,3},{5,6},{6,5},{7,8},{8,7},{9,10},{10,9},{11,... | collective-permute-start | bytes 1572872 | tf_op jit(solution)/shard_map/ppermute | solution.py:545
  110.8 0.1 collective-permute-start.6
  110.9 0.7 own_sums.1
  111.5 6.1 %collective-permute-done.7.outer_ref = f32[128,1024]{1,0:T(8,128)S(1)} collective-permute-done((f32[128,1024]{1,0:T(8,128)S(1)}, f32[128,1024]{1,0:T(8,128)S(1)}, u32[]{:S(2)}, u32[]{:S(2)}) %collective-permute-start.7) | collective-permute-done | bytes 524320 | tf_op jit(solution)/shard_map/ppermute | solution.py:545
  117.6 0.0 collective-permute-done.6.partner_ref
  117.6 0.3 sums.1
  117.9 8.8 %all_to_all.28.sums_ref = f32[16,1,128]{2,1,0:T(1,128)S(1)} all-to-all(f32[16,1,128]{2,1,0:T(1,128)S(1)} %get-tuple-element.56), channel_id=1, replica_groups=mesh['gx'=8,'yz_0'=4,'yz_1'=4,'yz_2'=2] {'gx','yz_2'}, dimensions={0} | all-to-all | bytes 16384 | tf_op jit(solution)/shard_map/all_to_all | solution.py:633
  126.7 17.5 %all_to_all.29.sums_ref = f32[16,1,128]{2,1,0:T(1,128)S(1)} all-to-all(f32[16,1,128]{2,1,0:T(1,128)S(1)} %add.3), channel_id=1, replica_groups=mesh['gx'=8,'yz_0'=4,'yz_1'=4,'yz_2'=2] {'yz_0','yz_1'}, dimensions={0} | all-to-all | bytes 16384 | tf_op jit(solution)/shard_map/all_to_all | solution.py:635
  144.2 1.2 final.1
  (1 shorter events, 0.0 us)
Async XLA Ops:
  4.9 41.1 %copy-start.8 = (s32[1,64]{1,0:T(1,128)S(1)}, s32[1,64]{1,0:T(1,128)}, u32[]{:S(2)}) copy-start(s32[1,64]{1,0:T(1,128)} %param.15) | copy-start | bytes 772
  46.0 10.5 %copy-start.2 = (f32[128,128]{1,0:T(8,128)S(1)}, f32[128,128]{1,0:T(8,128)}, u32[]{:S(2)}) copy-start(f32[128,128]{1,0:T(8,128)} %constant.30.clone.column_ref) | copy-start | bytes 196612
  46.1 10.5 %copy-start.7 = (f32[1,1024]{1,0:T(1,128)S(1)}, f32[1,1024]{1,0:T(1,128)}, u32[]{:S(2)}) copy-start(f32[1,1024]{1,0:T(1,128)} %constant.31.clone.lam_ref) | copy-start | bytes 12292
  48.2 16.1 %collective-permute-start.1 = (f32[2,128,1024]{2,1,0:T(8,128)S(1)}, f32[2,128,1024]{2,1,0:T(8,128)S(1)}, u32[]{:S(2)}, u32[]{:S(2)}) collective-permute-start(f32[2,128,1024]{2,1,0:T(8,128)S(1)} %get-tuple-element.31.z_ref), channel_id=1, source_target_pairs={{1,2},{2,1},{3,4},{4,3},{5,6},{6,5},{7,8},{8,7},{9,10},{10,9},{11,... | collective-permute-start | bytes 3145736 | tf_op jit(solution)/shard_map/ppermute | solution.py:545
  50.1 14.2 %collective-permute-start = (f32[2,128,1024]{2,1,0:T(8,128)S(1)}, f32[2,128,1024]{2,1,0:T(8,128)S(1)}, u32[]{:S(2)}, u32[]{:S(2)}) collective-permute-start(f32[2,128,1024]{2,1,0:T(8,128)S(1)} %get-tuple-element.31.z_ref), channel_id=1, source_target_pairs={{0,1},{1,0},{2,3},{3,2},{4,5},{5,4},{6,7},{7,6},{8,9},{9,8},{10,11... | collective-permute-start | bytes 3145736 | tf_op jit(solution)/shard_map/ppermute | solution.py:546
  50.2 7.9 %collective-permute-start.2 = (f32[2,1024]{1,0:T(2,128)S(1)}, f32[2,1024]{1,0:T(2,128)S(1)}, u32[]{:S(2)}, u32[]{:S(2)}) collective-permute-start(f32[2,1024]{1,0:T(2,128)S(1)} %get-tuple-element.38), channel_id=1, source_target_pairs={{0,32},{32,64},{64,96},{96,128},{128,160},{160,192},{192,224},{1,3... | collective-permute-start | bytes 24584 | tf_op jit(solution)/shard_map/ppermute | solution.py:577
  53.8 4.6 %collective-permute-start.3 = (f32[2,1024]{1,0:T(2,128)S(1)}, f32[2,1024]{1,0:T(2,128)S(1)}, u32[]{:S(2)}, u32[]{:S(2)}) collective-permute-start(f32[2,1024]{1,0:T(2,128)S(1)} %get-tuple-element.39), channel_id=1, source_target_pairs={{32,0},{64,32},{96,64},{128,96},{160,128},{192,160},{224,192},{33,... | collective-permute-start | bytes 24584 | tf_op jit(solution)/shard_map/ppermute | solution.py:578
  55.1 9.2 %copy-start = (bf16[2,512,512]{2,1,0:T(8,128)(2,1)S(1)}, bf16[2,512,512]{2,1,0:T(8,128)(2,1)}, u32[]{:S(2)}) copy-start(bf16[2,512,512]{2,1,0:T(8,128)(2,1)} %constant.27.clone.odd_ref) | copy-start | bytes 3145732
  55.1 9.2 %copy-start.1 = (bf16[2,512,512]{2,1,0:T(8,128)(2,1)S(1)}, bf16[2,512,512]{2,1,0:T(8,128)(2,1)}, u32[]{:S(2)}) copy-start(bf16[2,512,512]{2,1,0:T(8,128)(2,1)} %constant.26.clone.even_ref) | copy-start | bytes 3145732
  55.1 9.2 %copy-start.5 = (bf16[256,128]{1,0:T(8,128)(2,1)S(1)}, bf16[256,128]{1,0:T(8,128)(2,1)}, u32[]{:S(2)}) copy-start(bf16[256,128]{1,0:T(8,128)(2,1)} %constant.28.clone.small_ref) | copy-start | bytes 196612
  64.3 17.1 %copy-start.3 = (f32[7,7,8,128]{3,2,1,0:T(8,128)S(1)}, f32[7,7,8,128]{3,2,1,0:T(8,128)}, u32[]{:S(2)}) copy-start(f32[7,7,8,128]{3,2,1,0:T(8,128)} %constant.32.clone.cut_ref) | copy-start | bytes 602116
  64.3 17.1 %copy-start.4 = (bf16[256,128]{1,0:T(8,128)(2,1)S(1)}, bf16[256,128]{1,0:T(8,128)(2,1)}, u32[]{:S(2)}) copy-start(bf16[256,128]{1,0:T(8,128)(2,1)} %constant.29.clone.small_t_ref) | copy-start | bytes 196612
  64.3 17.1 %copy-start.6 = (f32[2,8,128]{2,1,0:T(8,128)S(1)}, f32[2,8,128]{2,1,0:T(8,128)}, u32[]{:S(2)}) copy-start(f32[2,8,128]{2,1,0:T(8,128)} %constant.33.clone.near_far_ref) | copy-start | bytes 24580
  83.2 10.5 %collective-permute-start.5 = (f32[128,1024]{1,0:T(8,128)S(1)}, f32[128,1024]{1,0:T(8,128)S(1)}, u32[]{:S(2)}, u32[]{:S(2)}) collective-permute-start(f32[128,1024]{1,0:T(8,128)S(1)} %get-tuple-element.44.scaled_ref), channel_id=1, source_target_pairs={{1,2},{2,1},{3,4},{4,3},{5,6},{6,5},{7,8},{8,7},{9,10},{10,9},{11,... | collective-permute-start | bytes 1572872 | tf_op jit(solution)/shard_map/ppermute | solution.py:545
  86.6 7.1 %collective-permute-start.4 = (f32[128,1024]{1,0:T(8,128)S(1)}, f32[128,1024]{1,0:T(8,128)S(1)}, u32[]{:S(2)}, u32[]{:S(2)}) collective-permute-start(f32[128,1024]{1,0:T(8,128)S(1)} %get-tuple-element.44.scaled_ref), channel_id=1, source_target_pairs={{0,1},{1,0},{2,3},{3,2},{4,5},{5,4},{6,7},{7,6},{8,9},{9,8},{10,11... | collective-permute-start | bytes 1572872 | tf_op jit(solution)/shard_map/ppermute | solution.py:546
  106.2 11.4 %collective-permute-start.7 = (f32[128,1024]{1,0:T(8,128)S(1)}, f32[128,1024]{1,0:T(8,128)S(1)}, u32[]{:S(2)}, u32[]{:S(2)}) collective-permute-start(f32[128,1024]{1,0:T(8,128)S(1)} %get-tuple-element.50.scaled_ref), channel_id=1, source_target_pairs={{1,2},{2,1},{3,4},{4,3},{5,6},{6,5},{7,8},{8,7},{9,10},{10,9},{11,... | collective-permute-start | bytes 1572872 | tf_op jit(solution)/shard_map/ppermute | solution.py:545
  110.8 6.9 %collective-permute-start.6 = (f32[128,1024]{1,0:T(8,128)S(1)}, f32[128,1024]{1,0:T(8,128)S(1)}, u32[]{:S(2)}, u32[]{:S(2)}) collective-permute-start(f32[128,1024]{1,0:T(8,128)S(1)} %get-tuple-element.50.scaled_ref), channel_id=1, source_target_pairs={{0,1},{1,0},{2,3},{3,2},{4,5},{5,4},{6,7},{7,6},{8,9},{9,8},{10,11... | collective-permute-start | bytes 1572872 | tf_op jit(solution)/shard_map/ppermute | solution.py:546

commit v7 on v6

--- a/solution.py
+++ b/solution.py
@@ -68,7 +68,6 @@
     column = np.zeros((XL, 128), np.float32)
     column[:, 0] = lam_x + FLOOR
     column[:, 1] = small[:, 0]
-    column[:, 2] = small[:, XL - 1]
     out["column"] = column
     out["lam_y"] = lam_y.astype(np.float32)[None]
     denom = lam_x[:, None] + lam_y[None] + FLOOR
@@ -143,16 +142,15 @@
         axis=1,
     )
     modes_ref[...] = of_table(small_ref, spectrum)
-    first = jnp.zeros((8, N), F32)
-    last = jnp.zeros((8, N), F32)
+    total = jnp.zeros((8, N), F32)
     for i in range(XL // 8):
         rows = pl.ds(8 * i, 8)
         modes = modes_ref[rows, :] * inverse_ref[rows]
         modes_ref[rows, :] = modes
-        first = first + modes * column_ref[rows, 1:2]
-        last = last + modes * column_ref[rows, 2:3]
-    first = as_tile(jnp.sum(first, axis=0, keepdims=True))
-    last = as_tile(jnp.sum(last, axis=0, keepdims=True))
+        total = total + modes * column_ref[rows, 1:2]
+    odd = (lax.broadcasted_iota(jnp.int32, (8, N), 0) & 1) == 1
+    first = as_tile(jnp.sum(total, axis=0, keepdims=True))
+    last = as_tile(jnp.sum(jnp.where(odd, -total, total), axis=0, keepdims=True))
     for j in range(SLABS):
         ends_ref[j, 0:8] = first
         ends_ref[j, 8:16] = last
@@ -199,7 +197,7 @@
     row = lax.broadcasted_iota(jnp.int32, dims, 1)
     few_lanes, few_rows = lane[0, :8], row[0, :8]
     edge = jnp.where((few_rows == 0) & (few_lanes == 0), 1.0, 0.0)
-    edge = jnp.where((few_rows == 1) & (few_lanes == B - 1), 1.0, edge)
+    edge = jnp.where((few_rows == 1) & (few_lanes == B - 1), 1.0, edge).astype(BF16)
 
     def inside(group, carry):
         bricks = pl.ds(group * GROUP, GROUP)
@@ -213,10 +211,10 @@
         flux_y = root * pltpu.roll(root, B - 1, 2) * (accel_y + pltpu.roll(accel_y, B - 1, 2))
         flux_y = jnp.where(lane < B - 1, flux_y, 0.0)
         inner_ref[bricks] = 0.5 * (inner + pltpu.roll(flux_y, 1, 2) - flux_y)
-        sides = lax.dot_general(
-            edge, accel_y.reshape(GROUP * BR, B), (((1,), (1,)), ((), ())),
-            precision=lax.Precision.HIGHEST, preferred_element_type=F32,
-        )
+        flat = accel_y.reshape(GROUP * BR, B)
+        high, middle = split(flat)
+        low = (flat - high.astype(F32) - middle.astype(F32)).astype(BF16)
+        sides = product(edge, high, True) + product(edge, middle, True) + product(edge, low, True)
         side_ref[group] = jnp.where(few_rows == 1, pltpu.roll(sides, BR, 1), sides)
         return carry
 
@@ -243,7 +241,7 @@
         out_ref[owner, END_ROW:] = ends
         return carry
 
-    lax.fori_loop(0, OWNERS, fill, 0, unroll=4)
+    lax.fori_loop(0, OWNERS, fill, 0, unroll=8)
 
 
 def place_kernel(solid_ref, got_ref, z_ref, first_ref, last_ref, from_ref, origin_ref, sem):
@@ -369,10 +367,11 @@
     before = all_ends_ref[jnp.maximum(slab - 1, 0), 8:16] - (near * low - far * farther_low)
     after = all_ends_ref[jnp.minimum(slab + 1, SLABS - 1), 0:8] - (far * farther_high - near * high)
     low_row, high_row = as_row(low), as_row(high)
-    for i in range(XL // 8):
-        rows = pl.ds(8 * i, 8)
-        change = column_ref[rows, 2:3] * high_row - column_ref[rows, 1:2] * low_row
-        work_ref[rows] = modes_ref[rows] - change * inverse_ref[rows]
+    odd = (lax.broadcasted_iota(jnp.int32, (8, N), 0) & 1) == 1
+    jumps = jnp.where(odd, -high_row, high_row) - low_row
+    for i in range(XL // 8):
+        rows = pl.ds(8 * i, 8)
+        work_ref[rows] = modes_ref[rows] - column_ref[rows, 1:2] * jumps * inverse_ref[rows]
     work_ref[0:XL] = of_table(small_t_ref, work_ref[0:XL])
     work_ref[XL : XL + 8] = jnp.concatenate([as_row(before), as_row(after), jnp.zeros((6, N), F32)], axis=0)
     even = by_table(work_ref[:, :H], even_ref, False)

time: 146 us -> 145 us (level)
  no operation moved by 1% of the time
where the time goes in v7:
time: 145 us
  blocking collectives  92.2 us (64%)
  waiting for transfers between devices  18.8 us (13%)
  Pallas kernels  17.6 us (12%)
  starting transfers between devices  15 us (10%)
    all_to_all x1, blocking collectives, on_device(): got = lax.all_to_all(send, YZ, split_axis=0, concat_axis=0, tiled=True)  41.1 us
    all_to_all x2, blocking collectives, updated(): lax.all_to_all(ends, 'gx', split_axis=0, concat_axis=0, tiled=True)  24.8 us
    ppermute x3, waiting for transfers between devices, neighbours(): outer = lax.ppermute(value, YZ, off_chip)  18.6 us
    pallas_call x13, Pallas kernels, with_spaces(): run(*(x if spec is SMEM else pltpu.with_memory_space_constraint(x, spec.m...  17.6 us
    all_to_all x1, blocking collectives, on_device(): lax.all_to_all(sums, ('yz_0', 'yz_1'), split_axis=0, concat_axis=0, tiled...  17.5 us
    ppermute x3, starting transfers between devices, neighbours(): outer = lax.ppermute(value, YZ, off_chip)  9.92 us
    all_to_all x1, blocking collectives, on_device(): lax.all_to_all(sums, ('gx', 'yz_2'), split_axis=0, concat_axis=0, tiled=T...  8.8 us
    ppermute x1, starting transfers between devices, on_device(): xlo = lax.ppermute(last, 'gx', up_x)  3.54 us
  transfers between devices with their start and end apart: 8, of which 4 were waited for; matrix products, arithmetic and copies ran while one was open for 0% of the time, Pallas kernels for 3%

profile of v7, /device:TPU:1, one launch (start us, length us, event | category | flops | bytes accessed | tf_op | source)
XLA Modules:
  0.0 144.7 jit_solution(11711312580708310452)
XLA Ops:
  0.6 0.1 pad_add_fusion.place_ref
  0.7 3.6 %pack.1 = f32[32,152,128]{2,1,0:T(8,128)S(1)} custom-call(s32[2]{0:T(128)S(1)} %pad_add_fusion.place_ref, s32[1,64]{1,0:T(1,128)} %slot_hbm.1, f32[64,48,128]{2,1,0:T(8,128)} %bitcast.9, f32[64,16,128]{2,1,0:T(8,128)} %bitcast.10), custom_call_target="tpu_custom_call" | custom-call | tf_op jit(solution)/shard_map/pack/pallas_call | solution.py:518
  4.3 0.0 copy-start.8
  4.3 41.1 %all_to_all.25.got_ref = f32[32,152,128]{2,1,0:T(8,128)S(1)} all-to-all(f32[32,152,128]{2,1,0:T(8,128)S(1)} %pack.1), channel_id=1, replica_groups=mesh['gx'=8,'yz_0'=4,'yz_1'=4,'yz_2'=2] {'yz_0','yz_1','yz_2'}, dimensions={0} | all-to-all | bytes 4980736 | tf_op jit(solution)/shard_map/all_to_all | solution.py:566
  45.4 0.0 copy-done.8
  45.4 0.0 copy-start.2
  45.4 0.0 copy-start.7
  45.4 2.1 %place.1 = (f32[2,128,1024]{2,1,0:T(8,128)S(1)}, f32[2,1024]{1,0:T(2,128)S(1)}, f32[2,1024]{1,0:T(2,128)S(1)}, s32[1,128]{1,0:T(1,128)S(1)}) custom-call(s32[64]{0:T(128)S(1)} %bitcast.7, f32[32,152,128]{2,1,0:T(8,128)S(1)} %all_to_all.25.got_ref), custom_call_target="tpu_custom_call" | custom-call | tf_op jit(solution)/shard_map/place/pallas_call | solution.py:518
  47.6 1.9 %collective-permute-start.1 = (f32[2,128,1024]{2,1,0:T(8,128)S(1)}, f32[2,128,1024]{2,1,0:T(8,128)S(1)}, u32[]{:S(2)}, u32[]{:S(2)}) collective-permute-start(f32[2,128,1024]{2,1,0:T(8,128)S(1)} %get-tuple-element.31.z_ref), channel_id=1, source_target_pairs={{1,2},{2,1},{3,4},{4,3},{5,6},{6,5},{7,8},{8,7},{9,10},{10,9},{11,... | collective-permute-start | bytes 3145736 | tf_op jit(solution)/shard_map/ppermute | solution.py:544
  49.5 0.1 collective-permute-start
  49.6 3.5 %collective-permute-start.2 = (f32[2,1024]{1,0:T(2,128)S(1)}, f32[2,1024]{1,0:T(2,128)S(1)}, u32[]{:S(2)}, u32[]{:S(2)}) collective-permute-start(f32[2,1024]{1,0:T(2,128)S(1)} %get-tuple-element.38), channel_id=1, source_target_pairs={{0,32},{32,64},{64,96},{96,128},{128,160},{160,192},{192,224},{1,3... | collective-permute-start | bytes 24584 | tf_op jit(solution)/shard_map/ppermute | solution.py:576
  53.1 1.3 collective-permute-start.3
  54.4 0.0 copy-start
  54.4 0.0 copy-start.1
  54.5 0.0 copy-start.5
  54.5 1.5 %place_rest.1 = (f32[128,1024]{1,0:T(8,128)S(1)}, f32[128,1024]{1,0:T(8,128)S(1)}, f32[128,1024]{1,0:T(8,128)S(1)}) custom-call(s32[64]{0:T(128)S(1)} %bitcast.8, s32[1,128]{1,0:T(1,128)S(1)} %get-tuple-element.32.from_ref, f32[32,152,128]{2,1,0:T(8,128)S(1)} %all_to_all.25.got_ref), custom_call_target="tpu_custom_call" | custom-call | tf_op jit(solution)/shard_map/place_rest/pallas_call | solution.py:518
  55.9 0.0 copy-done.2
  56.0 0.0 copy-done.7
  56.0 1.5 %prepare.1 = (f32[128,1024]{1,0:T(8,128)S(1)}, f32[128,1024]{1,0:T(8,128)S(1)}, f32[128,1024]{1,0:T(8,128)S(1)}) custom-call(f32[2,128,1024]{2,1,0:T(8,128)S(1)} %get-tuple-element.31.z_ref, f32[128,1024]{1,0:T(8,128)S(1)} %get-tuple-element.33.inner_ref, f32[128,1024]{1,0:T(8,128)S(1)} %get-tuple-element.34.x_ends_ref, ...), custom_call_target="tpu_custom_call" | custom-call | tf_op jit(solution)/shard_map/prepare/pallas_call | solution.py:518
  57.5 0.0 collective-permute-done.2.xlo_ref
  57.5 0.2 collective-permute-done.3.xhi_ref
  57.7 6.0 %collective-permute-done.1.outer_ref = f32[2,128,1024]{2,1,0:T(8,128)S(1)} collective-permute-done((f32[2,128,1024]{2,1,0:T(8,128)S(1)}, f32[2,128,1024]{2,1,0:T(8,128)S(1)}, u32[]{:S(2)}, u32[]{:S(2)}) %collective-permute-start.1) | collective-permute-done | bytes 1048608 | tf_op jit(solution)/shard_map/ppermute | solution.py:544
  63.7 0.0 collective-permute-done.partner_ref
  63.7 0.0 copy-done
  63.7 0.0 copy-done.1
  63.7 0.0 copy-done.5
  63.7 0.0 copy-start.3
  63.7 0.0 copy-start.4
  63.7 0.0 copy-start.6
  63.7 1.8 %setup.1 = (f32[128,1024]{1,0:T(8,128)S(1)}, f32[128,1024]{1,0:T(8,128)S(1)}, f32[128,1024]{1,0:T(8,128)S(1)}, f32[8,16,128]{2,1,0:T(8,128)S(1)}) custom-call(s32[2]{0:T(128)S(1)} %pad_add_fusion.place_ref, f32[2,128,1024]{2,1,0:T(8,128)S(1)} %get-tuple-element.31.z_ref, f32[128,1024]{1,0:T(8,128)S(1)} %get-tuple-element.36.beside_ref, ...), custom_call_target="tpu_custom_call" | custom-call | tf_op jit(solution)/shard_map/setup/pallas_call | solution.py:518
  65.6 15.2 %all_to_all.26.all_ends_ref = f32[8,16,128]{2,1,0:T(8,128)S(1)} all-to-all(f32[8,16,128]{2,1,0:T(8,128)S(1)} %get-tuple-element.42), channel_id=1, replica_groups=mesh['gx'=8,'yz_0'=4,'yz_1'=4,'yz_2'=2] {'gx'}, dimensions={0} | all-to-all | bytes 131072 | tf_op jit(solution)/shard_map/all_to_all | solution.py:596
  80.8 0.0 copy-done.3
  80.8 0.0 copy-done.4
  80.8 0.0 copy-done.6
  80.8 1.7 %update.2 = (f32[128,1024]{1,0:T(8,128)S(1)}, f32[128,1024]{1,0:T(8,128)S(1)}, f32[2,1024]{1,0:T(2,128)S(1)}) custom-call(s32[2]{0:T(128)S(1)} %pad_add_fusion.place_ref, f32[128,1024]{1,0:T(8,128)S(1)} %get-tuple-element.41.modes_ref, f32[8,16,128]{2,1,0:T(8,128)S(1)} %all_to_all.26.all_ends_ref, f32[2,128,1024]{2,1,0:T(8,128)S(1)} %get-tuple-element.31.z_ref, ...), custom_call_target="tpu_custom_call" | custom-call | tf_op jit(solution)/shard_map/update/pallas_call | solution.py:518
  82.5 3.4 %collective-permute-start.5 = (f32[128,1024]{1,0:T(8,128)S(1)}, f32[128,1024]{1,0:T(8,128)S(1)}, u32[]{:S(2)}, u32[]{:S(2)}) collective-permute-start(f32[128,1024]{1,0:T(8,128)S(1)} %get-tuple-element.44.scaled_ref), channel_id=1, source_target_pairs={{1,2},{2,1},{3,4},{4,3},{5,6},{6,5},{7,8},{8,7},{9,10},{10,9},{11,... | collective-permute-start | bytes 1572872 | tf_op jit(solution)/shard_map/ppermute | solution.py:544
  85.9 0.1 collective-permute-start.4
  86.0 0.4 own.1.own_ref
  86.5 6.5 %collective-permute-done.5.outer_ref = f32[128,1024]{1,0:T(8,128)S(1)} collective-permute-done((f32[128,1024]{1,0:T(8,128)S(1)}, f32[128,1024]{1,0:T(8,128)S(1)}, u32[]{:S(2)}, u32[]{:S(2)}) %collective-permute-start.5) | collective-permute-done | bytes 524320 | tf_op jit(solution)/shard_map/ppermute | solution.py:544
  93.0 0.0 collective-permute-done.4.partner_ref
  93.0 1.1 image.1
  94.1 9.6 %all_to_all.27.all_ends_ref = f32[8,16,128]{2,1,0:T(8,128)S(1)} all-to-all(f32[8,16,128]{2,1,0:T(8,128)S(1)} %get-tuple-element.48), channel_id=1, replica_groups=mesh['gx'=8,'yz_0'=4,'yz_1'=4,'yz_2'=2] {'gx'}, dimensions={0} | all-to-all | bytes 131072 | tf_op jit(solution)/shard_map/all_to_all | solution.py:596
  103.7 1.7 %update.3 = (f32[128,1024]{1,0:T(8,128)S(1)}, f32[128,1024]{1,0:T(8,128)S(1)}, f32[2,1024]{1,0:T(2,128)S(1)}) custom-call(s32[2]{0:T(128)S(1)} %pad_add_fusion.place_ref, f32[128,1024]{1,0:T(8,128)S(1)} %get-tuple-element.47.modes_ref, f32[8,16,128]{2,1,0:T(8,128)S(1)} %all_to_all.27.all_ends_ref, f32[2,128,1024]{2,1,0:T(8,128)S(1)} %get-tuple-element.31.z_ref, ...), custom_call_target="tpu_custom_call" | custom-call | tf_op jit(solution)/shard_map/update/pallas_call | solution.py:518
  105.4 4.6 %collective-permute-start.7 = (f32[128,1024]{1,0:T(8,128)S(1)}, f32[128,1024]{1,0:T(8,128)S(1)}, u32[]{:S(2)}, u32[]{:S(2)}) collective-permute-start(f32[128,1024]{1,0:T(8,128)S(1)} %get-tuple-element.50.scaled_ref), channel_id=1, source_target_pairs={{1,2},{2,1},{3,4},{4,3},{5,6},{6,5},{7,8},{8,7},{9,10},{10,9},{11,... | collective-permute-start | bytes 1572872 | tf_op jit(solution)/shard_map/ppermute | solution.py:544
  110.0 0.1 collective-permute-start.6
  110.1 0.7 own_sums.1
  110.8 6.1 %collective-permute-done.7.outer_ref = f32[128,1024]{1,0:T(8,128)S(1)} collective-permute-done((f32[128,1024]{1,0:T(8,128)S(1)}, f32[128,1024]{1,0:T(8,128)S(1)}, u32[]{:S(2)}, u32[]{:S(2)}) %collective-permute-start.7) | collective-permute-done | bytes 524320 | tf_op jit(solution)/shard_map/ppermute | solution.py:544
  116.9 0.0 collective-permute-done.6.partner_ref
  116.9 0.3 sums.1
  117.2 8.8 %all_to_all.28.sums_ref = f32[16,1,128]{2,1,0:T(1,128)S(1)} all-to-all(f32[16,1,128]{2,1,0:T(1,128)S(1)} %get-tuple-element.56), channel_id=1, replica_groups=mesh['gx'=8,'yz_0'=4,'yz_1'=4,'yz_2'=2] {'gx','yz_2'}, dimensions={0} | all-to-all | bytes 16384 | tf_op jit(solution)/shard_map/all_to_all | solution.py:632
  126.0 17.5 %all_to_all.29.sums_ref = f32[16,1,128]{2,1,0:T(1,128)S(1)} all-to-all(f32[16,1,128]{2,1,0:T(1,128)S(1)} %add.3), channel_id=1, replica_groups=mesh['gx'=8,'yz_0'=4,'yz_1'=4,'yz_2'=2] {'yz_0','yz_1'}, dimensions={0} | all-to-all | bytes 16384 | tf_op jit(solution)/shard_map/all_to_all | solution.py:634
  143.5 1.2 final.1
  (1 shorter events, 0.0 us)
Async XLA Ops:
  4.3 41.1 %copy-start.8 = (s32[1,64]{1,0:T(1,128)S(1)}, s32[1,64]{1,0:T(1,128)}, u32[]{:S(2)}) copy-start(s32[1,64]{1,0:T(1,128)} %param.15) | copy-start | bytes 772
  45.4 10.5 %copy-start.2 = (f32[128,128]{1,0:T(8,128)S(1)}, f32[128,128]{1,0:T(8,128)}, u32[]{:S(2)}) copy-start(f32[128,128]{1,0:T(8,128)} %constant.30.clone.column_ref) | copy-start | bytes 196612
  45.4 10.5 %copy-start.7 = (f32[1,1024]{1,0:T(1,128)S(1)}, f32[1,1024]{1,0:T(1,128)}, u32[]{:S(2)}) copy-start(f32[1,1024]{1,0:T(1,128)} %constant.31.clone.lam_ref) | copy-start | bytes 12292
  47.6 16.1 %collective-permute-start.1 = (f32[2,128,1024]{2,1,0:T(8,128)S(1)}, f32[2,128,1024]{2,1,0:T(8,128)S(1)}, u32[]{:S(2)}, u32[]{:S(2)}) collective-permute-start(f32[2,128,1024]{2,1,0:T(8,128)S(1)} %get-tuple-element.31.z_ref), channel_id=1, source_target_pairs={{1,2},{2,1},{3,4},{4,3},{5,6},{6,5},{7,8},{8,7},{9,10},{10,9},{11,... | collective-permute-start | bytes 3145736 | tf_op jit(solution)/shard_map/ppermute | solution.py:544
  49.5 14.2 %collective-permute-start = (f32[2,128,1024]{2,1,0:T(8,128)S(1)}, f32[2,128,1024]{2,1,0:T(8,128)S(1)}, u32[]{:S(2)}, u32[]{:S(2)}) collective-permute-start(f32[2,128,1024]{2,1,0:T(8,128)S(1)} %get-tuple-element.31.z_ref), channel_id=1, source_target_pairs={{0,1},{1,0},{2,3},{3,2},{4,5},{5,4},{6,7},{7,6},{8,9},{9,8},{10,11... | collective-permute-start | bytes 3145736 | tf_op jit(solution)/shard_map/ppermute | solution.py:545
  49.6 7.9 %collective-permute-start.2 = (f32[2,1024]{1,0:T(2,128)S(1)}, f32[2,1024]{1,0:T(2,128)S(1)}, u32[]{:S(2)}, u32[]{:S(2)}) collective-permute-start(f32[2,1024]{1,0:T(2,128)S(1)} %get-tuple-element.38), channel_id=1, source_target_pairs={{0,32},{32,64},{64,96},{96,128},{128,160},{160,192},{192,224},{1,3... | collective-permute-start | bytes 24584 | tf_op jit(solution)/shard_map/ppermute | solution.py:576
  53.1 4.6 %collective-permute-start.3 = (f32[2,1024]{1,0:T(2,128)S(1)}, f32[2,1024]{1,0:T(2,128)S(1)}, u32[]{:S(2)}, u32[]{:S(2)}) collective-permute-start(f32[2,1024]{1,0:T(2,128)S(1)} %get-tuple-element.39), channel_id=1, source_target_pairs={{32,0},{64,32},{96,64},{128,96},{160,128},{192,160},{224,192},{33,... | collective-permute-start | bytes 24584 | tf_op jit(solution)/shard_map/ppermute | solution.py:577
  54.4 9.2 %copy-start = (bf16[2,512,512]{2,1,0:T(8,128)(2,1)S(1)}, bf16[2,512,512]{2,1,0:T(8,128)(2,1)}, u32[]{:S(2)}) copy-start(bf16[2,512,512]{2,1,0:T(8,128)(2,1)} %constant.27.clone.odd_ref) | copy-start | bytes 3145732
  54.4 9.2 %copy-start.1 = (bf16[2,512,512]{2,1,0:T(8,128)(2,1)S(1)}, bf16[2,512,512]{2,1,0:T(8,128)(2,1)}, u32[]{:S(2)}) copy-start(bf16[2,512,512]{2,1,0:T(8,128)(2,1)} %constant.26.clone.even_ref) | copy-start | bytes 3145732
  54.5 9.2 %copy-start.5 = (bf16[256,128]{1,0:T(8,128)(2,1)S(1)}, bf16[256,128]{1,0:T(8,128)(2,1)}, u32[]{:S(2)}) copy-start(bf16[256,128]{1,0:T(8,128)(2,1)} %constant.28.clone.small_ref) | copy-start | bytes 196612
  63.7 17.1 %copy-start.3 = (f32[7,7,8,128]{3,2,1,0:T(8,128)S(1)}, f32[7,7,8,128]{3,2,1,0:T(8,128)}, u32[]{:S(2)}) copy-start(f32[7,7,8,128]{3,2,1,0:T(8,128)} %constant.32.clone.cut_ref) | copy-start | bytes 602116
  63.7 17.1 %copy-start.4 = (bf16[256,128]{1,0:T(8,128)(2,1)S(1)}, bf16[256,128]{1,0:T(8,128)(2,1)}, u32[]{:S(2)}) copy-start(bf16[256,128]{1,0:T(8,128)(2,1)} %constant.29.clone.small_t_ref) | copy-start | bytes 196612
  63.7 17.1 %copy-start.6 = (f32[2,8,128]{2,1,0:T(8,128)S(1)}, f32[2,8,128]{2,1,0:T(8,128)}, u32[]{:S(2)}) copy-start(f32[2,8,128]{2,1,0:T(8,128)} %constant.33.clone.near_far_ref) | copy-start | bytes 24580
  82.5 10.5 %collective-permute-start.5 = (f32[128,1024]{1,0:T(8,128)S(1)}, f32[128,1024]{1,0:T(8,128)S(1)}, u32[]{:S(2)}, u32[]{:S(2)}) collective-permute-start(f32[128,1024]{1,0:T(8,128)S(1)} %get-tuple-element.44.scaled_ref), channel_id=1, source_target_pairs={{1,2},{2,1},{3,4},{4,3},{5,6},{6,5},{7,8},{8,7},{9,10},{10,9},{11,... | collective-permute-start | bytes 1572872 | tf_op jit(solution)/shard_map/ppermute | solution.py:544
  85.9 7.1 %collective-permute-start.4 = (f32[128,1024]{1,0:T(8,128)S(1)}, f32[128,1024]{1,0:T(8,128)S(1)}, u32[]{:S(2)}, u32[]{:S(2)}) collective-permute-start(f32[128,1024]{1,0:T(8,128)S(1)} %get-tuple-element.44.scaled_ref), channel_id=1, source_target_pairs={{0,1},{1,0},{2,3},{3,2},{4,5},{5,4},{6,7},{7,6},{8,9},{9,8},{10,11... | collective-permute-start | bytes 1572872 | tf_op jit(solution)/shard_map/ppermute | solution.py:545
  105.4 11.4 %collective-permute-start.7 = (f32[128,1024]{1,0:T(8,128)S(1)}, f32[128,1024]{1,0:T(8,128)S(1)}, u32[]{:S(2)}, u32[]{:S(2)}) collective-permute-start(f32[128,1024]{1,0:T(8,128)S(1)} %get-tuple-element.50.scaled_ref), channel_id=1, source_target_pairs={{1,2},{2,1},{3,4},{4,3},{5,6},{6,5},{7,8},{8,7},{9,10},{10,9},{11,... | collective-permute-start | bytes 1572872 | tf_op jit(solution)/shard_map/ppermute | solution.py:544
  110.0 6.9 %collective-permute-start.6 = (f32[128,1024]{1,0:T(8,128)S(1)}, f32[128,1024]{1,0:T(8,128)S(1)}, u32[]{:S(2)}, u32[]{:S(2)}) collective-permute-start(f32[128,1024]{1,0:T(8,128)S(1)} %get-tuple-element.50.scaled_ref), channel_id=1, source_target_pairs={{0,1},{1,0},{2,3},{3,2},{4,5},{5,4},{6,7},{7,6},{8,9},{9,8},{10,11... | collective-permute-start | bytes 1572872 | tf_op jit(solution)/shard_map/ppermute | solution.py:545

commit v8 on v7

--- a/solution.py
+++ b/solution.py
@@ -268,7 +268,7 @@
             z_ref[1, rows, cols] = got_ref[source, pl.ds(at + 2 * BR, BR)] * fluid
         return carry
 
-    lax.fori_loop(0, XL // BR, line, 0)
+    lax.fori_loop(0, XL // BR, line, 0, unroll=4)
     for ref, row, end in ((first_ref, 0, 0), (last_ref, XL - 1, 1)):
         ref[0:1] = z_ref[1, row : row + 1]
         for y in range(N // B):

time: 145 us -> 145 us (level)
  no operation moved by 1% of the time
where the time goes in v8:
time: 145 us
  blocking collectives  92.2 us (64%)
  waiting for transfers between devices  18.8 us (13%)
  Pallas kernels  17.7 us (12%)
  starting transfers between devices  15 us (10%)
    all_to_all x1, blocking collectives, on_device(): got = lax.all_to_all(send, YZ, split_axis=0, concat_axis=0, tiled=True)  41.1 us
    all_to_all x2, blocking collectives, updated(): lax.all_to_all(ends, 'gx', split_axis=0, concat_axis=0, tiled=True)  24.8 us
    ppermute x3, waiting for transfers between devices, neighbours(): outer = lax.ppermute(value, YZ, off_chip)  18.6 us
    pallas_call x13, Pallas kernels, with_spaces(): run(*(x if spec is SMEM else pltpu.with_memory_space_constraint(x, spec.m...  17.7 us
    all_to_all x1, blocking collectives, on_device(): lax.all_to_all(sums, ('yz_0', 'yz_1'), split_axis=0, concat_axis=0, tiled...  17.5 us
    ppermute x3, starting transfers between devices, neighbours(): outer = lax.ppermute(value, YZ, off_chip)  9.93 us
    all_to_all x1, blocking collectives, on_device(): lax.all_to_all(sums, ('gx', 'yz_2'), split_axis=0, concat_axis=0, tiled=T...  8.8 us
    ppermute x1, starting transfers between devices, on_device(): xlo = lax.ppermute(last, 'gx', up_x)  3.54 us
  transfers between devices with their start and end apart: 8, of which 4 were waited for; matrix products, arithmetic and copies ran while one was open for 0% of the time, Pallas kernels for 3%

profile of v8, /device:TPU:1, one launch (start us, length us, event | category | flops | bytes accessed | tf_op | source)
XLA Modules:
  0.0 144.8 jit_solution(13983299707243739883)
XLA Ops:
  0.6 0.1 pad_add_fusion.place_ref
  0.7 3.6 %pack.1 = f32[32,152,128]{2,1,0:T(8,128)S(1)} custom-call(s32[2]{0:T(128)S(1)} %pad_add_fusion.place_ref, s32[1,64]{1,0:T(1,128)} %slot_hbm.1, f32[64,48,128]{2,1,0:T(8,128)} %bitcast.9, f32[64,16,128]{2,1,0:T(8,128)} %bitcast.10), custom_call_target="tpu_custom_call" | custom-call | tf_op jit(solution)/shard_map/pack/pallas_call | solution.py:518
  4.3 0.0 copy-start.8
  4.3 41.1 %all_to_all.25.got_ref = f32[32,152,128]{2,1,0:T(8,128)S(1)} all-to-all(f32[32,152,128]{2,1,0:T(8,128)S(1)} %pack.1), channel_id=1, replica_groups=mesh['gx'=8,'yz_0'=4,'yz_1'=4,'yz_2'=2] {'yz_0','yz_1','yz_2'}, dimensions={0} | all-to-all | bytes 4980736 | tf_op jit(solution)/shard_map/all_to_all | solution.py:566
  45.4 0.0 copy-done.8
  45.4 0.0 copy-start.2
  45.4 0.0 copy-start.7
  45.4 2.2 %place.1 = (f32[2,128,1024]{2,1,0:T(8,128)S(1)}, f32[2,1024]{1,0:T(2,128)S(1)}, f32[2,1024]{1,0:T(2,128)S(1)}, s32[1,128]{1,0:T(1,128)S(1)}) custom-call(s32[64]{0:T(128)S(1)} %bitcast.7, f32[32,152,128]{2,1,0:T(8,128)S(1)} %all_to_all.25.got_ref), custom_call_target="tpu_custom_call" | custom-call | tf_op jit(solution)/shard_map/place/pallas_call | solution.py:518
  47.6 1.9 %collective-permute-start.1 = (f32[2,128,1024]{2,1,0:T(8,128)S(1)}, f32[2,128,1024]{2,1,0:T(8,128)S(1)}, u32[]{:S(2)}, u32[]{:S(2)}) collective-permute-start(f32[2,128,1024]{2,1,0:T(8,128)S(1)} %get-tuple-element.31.z_ref), channel_id=1, source_target_pairs={{1,2},{2,1},{3,4},{4,3},{5,6},{6,5},{7,8},{8,7},{9,10},{10,9},{11,... | collective-permute-start | bytes 3145736 | tf_op jit(solution)/shard_map/ppermute | solution.py:544
  49.6 0.1 collective-permute-start
  49.7 3.5 %collective-permute-start.2 = (f32[2,1024]{1,0:T(2,128)S(1)}, f32[2,1024]{1,0:T(2,128)S(1)}, u32[]{:S(2)}, u32[]{:S(2)}) collective-permute-start(f32[2,1024]{1,0:T(2,128)S(1)} %get-tuple-element.38), channel_id=1, source_target_pairs={{0,32},{32,64},{64,96},{96,128},{128,160},{160,192},{192,224},{1,3... | collective-permute-start | bytes 24584 | tf_op jit(solution)/shard_map/ppermute | solution.py:576
  53.2 1.3 collective-permute-start.3
  54.5 0.0 copy-start
  54.5 0.0 copy-start.1
  54.5 0.0 copy-start.5
  54.6 1.5 %place_rest.1 = (f32[128,1024]{1,0:T(8,128)S(1)}, f32[128,1024]{1,0:T(8,128)S(1)}, f32[128,1024]{1,0:T(8,128)S(1)}) custom-call(s32[64]{0:T(128)S(1)} %bitcast.8, s32[1,128]{1,0:T(1,128)S(1)} %get-tuple-element.32.from_ref, f32[32,152,128]{2,1,0:T(8,128)S(1)} %all_to_all.25.got_ref), custom_call_target="tpu_custom_call" | custom-call | tf_op jit(solution)/shard_map/place_rest/pallas_call | solution.py:518
  56.0 0.0 copy-done.2
  56.0 0.0 copy-done.7
  56.0 1.5 %prepare.1 = (f32[128,1024]{1,0:T(8,128)S(1)}, f32[128,1024]{1,0:T(8,128)S(1)}, f32[128,1024]{1,0:T(8,128)S(1)}) custom-call(f32[2,128,1024]{2,1,0:T(8,128)S(1)} %get-tuple-element.31.z_ref, f32[128,1024]{1,0:T(8,128)S(1)} %get-tuple-element.33.inner_ref, f32[128,1024]{1,0:T(8,128)S(1)} %get-tuple-element.34.x_ends_ref, ...), custom_call_target="tpu_custom_call" | custom-call | tf_op jit(solution)/shard_map/prepare/pallas_call | solution.py:518
  57.6 0.0 collective-permute-done.2.xlo_ref
  57.6 0.2 collective-permute-done.3.xhi_ref
  57.8 6.0 %collective-permute-done.1.outer_ref = f32[2,128,1024]{2,1,0:T(8,128)S(1)} collective-permute-done((f32[2,128,1024]{2,1,0:T(8,128)S(1)}, f32[2,128,1024]{2,1,0:T(8,128)S(1)}, u32[]{:S(2)}, u32[]{:S(2)}) %collective-permute-start.1) | collective-permute-done | bytes 1048608 | tf_op jit(solution)/shard_map/ppermute | solution.py:544
  63.8 0.0 collective-permute-done.partner_ref
  63.8 0.0 copy-done
  63.8 0.0 copy-done.1
  63.8 0.0 copy-done.5
  63.8 0.0 copy-start.3
  63.8 0.0 copy-start.4
  63.8 0.0 copy-start.6
  63.8 1.8 %setup.1 = (f32[128,1024]{1,0:T(8,128)S(1)}, f32[128,1024]{1,0:T(8,128)S(1)}, f32[128,1024]{1,0:T(8,128)S(1)}, f32[8,16,128]{2,1,0:T(8,128)S(1)}) custom-call(s32[2]{0:T(128)S(1)} %pad_add_fusion.place_ref, f32[2,128,1024]{2,1,0:T(8,128)S(1)} %get-tuple-element.31.z_ref, f32[128,1024]{1,0:T(8,128)S(1)} %get-tuple-element.36.beside_ref, ...), custom_call_target="tpu_custom_call" | custom-call | tf_op jit(solution)/shard_map/setup/pallas_call | solution.py:518
  65.7 15.2 %all_to_all.26.all_ends_ref = f32[8,16,128]{2,1,0:T(8,128)S(1)} all-to-all(f32[8,16,128]{2,1,0:T(8,128)S(1)} %get-tuple-element.42), channel_id=1, replica_groups=mesh['gx'=8,'yz_0'=4,'yz_1'=4,'yz_2'=2] {'gx'}, dimensions={0} | all-to-all | bytes 131072 | tf_op jit(solution)/shard_map/all_to_all | solution.py:596
  80.9 0.0 copy-done.3
  80.9 0.0 copy-done.4
  80.9 0.0 copy-done.6
  80.9 1.7 %update.2 = (f32[128,1024]{1,0:T(8,128)S(1)}, f32[128,1024]{1,0:T(8,128)S(1)}, f32[2,1024]{1,0:T(2,128)S(1)}) custom-call(s32[2]{0:T(128)S(1)} %pad_add_fusion.place_ref, f32[128,1024]{1,0:T(8,128)S(1)} %get-tuple-element.41.modes_ref, f32[8,16,128]{2,1,0:T(8,128)S(1)} %all_to_all.26.all_ends_ref, f32[2,128,1024]{2,1,0:T(8,128)S(1)} %get-tuple-element.31.z_ref, ...), custom_call_target="tpu_custom_call" | custom-call | tf_op jit(solution)/shard_map/update/pallas_call | solution.py:518
  82.6 3.4 %collective-permute-start.5 = (f32[128,1024]{1,0:T(8,128)S(1)}, f32[128,1024]{1,0:T(8,128)S(1)}, u32[]{:S(2)}, u32[]{:S(2)}) collective-permute-start(f32[128,1024]{1,0:T(8,128)S(1)} %get-tuple-element.44.scaled_ref), channel_id=1, source_target_pairs={{1,2},{2,1},{3,4},{4,3},{5,6},{6,5},{7,8},{8,7},{9,10},{10,9},{11,... | collective-permute-start | bytes 1572872 | tf_op jit(solution)/shard_map/ppermute | solution.py:544
  86.0 0.1 collective-permute-start.4
  86.1 0.4 own.1.own_ref
  86.5 6.5 %collective-permute-done.5.outer_ref = f32[128,1024]{1,0:T(8,128)S(1)} collective-permute-done((f32[128,1024]{1,0:T(8,128)S(1)}, f32[128,1024]{1,0:T(8,128)S(1)}, u32[]{:S(2)}, u32[]{:S(2)}) %collective-permute-start.5) | collective-permute-done | bytes 524320 | tf_op jit(solution)/shard_map/ppermute | solution.py:544
  93.1 0.0 collective-permute-done.4.partner_ref
  93.1 1.1 image.1
  94.2 9.6 %all_to_all.27.all_ends_ref = f32[8,16,128]{2,1,0:T(8,128)S(1)} all-to-all(f32[8,16,128]{2,1,0:T(8,128)S(1)} %get-tuple-element.48), channel_id=1, replica_groups=mesh['gx'=8,'yz_0'=4,'yz_1'=4,'yz_2'=2] {'gx'}, dimensions={0} | all-to-all | bytes 131072 | tf_op jit(solution)/shard_map/all_to_all | solution.py:596
  103.8 1.7 %update.3 = (f32[128,1024]{1,0:T(8,128)S(1)}, f32[128,1024]{1,0:T(8,128)S(1)}, f32[2,1024]{1,0:T(2,128)S(1)}) custom-call(s32[2]{0:T(128)S(1)} %pad_add_fusion.place_ref, f32[128,1024]{1,0:T(8,128)S(1)} %get-tuple-element.47.modes_ref, f32[8,16,128]{2,1,0:T(8,128)S(1)} %all_to_all.27.all_ends_ref, f32[2,128,1024]{2,1,0:T(8,128)S(1)} %get-tuple-element.31.z_ref, ...), custom_call_target="tpu_custom_call" | custom-call | tf_op jit(solution)/shard_map/update/pallas_call | solution.py:518
  105.5 4.6 %collective-permute-start.7 = (f32[128,1024]{1,0:T(8,128)S(1)}, f32[128,1024]{1,0:T(8,128)S(1)}, u32[]{:S(2)}, u32[]{:S(2)}) collective-permute-start(f32[128,1024]{1,0:T(8,128)S(1)} %get-tuple-element.50.scaled_ref), channel_id=1, source_target_pairs={{1,2},{2,1},{3,4},{4,3},{5,6},{6,5},{7,8},{8,7},{9,10},{10,9},{11,... | collective-permute-start | bytes 1572872 | tf_op jit(solution)/shard_map/ppermute | solution.py:544
  110.1 0.1 collective-permute-start.6
  110.2 0.7 own_sums.1
  110.9 6.1 %collective-permute-done.7.outer_ref = f32[128,1024]{1,0:T(8,128)S(1)} collective-permute-done((f32[128,1024]{1,0:T(8,128)S(1)}, f32[128,1024]{1,0:T(8,128)S(1)}, u32[]{:S(2)}, u32[]{:S(2)}) %collective-permute-start.7) | collective-permute-done | bytes 524320 | tf_op jit(solution)/shard_map/ppermute | solution.py:544
  116.9 0.0 collective-permute-done.6.partner_ref
  116.9 0.3 sums.1
  117.3 8.8 %all_to_all.28.sums_ref = f32[16,1,128]{2,1,0:T(1,128)S(1)} all-to-all(f32[16,1,128]{2,1,0:T(1,128)S(1)} %get-tuple-element.56), channel_id=1, replica_groups=mesh['gx'=8,'yz_0'=4,'yz_1'=4,'yz_2'=2] {'gx','yz_2'}, dimensions={0} | all-to-all | bytes 16384 | tf_op jit(solution)/shard_map/all_to_all | solution.py:632
  126.1 17.5 %all_to_all.29.sums_ref = f32[16,1,128]{2,1,0:T(1,128)S(1)} all-to-all(f32[16,1,128]{2,1,0:T(1,128)S(1)} %add.3), channel_id=1, replica_groups=mesh['gx'=8,'yz_0'=4,'yz_1'=4,'yz_2'=2] {'yz_0','yz_1'}, dimensions={0} | all-to-all | bytes 16384 | tf_op jit(solution)/shard_map/all_to_all | solution.py:634
  143.6 1.2 final.1
  (1 shorter events, 0.0 us)
Async XLA Ops:
  4.3 41.1 %copy-start.8 = (s32[1,64]{1,0:T(1,128)S(1)}, s32[1,64]{1,0:T(1,128)}, u32[]{:S(2)}) copy-start(s32[1,64]{1,0:T(1,128)} %param.15) | copy-start | bytes 772
  45.4 10.6 %copy-start.2 = (f32[128,128]{1,0:T(8,128)S(1)}, f32[128,128]{1,0:T(8,128)}, u32[]{:S(2)}) copy-start(f32[128,128]{1,0:T(8,128)} %constant.30.clone.column_ref) | copy-start | bytes 196612
  45.4 10.6 %copy-start.7 = (f32[1,1024]{1,0:T(1,128)S(1)}, f32[1,1024]{1,0:T(1,128)}, u32[]{:S(2)}) copy-start(f32[1,1024]{1,0:T(1,128)} %constant.31.clone.lam_ref) | copy-start | bytes 12292
  47.6 16.1 %collective-permute-start.1 = (f32[2,128,1024]{2,1,0:T(8,128)S(1)}, f32[2,128,1024]{2,1,0:T(8,128)S(1)}, u32[]{:S(2)}, u32[]{:S(2)}) collective-permute-start(f32[2,128,1024]{2,1,0:T(8,128)S(1)} %get-tuple-element.31.z_ref), channel_id=1, source_target_pairs={{1,2},{2,1},{3,4},{4,3},{5,6},{6,5},{7,8},{8,7},{9,10},{10,9},{11,... | collective-permute-start | bytes 3145736 | tf_op jit(solution)/shard_map/ppermute | solution.py:544
  49.6 14.2 %collective-permute-start = (f32[2,128,1024]{2,1,0:T(8,128)S(1)}, f32[2,128,1024]{2,1,0:T(8,128)S(1)}, u32[]{:S(2)}, u32[]{:S(2)}) collective-permute-start(f32[2,128,1024]{2,1,0:T(8,128)S(1)} %get-tuple-element.31.z_ref), channel_id=1, source_target_pairs={{0,1},{1,0},{2,3},{3,2},{4,5},{5,4},{6,7},{7,6},{8,9},{9,8},{10,11... | collective-permute-start | bytes 3145736 | tf_op jit(solution)/shard_map/ppermute | solution.py:545
  49.7 7.9 %collective-permute-start.2 = (f32[2,1024]{1,0:T(2,128)S(1)}, f32[2,1024]{1,0:T(2,128)S(1)}, u32[]{:S(2)}, u32[]{:S(2)}) collective-permute-start(f32[2,1024]{1,0:T(2,128)S(1)} %get-tuple-element.38), channel_id=1, source_target_pairs={{0,32},{32,64},{64,96},{96,128},{128,160},{160,192},{192,224},{1,3... | collective-permute-start | bytes 24584 | tf_op jit(solution)/shard_map/ppermute | solution.py:576
  53.2 4.6 %collective-permute-start.3 = (f32[2,1024]{1,0:T(2,128)S(1)}, f32[2,1024]{1,0:T(2,128)S(1)}, u32[]{:S(2)}, u32[]{:S(2)}) collective-permute-start(f32[2,1024]{1,0:T(2,128)S(1)} %get-tuple-element.39), channel_id=1, source_target_pairs={{32,0},{64,32},{96,64},{128,96},{160,128},{192,160},{224,192},{33,... | collective-permute-start | bytes 24584 | tf_op jit(solution)/shard_map/ppermute | solution.py:577
  54.5 9.2 %copy-start = (bf16[2,512,512]{2,1,0:T(8,128)(2,1)S(1)}, bf16[2,512,512]{2,1,0:T(8,128)(2,1)}, u32[]{:S(2)}) copy-start(bf16[2,512,512]{2,1,0:T(8,128)(2,1)} %constant.27.clone.odd_ref) | copy-start | bytes 3145732
  54.5 9.2 %copy-start.1 = (bf16[2,512,512]{2,1,0:T(8,128)(2,1)S(1)}, bf16[2,512,512]{2,1,0:T(8,128)(2,1)}, u32[]{:S(2)}) copy-start(bf16[2,512,512]{2,1,0:T(8,128)(2,1)} %constant.26.clone.even_ref) | copy-start | bytes 3145732
  54.5 9.2 %copy-start.5 = (bf16[256,128]{1,0:T(8,128)(2,1)S(1)}, bf16[256,128]{1,0:T(8,128)(2,1)}, u32[]{:S(2)}) copy-start(bf16[256,128]{1,0:T(8,128)(2,1)} %constant.28.clone.small_ref) | copy-start | bytes 196612
  63.8 17.1 %copy-start.3 = (f32[7,7,8,128]{3,2,1,0:T(8,128)S(1)}, f32[7,7,8,128]{3,2,1,0:T(8,128)}, u32[]{:S(2)}) copy-start(f32[7,7,8,128]{3,2,1,0:T(8,128)} %constant.32.clone.cut_ref) | copy-start | bytes 602116
  63.8 17.1 %copy-start.4 = (bf16[256,128]{1,0:T(8,128)(2,1)S(1)}, bf16[256,128]{1,0:T(8,128)(2,1)}, u32[]{:S(2)}) copy-start(bf16[256,128]{1,0:T(8,128)(2,1)} %constant.29.clone.small_t_ref) | copy-start | bytes 196612
  63.8 17.1 %copy-start.6 = (f32[2,8,128]{2,1,0:T(8,128)S(1)}, f32[2,8,128]{2,1,0:T(8,128)}, u32[]{:S(2)}) copy-start(f32[2,8,128]{2,1,0:T(8,128)} %constant.33.clone.near_far_ref) | copy-start | bytes 24580
  82.6 10.5 %collective-permute-start.5 = (f32[128,1024]{1,0:T(8,128)S(1)}, f32[128,1024]{1,0:T(8,128)S(1)}, u32[]{:S(2)}, u32[]{:S(2)}) collective-permute-start(f32[128,1024]{1,0:T(8,128)S(1)} %get-tuple-element.44.scaled_ref), channel_id=1, source_target_pairs={{1,2},{2,1},{3,4},{4,3},{5,6},{6,5},{7,8},{8,7},{9,10},{10,9},{11,... | collective-permute-start | bytes 1572872 | tf_op jit(solution)/shard_map/ppermute | solution.py:544
  86.0 7.1 %collective-permute-start.4 = (f32[128,1024]{1,0:T(8,128)S(1)}, f32[128,1024]{1,0:T(8,128)S(1)}, u32[]{:S(2)}, u32[]{:S(2)}) collective-permute-start(f32[128,1024]{1,0:T(8,128)S(1)} %get-tuple-element.44.scaled_ref), channel_id=1, source_target_pairs={{0,1},{1,0},{2,3},{3,2},{4,5},{5,4},{6,7},{7,6},{8,9},{9,8},{10,11... | collective-permute-start | bytes 1572872 | tf_op jit(solution)/shard_map/ppermute | solution.py:545
  105.5 11.4 %collective-permute-start.7 = (f32[128,1024]{1,0:T(8,128)S(1)}, f32[128,1024]{1,0:T(8,128)S(1)}, u32[]{:S(2)}, u32[]{:S(2)}) collective-permute-start(f32[128,1024]{1,0:T(8,128)S(1)} %get-tuple-element.50.scaled_ref), channel_id=1, source_target_pairs={{1,2},{2,1},{3,4},{4,3},{5,6},{6,5},{7,8},{8,7},{9,10},{10,9},{11,... | collective-permute-start | bytes 1572872 | tf_op jit(solution)/shard_map/ppermute | solution.py:544
  110.1 6.9 %collective-permute-start.6 = (f32[128,1024]{1,0:T(8,128)S(1)}, f32[128,1024]{1,0:T(8,128)S(1)}, u32[]{:S(2)}, u32[]{:S(2)}) collective-permute-start(f32[128,1024]{1,0:T(8,128)S(1)} %get-tuple-element.50.scaled_ref), channel_id=1, source_target_pairs={{0,1},{1,0},{2,3},{3,2},{4,5},{5,4},{6,7},{7,6},{8,9},{9,8},{10,11... | collective-permute-start | bytes 1572872 | tf_op jit(solution)/shard_map/ppermute | solution.py:545
